TPU v7x, 256 devices: a whole 4x4x8 slice. The times are simulated.
256 devices in a mesh: dp: 8 (over z), ctx: 32 (over y, x, core).
Axes of the slice: x: 4, y: 4, z: 8, core: 2. Of those that a mesh axis runs over, the one named last changes fastest.
Arguments:
- queries: bfloat16 [8, 4096, 2048], P('dp', 'ctx'), may hold values from -6 to 6
- keys: bfloat16 [8, 4096, 2048], P('dp', 'ctx'), may hold values from -6 to 6
- values: bfloat16 [8, 4096, 2048], P('dp', 'ctx'), may hold values from -6 to 6
- grad_output: bfloat16 [8, 4096, 2048], P('dp', 'ctx'), may hold values from -6 to 6
- out_gain: float32 [2048], replicated, may hold values from 0.5 to 1.5
- doc_lengths: int32 [8, 12], P('dp'), may hold values from 1 to 1365, 4096 in all within a row
Outputs:
- output: bfloat16 [8, 4096, 2048], P('dp', 'ctx')
- grad_queries: bfloat16 [8, 4096, 2048], P('dp', 'ctx')
- grad_keys: bfloat16 [8, 4096, 2048], P('dp', 'ctx')
- grad_values: bfloat16 [8, 4096, 2048], P('dp', 'ctx')
- grad_gain: float32 [2048], replicated
Inputs may be any that keep to these rules, and one draw needn't show every extreme that they name: `doc_lengths`: each row holds the lengths of 12 documents packed end to end; they sum to 4096, and the largest is exactly 1365.
All inputs are finite; a program needn't handle non-finite values.
Results may differ from a plain program's by a relative error of at most 0.012.
The roundings to bfloat16 on the way count: a program that leaves them out, or rounds other values in their place, can miss the bound.
Values may be sent and summed in bfloat16 or wider, within the bound.
No kernel may reach another device: no remote copies, remote signals or barrier semaphores. Data moves between devices by JAX's collectives and lax.ppermute only.
A program may use at most 64 MiB of HBM per device.

v0:
```python
import math

import jax
import jax.numpy as jnp
from jax import lax
from jax.sharding import PartitionSpec as P

H = 32
E = 64


eps = 1e-05


def entering(part, axis, combine, identity):
    place = lax.axis_index(axis)
    gathered = jax.tree.map(lambda a: lax.all_gather(a, axis), part)
    state = jax.tree.map(lambda a, e: jnp.zeros_like(a) + jnp.asarray(e, a.dtype), part, identity)

    def entering_one(step, state):
        return combine(
            state, jax.tree.map(lambda a: lax.dynamic_index_in_dim(a, step, 0, False), gathered)
        )

    return lax.fori_loop(0, place, entering_one, state)


def carried_in(shard, axis, join, neutral):
    count = lax.axis_size(axis)
    place = lax.axis_index(axis)
    ahead = count - 1 - place
    gathered = jax.tree.map(
        lambda a, kind: lax.all_gather(a.astype(kind), axis), shard, (jnp.bfloat16, jnp.bfloat16)
    )
    state = jax.tree.map(lambda a, e: jnp.zeros_like(a) + jnp.asarray(e, a.dtype), shard, neutral)

    def carried_one(step, state):
        source = count - 1 - step
        return join(
            state,
            jax.tree.map(
                lambda a, own: lax.dynamic_index_in_dim(a, source, 0, False).astype(own.dtype),
                gathered,
                shard,
            ),
        )

    return lax.fori_loop(0, ahead, carried_one, state)


def doc_geometry(doc_lengths, positions):
    doc_ends = jnp.cumsum(doc_lengths, axis=1)
    begins = doc_ends - doc_lengths
    doc_ids = jnp.sum((positions[None, :, None] >= doc_ends[:, None, :]).astype(jnp.int32), axis=2)
    starts = jnp.sum((positions[None, :, None] == begins[:, None, :]).astype(jnp.float32), axis=2)
    return (doc_ids, starts)


def chain_join(earlier, later):
    keep = (1.0 - later[1]).reshape((-1,) + (1,) * (later[0].ndim - 1))
    state_sum = later[0] + keep * earlier[0]
    return (state_sum, jnp.maximum(earlier[1], later[1]))


def split_product(form, data, state):
    high_part = state.astype(jnp.bfloat16)
    low_part = (state - lax.optimization_barrier(high_part).astype(jnp.float32)).astype(
        jnp.bfloat16
    )
    first = jnp.einsum(form, data, high_part, preferred_element_type=jnp.float32)
    return first + jnp.einsum(form, data, low_part, preferred_element_type=jnp.float32)


def blocks_math(
    queries, keys, values, grad_output, gain_heads, doc_ids, starts, forward_carry, backward_carry
):
    counted = jnp.cumsum(starts, axis=1)
    totals = counted[:, -1:]
    before = (counted == 0).astype(jnp.float32)[:, :, None, None]
    after_mask = (totals - counted == 0).astype(jnp.float32)[:, :, None, None]
    opened = jnp.minimum(totals[:, 0], 1.0)
    row_ids = jnp.arange(queries.shape[1])
    causal = row_ids[:, None] >= row_ids[None, :]
    doc_mask = jnp.logical_and(causal[None], doc_ids[:, :, None] == doc_ids[:, None, :]).astype(
        jnp.float32
    )[:, None]
    scores = jnp.einsum("btge,bsge->bgts", queries, keys, preferred_element_type=jnp.float32)
    weights = (scores * doc_mask).astype(jnp.bfloat16)
    own_state = jnp.einsum(
        "bsge,bsgf->bgef",
        keys * after_mask.astype(jnp.bfloat16),
        values,
        preferred_element_type=jnp.float32,
    )
    carried = forward_carry(own_state, opened)
    attended = jnp.einsum("bgts,bsgf->btgf", weights, values, preferred_element_type=jnp.float32)
    attended = attended + before * split_product("btge,bgef->btgf", queries, carried)
    root_mean = jnp.sqrt(jnp.mean(attended * attended, axis=-1, keepdims=True) + eps)
    normed = attended / root_mean
    output = (gain_heads * normed).astype(jnp.bfloat16)
    dyf = grad_output.astype(jnp.float32)
    dnormed = dyf * gain_heads
    grad_att = (
        (dnormed - normed * jnp.mean(dnormed * normed, axis=-1, keepdims=True)) / root_mean
    ).astype(jnp.bfloat16)
    gain_part = jnp.sum(dyf * normed, axis=(0, 1))
    grad_scores = jnp.einsum(
        "btgf,bsgf->bgts", grad_att, values, preferred_element_type=jnp.float32
    )
    grad_weights = (grad_scores * doc_mask).astype(jnp.bfloat16)
    back_state = jnp.einsum(
        "btge,btgf->bgef",
        queries * before.astype(jnp.bfloat16),
        grad_att,
        preferred_element_type=jnp.float32,
    )
    back_carried = backward_carry(back_state, opened)
    grad_q = jnp.einsum("bgts,bsge->btge", grad_weights, keys, preferred_element_type=jnp.float32)
    grad_q = grad_q + before * split_product("btgf,bgef->btge", grad_att, carried)
    grad_k = jnp.einsum(
        "bgts,btge->bsge", grad_weights, queries, preferred_element_type=jnp.float32
    )
    grad_k = grad_k + after_mask * split_product("bsgf,bgef->bsge", values, back_carried)
    grad_v = jnp.einsum("bgts,btgf->bsgf", weights, grad_att, preferred_element_type=jnp.float32)
    grad_v = grad_v + after_mask * split_product("bsge,bgef->bsgf", keys, back_carried)
    return (
        output,
        grad_q.astype(jnp.bfloat16),
        grad_k.astype(jnp.bfloat16),
        grad_v.astype(jnp.bfloat16),
        gain_part,
    )


def per_device(queries, keys, values, grad_output, out_gain, doc_lengths):
    local_seqs, block_len, width = queries.shape
    ctx_count = lax.axis_size("ctx")
    ctx_index = lax.axis_index("ctx")
    shape4 = (local_seqs, block_len, H, E)
    quad = tuple((item.reshape(shape4) for item in (queries, keys, values, grad_output)))
    gain_heads = out_gain.reshape(H, E)
    positions = ctx_index * block_len + jnp.arange(block_len, dtype=jnp.int32)
    doc_ids, starts = doc_geometry(doc_lengths, positions)

    def chain_forward(state, opened):
        wide = state.reshape(state.shape[0], H, E * E)
        moved = entering(
            (wide, opened), "ctx", chain_join, (jnp.zeros_like(wide), jnp.zeros_like(opened))
        )[0]
        return moved.reshape(state.shape)

    def chain_backward(state, opened):
        wide = state.reshape(state.shape[0], H, E * E)
        moved = carried_in(
            (wide, opened), "ctx", chain_join, (jnp.zeros_like(wide), jnp.zeros_like(opened))
        )[0]
        return moved.reshape(state.shape)

    results = blocks_math(
        quad[0],
        quad[1],
        quad[2],
        quad[3],
        gain_heads,
        doc_ids,
        starts,
        chain_forward,
        chain_backward,
    )
    returned = results[:4]
    gain_terms = results[4]
    total_tokens = local_seqs * lax.axis_size("dp") * block_len * ctx_count
    grad_gain = lax.psum(gain_terms.reshape(H * E), ("dp", "ctx")) / math.sqrt(total_tokens)
    flat = (local_seqs, block_len, H * E)
    outputs = tuple((item.reshape(flat) for item in returned))
    return (outputs[0], outputs[1], outputs[2], outputs[3], grad_gain)


def solution(mesh):
    placed = (
        P("dp", "ctx", None),
        P("dp", "ctx", None),
        P("dp", "ctx", None),
        P("dp", "ctx", None),
        P(),
        P("dp", None),
    )
    return jax.shard_map(
        per_device,
        mesh=mesh,
        in_specs=placed,
        out_specs=(
            P("dp", "ctx", None),
            P("dp", "ctx", None),
            P("dp", "ctx", None),
            P("dp", "ctx", None),
            P(),
        ),
        check_vma=False,
    )
```

profile of v0, /device:TPU:2, one launch (start us, length us, event | category | flops | bytes accessed | tf_op | source)
XLA Modules:
  0.0 418.2 jit_solution(17803829553141644253)
XLA Ops:
  19.2 63.2 %all-reduce = f32[32]{0:T(128)S(1)} all-reduce(f32[32]{0:T(128)S(1)} %bitcast_dynamic-update-slice_fusion), channel_id=1, replica_groups=mesh['dp'=8,'ctx'=32] {'ctx'}, use_global_device_ids=true, to_apply=%add | all-reduce | flops 32 | bytes 256
  83.2 12.1 %all-gather.3.cloned.1.call-done = f32[32,1,32,4096]{3,2,1,0:T(8,128)} async-done(((f32[1,1,32,4096]{3,2,1,0:T(8,128)}), f32[32,1,32,4096]{3,2,1,0:T(8,128)}) %all-gather.3.cloned.1.call-update) | async-done | bytes 16777232 | tf_op jit(solution)/shard_map/all_gather | solution.py:17
  95.3 5.0 %while.26 = (s32[]{:T(128)}, f32[1,32,4096]{2,1,0:T(8,128)S(1)}, s32[]{:T(128)}, f32[32,1,32,4096]{3,2,1,0:T(8,128)}, f32[32,1]{0,1:T(1,128)S(1)}, /*index=5*/s32[]{:T(128)}, s32[]{:T(128)}, s32[]{:T(128)}) while((s32[]{:T(128)}, f32[1,32,4096]{2,1,0:T(8,128)S(1)}, s32[]{:T(128)}, f32[32,1,32,4096]{3,2,1,0:T(8,128)}, f32[32,1]{0,1:T(1,128)S(1)}, ...), condition=%wide.region_5.6_spmd, body=%wide.region_4.5_spmd.sunk | while | flops 262150 | bytes 1573003 | solution.py:25
  96.0 1.9 bitcast_add_fusion.2
  98.5 1.9 bitcast_add_fusion.2
  110.2 133.4 %all-reduce.1 = bf16[32]{0:T(256)(128)(2,1)S(1)} all-reduce(bf16[32]{0:T(256)(128)(2,1)S(1)} %dynamic-update-slice.1), channel_id=1, replica_groups=mesh['dp'=8,'ctx'=32] {'ctx'}, use_global_device_ids=true, to_apply=%add.1 | all-reduce | flops 32 | bytes 128
  248.9 78.5 %psum.7 = f32[2048]{0:T(1024)S(1)} all-reduce(f32[2048]{0:T(1024)S(1)} %reshape.507), channel_id=1, replica_groups=mesh['dp'=8,'ctx'=32] {'dp','ctx'}, use_global_device_ids=true, to_apply=%region_11.12 | all-reduce | flops 2048 | bytes 16384 | tf_op jit(solution)/shard_map/psum | solution.py:173
  328.0 69.9 %while.27 = (s32[]{:T(128)}, f32[1,32,4096]{2,1,0:T(8,128)S(1)}, s32[]{:T(128)}, bf16[32,1,32,4096]{3,2,1,0:T(8,128)(2,1)}, bf16[32,1]{0,1:T(2,128)(2,1)S(1)}, /*index=5*/s32[]{:T(128)}, s32[]{:T(128)}, s32[]{:T(128)}, s32[]{:T(128)}) while((s32[]{:T(128)}, f32[1,32,4096]{2,1,0:T(8,128)S(1)}, s32[]{:T(128)}, ...), condition=%wide.region_9.10_spmd, body=%wide.region_8.9_spmd.sunk | while | flops 393223 | bytes 1310877 | solution.py:48
  328.7 1.8 convert_add_fusion.2
  331.1 1.8 convert_add_fusion.2
  333.5 1.8 convert_add_fusion.2
  335.9 1.8 convert_add_fusion.2
  338.3 1.8 convert_add_fusion.2
  340.7 1.8 convert_add_fusion.2
  343.1 1.8 convert_add_fusion.2
  345.5 1.8 convert_add_fusion.2
  347.9 1.8 convert_add_fusion.2
  362.3 1.8 convert_add_fusion.2
  364.7 1.8 convert_add_fusion.2
  367.1 1.8 convert_add_fusion.2
  386.3 1.8 convert_add_fusion.2
  388.7 1.8 convert_add_fusion.2
  391.1 1.8 convert_add_fusion.2
  408.1 1.8 fusion.11
  (137 shorter events, 82.6 us)
Async XLA Ops:
  7.2 88.1 %all-gather.3.cloned.1.call-start = ((), (), s32[]{:S(2)}) async-start(), calls=%async_computation | async-start | bytes 17301504 | tf_op jit(solution)/shard_map/all_gather | solution.py:17
  13.4 3.2 copy-start.12
  13.4 4.5 %copy-start.13 = (f32[2048]{0:T(1024)S(1)}, f32[2048]{0:T(1024)}, u32[]{:S(2)}) copy-start(f32[2048]{0:T(1024)} %param.14) | copy-start | bytes 24580
  13.4 4.5 %copy-start.14 = (u32[256]{0:T(256)S(1)}, u32[256]{0:T(256)}, u32[]{:S(2)}) copy-start(u32[256]{0:T(256)} %constant.98) | copy-start | bytes 3076
  14.6 313.4 %all-gather.5.cloned.1.call-start = ((), (), s32[]{:S(2)}) async-start(), calls=%async_computation.1 | async-start | bytes 8650752 | tf_op jit(solution)/shard_map/all_gather | solution.py:33
  83.2 20.9 %copy-start.2 = (bf16[32,128,128]{2,1,0:T(8,128)(2,1)}, bf16[32,128,128]{2,1,0:T(8,128)(2,1)S(1)}, u32[]{:S(2)}) copy-start(bf16[32,128,128]{2,1,0:T(8,128)(2,1)S(1)} %multiply_convert_fusion.1) | copy-start | bytes 3145732
  102.4 1.2 copy-start
  103.7 0.8 copy-start.7
  104.5 1.2 copy-start.6
  243.6 1.2 copy-start.1
  243.6 1.4 copy-start.8
  245.0 1.1 copy-start.4
  246.0 1.8 copy-start.11
  404.0 1.4 copy-start.10
  404.1 1.7 copy-start.9
  405.5 1.2 copy-start.3
  408.1 1.8 copy-start.5
Sparse Core Ops, SparseCore 0:
  14.7 80.5 all-gather.2
  109.6 128.9 all-gather.4
where the time goes:
time: 425 us; the launch traced here: 418 us
  blocking collectives  275 us (65%)
  other arithmetic  79.5 us (19%)
  local copies, waits for them, and re-layouts  25.1 us (6%)
  between operations  15.1 us (4%)
  waiting for transfers between devices  12.2 us (3%)
  matrix products  10.3 us (2%)
    unnamed x2, blocking collectives  197 us
    psum x1, blocking collectives, per_device(): lax.psum(gain_terms.reshape(H * E), ('dp', 'ctx')) / math.sqrt(total_tokens)  78.5 us
    add x31, other arithmetic, chain_join(): state_sum = later[0] + keep * earlier[0]  55.7 us
    sub x31, other arithmetic, chain_join(): keep = (1.0 - later[1]).reshape((-1,) + (1,) * (later[0].ndim - 1))  18.2 us
    unnamed x42, local copies, waits for them, and re-layouts  15.2 us
    all_gather x1, waiting for transfers between devices, entering(): gathered = jax.tree.map(lambda a: lax.all_gather(a, axis), part)  12.1 us
  transfers between devices with their start and end apart: 2, of which 1 were waited for; matrix products, arithmetic and copies ran while one was open for 2% of the time, Pallas kernels for 0%

commit v1 on v0

v1 whole, which is shorter than its diff:
```python
import math

import jax
import jax.numpy as jnp
from jax import lax
from jax.experimental import pallas as pl
from jax.experimental.pallas import tpu as pltpu
from jax.sharding import PartitionSpec as P

H = 32
E = 64
PAIR = 2 * E
PAIRS = H // 2
DOCS = 12
BLK = 128
NBLK = 32
ROWS = 32
WIDE = 48

eps = 1e-05
f32 = jnp.float32
bf16 = jnp.bfloat16


def dot(a, b):
    return lax.dot_general(a, b, (((1,), (0,)), ((), ())), preferred_element_type=f32)


def dot_nt(a, b):
    return lax.dot_general(a, b, (((1,), (1,)), ((), ())), preferred_element_type=f32)


def dot_tn(a, b):
    return lax.dot_general(a, b, (((0,), (0,)), ((), ())), preferred_element_type=f32)


def bounds(len_ref):
    begins, total = [], jnp.int32(0)
    for k in range(DOCS):
        begins.append(total)
        total = total + len_ref[0, k]
    return begins


def block_masks(begins, base):
    shape = (BLK, BLK)
    row = lax.broadcasted_iota(jnp.int32, shape, 0) + base
    col = lax.broadcasted_iota(jnp.int32, shape, 1) + base
    row_id = jnp.zeros(shape, jnp.int32)
    col_id = jnp.zeros(shape, jnp.int32)
    first_id = jnp.int32(0)
    last_id = jnp.int32(0)
    for begin in begins:
        row_id = row_id + (row >= begin).astype(jnp.int32)
        col_id = col_id + (col >= begin).astype(jnp.int32)
        first_id = first_id + (begin < base).astype(jnp.int32)
        last_id = last_id + (begin < base + BLK).astype(jnp.int32)
    doc_mask = jnp.logical_and(row >= col, row_id == col_id)
    before = row_id == first_id
    after = row_id == last_id
    return doc_mask, before, after


def halves():
    return lax.broadcasted_iota(jnp.int32, (BLK, PAIR), 1) < E


def pick(cond, a):
    return jnp.where(cond, a, jnp.zeros_like(a))


def heads(left, a):
    return jnp.concatenate([pick(left, a), pick(jnp.logical_not(left), a)], axis=0)


def squeeze_state(left, full):
    return jnp.where(left[:E], full[:E], full[E:])


def spread_state(left, state):
    return jnp.concatenate(
        [pick(left[:E], state), pick(jnp.logical_not(left[:E]), state)], axis=0
    )


def own_state_kernel(len_ref, k_ref, v_ref, state_ref):
    base = lax.axis_index("ctx") * BLK
    _, _, after = block_masks(bounds(len_ref), base)
    left = halves()
    for p in range(PAIRS):
        lanes = slice(p * PAIR, (p + 1) * PAIR)
        k = pick(after, k_ref[0, :, lanes])
        full = dot_tn(k, v_ref[0, :, lanes])
        state_ref[p * E : (p + 1) * E, :] = squeeze_state(left, full).astype(bf16)


def keeps(len_ref):
    begins = bounds(len_ref)
    out = []
    for j in range(NBLK):
        opened = jnp.bool_(False)
        for begin in begins:
            opened = jnp.logical_or(
                opened, jnp.logical_and(begin >= j * BLK, begin < (j + 1) * BLK)
            )
        out.append(jnp.where(opened, 0.0, 1.0).astype(f32))
    return out


def scan_kernel(len_ref, x_ref, o_ref):
    keep = keeps(len_ref)
    carry = jnp.zeros((ROWS, PAIR), f32)
    for j in range(NBLK):
        o_ref[j] = carry.astype(bf16)
        carry = x_ref[j].astype(f32) + keep[j] * carry


def back_scan_kernel(len_ref, x_ref, o_ref):
    keep = keeps(len_ref)
    carry = jnp.zeros((ROWS, PAIR), f32)
    gain = jnp.zeros((1, PAIR), f32)
    for j in reversed(range(NBLK)):
        o_ref[j, :ROWS] = carry.astype(bf16)
        carry = x_ref[j, :ROWS].astype(f32) + keep[j] * carry
        gain = gain + x_ref[j, ROWS : ROWS + 1].astype(f32) + x_ref[j, ROWS + 1 : ROWS + 2].astype(f32)
    high = gain.astype(bf16)
    low = (gain - high.astype(f32)).astype(bf16)
    tile = jnp.concatenate([high, low, jnp.zeros((WIDE - ROWS - 2, PAIR), bf16)], axis=0)
    for j in range(NBLK):
        o_ref[j, ROWS:] = tile


def middle_kernel(
    len_ref, q_ref, k_ref, v_ref, g_ref, gain_ref, c_ref, out_ref, gq_ref, pk_ref, pv_ref, back_ref
):
    base = lax.axis_index("ctx") * BLK
    doc_mask, before, _ = block_masks(bounds(len_ref), base)
    mask2 = jnp.concatenate([doc_mask, doc_mask], axis=0)
    left = halves()
    same = (lax.broadcasted_iota(jnp.int32, (PAIR, PAIR), 0) < E) == left
    ones = jnp.where(same, 1.0 / E, 0.0).astype(bf16)
    ones2 = jnp.concatenate([ones, ones], axis=0)
    for p in range(PAIRS):
        lanes = slice(p * PAIR, (p + 1) * PAIR)
        q, k, v = q_ref[0, :, lanes], k_ref[0, :, lanes], v_ref[0, :, lanes]
        gain = gain_ref[:, lanes]
        q2, k2, v2 = heads(left, q), heads(left, k), heads(left, v)
        carried = spread_state(left, c_ref[p * E : (p + 1) * E, :])
        qb = pick(before, q)
        weights = pick(mask2, dot_nt(q2, k)).astype(bf16)
        att = dot(jnp.concatenate([weights[:BLK], weights[BLK:]], axis=1), v2) + dot(qb, carried)
        dy = g_ref[0, :, lanes].astype(f32)
        d = dy * gain
        terms = jnp.concatenate([att * att, d * att], axis=0)
        high = terms.astype(bf16)
        low = (terms - high.astype(f32)).astype(bf16)
        means = dot(jnp.concatenate([high, low], axis=1), ones2)
        r = lax.rsqrt(means[:BLK] + eps)
        normed = att * r
        out_ref[0, :, lanes] = (gain * normed).astype(bf16)
        ga = ((d - normed * (means[BLK:] * r)) * r).astype(bf16)
        part = jnp.sum(dy * normed, axis=0, keepdims=True)
        part_high = part.astype(bf16)
        part_low = (part - part_high.astype(f32)).astype(bf16)
        tile = jnp.concatenate(
            [part_high, part_low, jnp.zeros((WIDE - ROWS - 2, PAIR), bf16)], axis=0
        )
        state = squeeze_state(left, dot_tn(qb, ga)).astype(bf16)
        for i in range(2):
            back_ref[2 * p + i, :ROWS] = state[i * ROWS : (i + 1) * ROWS]
            back_ref[2 * p + i, ROWS:] = tile
        ga2 = heads(left, ga)
        gw = pick(mask2, dot_nt(ga2, v)).astype(bf16)
        gq = dot(jnp.concatenate([gw[:BLK], gw[BLK:]], axis=1), k2)
        gq = gq + dot_nt(pick(before, ga), carried)
        gq_ref[0, :, lanes] = gq.astype(bf16)
        pk_ref[:, lanes] = dot_tn(gw, q2)
        pv_ref[:, lanes] = dot_tn(weights, ga2)


def last_kernel(len_ref, k_ref, v_ref, pk_ref, pv_ref, bc_ref, gk_ref, gv_ref, gain_ref):
    base = lax.axis_index("ctx") * BLK
    _, _, after = block_masks(bounds(len_ref), base)
    left = halves()
    for p in range(PAIRS):
        lanes = slice(p * PAIR, (p + 1) * PAIR)
        k = pick(after, k_ref[0, :, lanes])
        v = pick(after, v_ref[0, :, lanes])
        state = jnp.concatenate([bc_ref[2 * p, :ROWS], bc_ref[2 * p + 1, :ROWS]], axis=0)
        carried = spread_state(left, state)
        gk_ref[0, :, lanes] = (pk_ref[:, lanes] + dot_nt(v, carried)).astype(bf16)
        gv_ref[0, :, lanes] = (pv_ref[:, lanes] + dot(k, carried)).astype(bf16)
        high = bc_ref[2 * p, ROWS : ROWS + 1].astype(f32)
        gain_ref[:, lanes] = high + bc_ref[2 * p, ROWS + 1 : ROWS + 2].astype(f32)


def call(kernel, outs, n_in, name):
    vmem = pl.BlockSpec(memory_space=pltpu.VMEM)
    smem = pl.BlockSpec(memory_space=pltpu.SMEM)
    return pl.pallas_call(
        kernel,
        out_shape=outs,
        in_specs=[smem] + [vmem] * n_in,
        out_specs=jax.tree.map(lambda _: vmem, outs),
        compiler_params=pltpu.CompilerParams(vmem_limit_bytes=48 << 20),
        name=name,
    )


def per_device(queries, keys, values, grad_output, out_gain, doc_lengths):
    shape = jax.ShapeDtypeStruct
    full = shape(queries.shape, bf16)
    plain = shape((BLK, H * E), f32)
    narrow = shape((NBLK, ROWS, PAIR), bf16)
    wide = shape((NBLK, WIDE, PAIR), bf16)
    gain = out_gain.reshape(1, H * E)

    def swap(a):
        return lax.all_to_all(a, "ctx", 0, 0, tiled=True)

    own = call(own_state_kernel, shape((PAIRS * E, PAIR), bf16), 2, "own_state")(
        doc_lengths, keys, values
    )
    moved = swap(own.reshape(narrow.shape))
    moved = call(scan_kernel, narrow, 1, "scan")(doc_lengths, moved)
    carried = swap(moved).reshape(PAIRS * E, PAIR)
    output, grad_q, part_k, part_v, back = call(
        middle_kernel, (full, full, plain, plain, wide), 6, "middle"
    )(doc_lengths, queries, keys, values, grad_output, gain, carried)
    moved = swap(back)
    moved = call(back_scan_kernel, wide, 1, "back_scan")(doc_lengths, moved)
    back_carried = swap(moved)
    grad_k, grad_v, gain_terms = call(last_kernel, (full, full, shape((1, H * E), f32)), 5, "last")(
        doc_lengths, keys, values, part_k, part_v, back_carried
    )
    total_tokens = lax.axis_size("dp") * BLK * lax.axis_size("ctx")
    grad_gain = lax.psum(gain_terms.reshape(H * E), "dp") / math.sqrt(total_tokens)
    return (output, grad_q, grad_k, grad_v, grad_gain)


def solution(mesh):
    split = P("dp", "ctx", None)
    return jax.shard_map(
        per_device,
        mesh=mesh,
        in_specs=(split, split, split, split, P(), P("dp", None)),
        out_specs=(split, split, split, split, P()),
        check_vma=False,
    )
```

time: 425 us -> 98.1 us (0.23); the launches traced: 418 us -> 97.7 us
  blocking collectives: 275 us -> 75.7 us
  other arithmetic: 79.5 us -> 0.6 us
  local copies, waits for them, and re-layouts: 25.1 us -> 2.76 us
  Pallas kernels: 0 us -> 18 us
  between operations: 15.1 us -> 0.7 us
  waiting for transfers between devices: 12.2 us -> 0 us
  matrix products: 10.3 us -> 0 us
    unnamed x2 -> x0, blocking collectives: 197 us -> none
    psum x1, blocking collectives: 78.5 us -> 20.2 us  [per_device(): lax.psum(gain_terms.reshape(H * E), 'dp') / math.sqrt(total_tokens)]
    add x32 -> x0, other arithmetic: 55.7 us -> none  [the longest x31 55.7 us: chain_join(): state_sum = later[0] + keep * earlier[0]]
    all_to_all x0 -> x4, blocking collectives: none -> 55.4 us  [swap(): return lax.all_to_all(a, 'ctx', 0, 0, tiled=True)]
    sub x31 -> x0, other arithmetic: 18.2 us -> none  [chain_join(): keep = (1.0 - later[1]).reshape((-1,) + (1,) * (later[0].ndim - 1))]
    pallas_call x0 -> x5, Pallas kernels: none -> 18 us  [the longest x1 12.8 us: per_device(): call(middle_kernel, (full, full, plain, plain, wide), 6, 'middle')]
    unnamed x42 -> x16, local copies, waits for them, and re-layouts: 15.2 us -> 2.76 us
    all_gather x2 -> x0, waiting for transfers between devices: 12.1 us -> none  [the longest x1 12.1 us: entering(): gathered = jax.tree.map(lambda a: lax.all_gather(a, axis), part)]
  transfers between devices with their start and end apart: 2 -> 0, of which waited for: 1 -> 0; matrix products, arithmetic and copies ran while one was open for 2% -> 0% of each run, Pallas kernels for 0% -> 0%
where the time goes in v1:
time: 98.1 us; the launch traced here: 97.7 us
  blocking collectives  75.7 us (77%)
  Pallas kernels  18 us (18%)
  local copies, waits for them, and re-layouts  2.76 us (3%)
    all_to_all x4, blocking collectives, swap(): return lax.all_to_all(a, 'ctx', 0, 0, tiled=True)  55.4 us
    psum x1, blocking collectives, per_device(): lax.psum(gain_terms.reshape(H * E), 'dp') / math.sqrt(total_tokens)  20.2 us
    pallas_call x1, Pallas kernels, per_device(): call(middle_kernel, (full, full, plain, plain, wide), 6, 'middle')  12.8 us
    unnamed x16, local copies, waits for them, and re-layouts  2.76 us
    pallas_call x1, Pallas kernels, per_device(): call(last_kernel, (full, full, shape((1, H * E), f32)), 5, 'last')  2.18 us

profile of v1, /device:TPU:2, one launch (start us, length us, event | category | flops | bytes accessed | tf_op | source)
XLA Modules:
  0.0 97.7 jit_solution(16546964300074935480)
XLA Ops:
  0.6 0.0 copy-start
  0.6 1.0 %copy-done = bf16[1,128,2048]{2,1,0:T(8,128)(2,1)S(1)} copy-done((bf16[1,128,2048]{2,1,0:T(8,128)(2,1)S(1)}, bf16[1,128,2048]{2,1,0:T(8,128)(2,1)}, u32[]{:S(2)}) %copy-start) | copy-done | bytes 524312
  1.7 0.0 copy-start.2
  1.7 1.0 %copy-done.2 = bf16[1,128,2048]{2,1,0:T(8,128)(2,1)S(1)} copy-done((bf16[1,128,2048]{2,1,0:T(8,128)(2,1)S(1)}, bf16[1,128,2048]{2,1,0:T(8,128)(2,1)}, u32[]{:S(2)}) %copy-start.2) | copy-done | bytes 524312
  2.7 0.0 copy-start.6
  2.7 0.7 copy-done.6
  3.4 1.0 own_state.1
  4.3 0.0 copy-start.5
  4.4 15.2 %all_to_all.20.x_ref = bf16[32,32,128]{2,1,0:T(8,128)(2,1)S(1)} all-to-all(bf16[32,32,128]{2,1,0:T(8,128)(2,1)S(1)} %bitcast.4), channel_id=1, replica_groups=mesh['dp'=8,'ctx'=32] {'ctx'}, dimensions={0} | all-to-all | bytes 524288 | tf_op jit(solution)/shard_map/all_to_all | solution.py:219
  19.6 1.0 %scan.1 = bf16[32,32,128]{2,1,0:T(8,128)(2,1)S(1)} custom-call(s32[1,12]{1,0:T(1,128)S(1)} %copy-done.6, bf16[32,32,128]{2,1,0:T(8,128)(2,1)S(1)} %all_to_all.20.x_ref), custom_call_target="tpu_custom_call" | custom-call | tf_op jit(solution)/shard_map/scan/pallas_call | solution.py:225
  20.6 12.5 %all_to_all.21 = bf16[32,32,128]{2,1,0:T(8,128)(2,1)S(1)} all-to-all(bf16[32,32,128]{2,1,0:T(8,128)(2,1)S(1)} %scan.1), channel_id=1, replica_groups=mesh['dp'=8,'ctx'=32] {'ctx'}, dimensions={0} | all-to-all | bytes 524288 | tf_op jit(solution)/shard_map/all_to_all | solution.py:219
  33.1 0.0 copy-done.7
  33.1 0.0 copy-done.5
  33.1 0.0 copy-done.1
  33.1 0.0 copy-done.4
  33.1 12.8 %middle.1 = (bf16[1,128,2048]{2,1,0:T(8,128)(2,1)}, bf16[1,128,2048]{2,1,0:T(8,128)(2,1)}, f32[128,2048]{1,0:T(8,128)S(1)}, f32[128,2048]{1,0:T(8,128)S(1)}, bf16[32,48,128]{2,1,0:T(8,128)(2,1)S(1)}) custom-call(s32[1,12]{1,0:T(1,128)S(1)} %copy-done.6, bf16[1,128,2048]{2,1,0:T(8,128)(2,1)S(1)} %copy-done.4, bf16[1,128,2048]{2,1,0:T(8,128)(2,1)S(1)} %copy-done.1, ...), custom_call_target="tpu_custom_call" | custom-call | tf_op jit(solution)/shard_map/middle/pallas_call | solution.py:227
  45.9 13.8 %all_to_all.22.x_ref = bf16[32,48,128]{2,1,0:T(8,128)(2,1)S(1)} all-to-all(bf16[32,48,128]{2,1,0:T(8,128)(2,1)S(1)} %get-tuple-element.17), channel_id=1, replica_groups=mesh['dp'=8,'ctx'=32] {'ctx'}, dimensions={0} | all-to-all | bytes 786432 | tf_op jit(solution)/shard_map/all_to_all | solution.py:219
  59.8 1.0 %back_scan.1 = bf16[32,48,128]{2,1,0:T(8,128)(2,1)S(1)} custom-call(s32[1,12]{1,0:T(1,128)S(1)} %copy-done.6, bf16[32,48,128]{2,1,0:T(8,128)(2,1)S(1)} %all_to_all.22.x_ref), custom_call_target="tpu_custom_call" | custom-call | tf_op jit(solution)/shard_map/back_scan/pallas_call | solution.py:231
  60.8 0.0 copy-start.3
  60.8 13.9 %all_to_all.23.bc_ref = bf16[32,48,128]{2,1,0:T(8,128)(2,1)S(1)} all-to-all(bf16[32,48,128]{2,1,0:T(8,128)(2,1)S(1)} %back_scan.1), channel_id=1, replica_groups=mesh['dp'=8,'ctx'=32] {'ctx'}, dimensions={0} | all-to-all | bytes 786432 | tf_op jit(solution)/shard_map/all_to_all | solution.py:219
  74.7 0.0 copy-done.3
  74.7 2.2 %last.1 = (bf16[1,128,2048]{2,1,0:T(8,128)(2,1)}, bf16[1,128,2048]{2,1,0:T(8,128)(2,1)}, f32[1,2048]{1,0:T(1,128)S(1)}) custom-call(s32[1,12]{1,0:T(1,128)S(1)} %copy-done.6, bf16[1,128,2048]{2,1,0:T(8,128)(2,1)S(1)} %copy-done.1, bf16[1,128,2048]{2,1,0:T(8,128)(2,1)S(1)} %copy-done.3, f32[128,2048]{1,0:T(8,128)S(1)} %get-tuple-element.15.pk_ref, ...), custom_call_target="tpu_custom_call" | custom-call | tf_op jit(solution)/shard_map/last/pallas_call | solution.py:233
  76.9 20.2 %psum.7 = f32[2048]{0:T(1024)S(1)} all-reduce(f32[2048]{0:T(1024)S(1)} %bitcast.6), channel_id=1, replica_groups=mesh['dp'=8,'ctx'=32] {'dp'}, use_global_device_ids=true, to_apply=%region_0.0 | all-reduce | flops 2048 | bytes 16384 | tf_op jit(solution)/shard_map/psum | solution.py:237
  97.1 0.6 broadcast_multiply_fusion
  (3 shorter events, 0.0 us)
Async XLA Ops:
  0.6 1.0 %copy-start = (bf16[1,128,2048]{2,1,0:T(8,128)(2,1)S(1)}, bf16[1,128,2048]{2,1,0:T(8,128)(2,1)}, u32[]{:S(2)}) copy-start(bf16[1,128,2048]{2,1,0:T(8,128)(2,1)} %k_ref.5) | copy-start | bytes 1572868
  1.7 1.0 %copy-start.2 = (bf16[1,128,2048]{2,1,0:T(8,128)(2,1)S(1)}, bf16[1,128,2048]{2,1,0:T(8,128)(2,1)}, u32[]{:S(2)}) copy-start(bf16[1,128,2048]{2,1,0:T(8,128)(2,1)} %v_ref.5) | copy-start | bytes 1572868
  2.7 0.7 copy-start.6
  3.4 29.7 %copy-start.7 = (f32[2048]{0:T(1024)S(1)}, f32[2048]{0:T(1024)}, u32[]{:S(2)}) copy-start(f32[2048]{0:T(1024)} %param.10) | copy-start | bytes 24580
  4.3 28.7 %copy-start.5 = (bf16[1,128,2048]{2,1,0:T(8,128)(2,1)S(1)}, bf16[1,128,2048]{2,1,0:T(8,128)(2,1)}, u32[]{:S(2)}) copy-start(bf16[1,128,2048]{2,1,0:T(8,128)(2,1)} %g_ref.1) | copy-start | bytes 1572868
  19.6 13.5 %copy-start.1 = (bf16[1,128,2048]{2,1,0:T(8,128)(2,1)S(1)}, bf16[1,128,2048]{2,1,0:T(8,128)(2,1)}, u32[]{:S(2)}) copy-start(bf16[1,128,2048]{2,1,0:T(8,128)(2,1)} %k_ref.5) | copy-start | bytes 1572868
  19.6 13.5 %copy-start.4 = (bf16[1,128,2048]{2,1,0:T(8,128)(2,1)S(1)}, bf16[1,128,2048]{2,1,0:T(8,128)(2,1)}, u32[]{:S(2)}) copy-start(bf16[1,128,2048]{2,1,0:T(8,128)(2,1)} %q_ref.1) | copy-start | bytes 1572868
  60.8 13.9 %copy-start.3 = (bf16[1,128,2048]{2,1,0:T(8,128)(2,1)S(1)}, bf16[1,128,2048]{2,1,0:T(8,128)(2,1)}, u32[]{:S(2)}) copy-start(bf16[1,128,2048]{2,1,0:T(8,128)(2,1)} %v_ref.5) | copy-start | bytes 1572868

commit v2 on v1

v2 whole, which is shorter than its diff:
```python
import math

import jax
import jax.numpy as jnp
from jax import lax
from jax.experimental import pallas as pl
from jax.experimental.pallas import tpu as pltpu
from jax.sharding import PartitionSpec as P

H = 32
E = 64
PAIR = 2 * E
PAIRS = H // 2
HALF = PAIRS // 2
DOCS = 12
BLK = 128
CORES = 2
NX = 4
NY = 4
ROWS = HALF * E
SLICE = ROWS // NX
TILE = 2 * PAIRS

eps = 1e-05
f32 = jnp.float32
bf16 = jnp.bfloat16
i32 = jnp.int32


def dot(a, b):
    return lax.dot_general(a, b, (((1,), (0,)), ((), ())), preferred_element_type=f32)


def dot_nt(a, b):
    return lax.dot_general(a, b, (((1,), (1,)), ((), ())), preferred_element_type=f32)


def dot_tn(a, b):
    return lax.dot_general(a, b, (((0,), (0,)), ((), ())), preferred_element_type=f32)


def place():
    index = lax.axis_index("ctx")
    chip = index // CORES
    return index % CORES, chip % NX, chip // NX, chip


def bounds(len_ref):
    begins, total = [], jnp.int32(0)
    for k in range(DOCS):
        begins.append(total)
        total = total + len_ref[0, k]
    return begins


def clear(begins, low, size):
    found = jnp.bool_(False)
    for begin in begins:
        found = jnp.logical_or(found, jnp.logical_and(begin >= low, begin < low + size))
    return jnp.where(found, 0.0, 1.0).astype(f32)


def doc_ids(begins, positions):
    ids = jnp.zeros(positions.shape, i32)
    for begin in begins:
        ids = ids + (positions >= begin).astype(i32)
    return ids


def started(begins, end):
    count = jnp.int32(0)
    for begin in begins:
        count = count + (begin < end).astype(i32)
    return count


def positions(dim):
    return lax.broadcasted_iota(i32, (BLK, BLK), dim) + lax.axis_index("ctx") * BLK


def before_mask(begins):
    return doc_ids(begins, positions(0)) == started(begins, lax.axis_index("ctx") * BLK)


def after_mask(begins):
    return doc_ids(begins, positions(0)) == started(begins, (lax.axis_index("ctx") + 1) * BLK)


def pair_mask(begins):
    row, col = positions(0), positions(1)
    mask = jnp.logical_and(row >= col, doc_ids(begins, row) == doc_ids(begins, col))
    return jnp.concatenate([mask, mask], axis=0)


def left_lanes(rows):
    return lax.broadcasted_iota(i32, (rows, PAIR), 1) < E


def pick(cond, a):
    return jnp.where(cond, a, jnp.zeros_like(a))


def heads(a):
    left = left_lanes(a.shape[0])
    return jnp.concatenate([pick(left, a), pick(jnp.logical_not(left), a)], axis=0)


def fold(full):
    return jnp.where(left_lanes(E), full[:E], full[E:])


def beside(a):
    return jnp.concatenate([a[:BLK], a[BLK:]], axis=1)


def split(a):
    high = a.astype(bf16)
    return high, (a - high.astype(f32)).astype(bf16)


def local_pairs(core):
    for i in range(PAIRS):
        pair = (core * HALF + i) % PAIRS
        yield i, pair, pl.ds(pl.multiple_of(pair * PAIR, PAIR), PAIR)


def own_state_kernel(len_ref, k_ref, v_ref, keep_ref, send_ref):
    core, _, _, _ = place()
    after = after_mask(bounds(len_ref))
    for i, _, lanes in local_pairs(core):
        k = pick(after, k_ref[0, :, lanes])
        state = fold(dot_tn(k, v_ref[0, :, lanes])).astype(bf16)
        ref = keep_ref if i < HALF else send_ref
        ref[i % HALF * E : (i % HALF + 1) * E, :] = state


def rows_of(s):
    return pl.ds(pl.multiple_of(s * SLICE, SLICE), SLICE)


def chip_kernel(back):
    def kernel(len_ref, keep_ref, got_ref, *refs):
        core, x, _, chip = place()
        begins = bounds(len_ref)
        if back:
            gain_ref, *outs = refs
            high, low = split(gain_ref[...])
            gain = high.astype(f32) + low.astype(f32)
            gain = gain + (
                got_ref[ROWS : ROWS + PAIRS].astype(f32) + got_ref[ROWS + PAIRS :].astype(f32)
            )
            tile = jnp.concatenate(split(gain), axis=0)
        else:
            outs = refs
        through = clear(begins, (CORES * chip + (0 if back else 1)) * BLK, BLK)
        mine_passes = (core == 1) if back else (core == 0)
        a = jnp.where(mine_passes, through, 1.0)
        b = jnp.where(mine_passes, 1.0, through)
        for o, out in enumerate(outs):
            rows = rows_of((x + o) % NX)
            total = a * keep_ref[rows, :].astype(f32) + b * got_ref[rows, :].astype(f32)
            out[:SLICE] = total.astype(bf16)
            if back:
                out[SLICE:] = tile

    return kernel


def chips(refs, scratch, x):
    for o, ref in enumerate(refs):
        scratch[(x - o) % NX] = ref[...]
    return scratch


def chip_keeps(begins, y):
    return [clear(begins, (NX * y + xx) * CORES * BLK, CORES * BLK) for xx in range(NX)]


def row_kernel(back):
    def kernel(len_ref, r0, r1, r2, r3, out_ref, scratch):
        _, x, y, _ = place()
        keep = chip_keeps(bounds(len_ref), y)
        totals = chips((r0, r1, r2, r3), scratch, x)
        order = range(NX - 1, -1, -1) if back else range(NX)
        row = jnp.zeros((SLICE, PAIR), f32)
        for xx in order:
            row = totals[xx, :SLICE].astype(f32) + keep[xx] * row
        out_ref[:SLICE] = row.astype(bf16)
        if back:
            gain = jnp.zeros((PAIRS, PAIR), f32)
            for xx in range(NX):
                gain = gain + (
                    totals[xx, SLICE : SLICE + PAIRS].astype(f32)
                    + totals[xx, SLICE + PAIRS :].astype(f32)
                )
            out_ref[SLICE:] = jnp.concatenate(split(gain), axis=0)

    return kernel


def carry_kernel(back):
    def kernel(len_ref, r0, r1, r2, r3, a1_ref, a2_ref, *refs):
        _, x, y, _ = place()
        begins = bounds(len_ref)
        keep = chip_keeps(begins, y)
        if back:
            own_ref, a3_ref, o0, o1, o2, o3, gain_ref, scratch, moved, rows = refs
        else:
            o0, o1, o2, o3, scratch, moved = refs
        totals = chips((r0, r1, r2, r3), scratch, x)
        near = (y < NY - 1) if back else (y > 0)
        far = (y < NY - 2) if back else (y > 1)
        between = clear(begins, (y + (1 if back else -1)) * NX * CORES * BLK, NX * CORES * BLK)
        carry = jnp.where(near, 1.0, 0.0) * a1_ref[:SLICE].astype(f32)
        carry = carry + jnp.where(far, between, 0.0) * a2_ref[:SLICE].astype(f32)
        for xx in range(NX - 1, -1, -1) if back else range(NX):
            moved[xx] = carry.astype(bf16)
            carry = totals[xx, :SLICE].astype(f32) + keep[xx] * carry
        for o, out in enumerate((o0, o1, o2, o3)):
            out[...] = moved[(x + o) % NX]
        if back:
            parts = (own_ref[SLICE:], a1_ref[SLICE:], a2_ref[SLICE:], a3_ref[...])
            for o, part in enumerate(parts):
                rows[(y + o) % NY] = part[:PAIRS].astype(f32) + part[PAIRS:].astype(f32)
            gain_ref[...] = (rows[0] + rows[1]) + (rows[2] + rows[3])

    return kernel


def spread_kernel(back):
    def kernel(len_ref, d0, d1, d2, d3, keep_ref, got_ref, mine_ref, send_ref):
        core, x, _, chip = place()
        first = 1 if back else 0
        keep = clear(bounds(len_ref), (CORES * chip + first) * BLK, BLK)
        is_first = core == first
        for o, ref in enumerate((d0, d1, d2, d3)):
            rows = rows_of((x - o) % NX)
            state = jnp.where(is_first, keep_ref[rows, :].astype(f32), got_ref[rows, :].astype(f32))
            c = ref[...].astype(f32)
            d = state + keep * c
            mine_ref[rows, :] = jnp.where(is_first, c, d).astype(bf16)
            send_ref[rows, :] = jnp.where(is_first, d, c).astype(bf16)

    return kernel


def state_of(i, mine_ref, other_ref):
    ref = mine_ref if i < HALF else other_ref
    return heads(ref[i % HALF * E : (i % HALF + 1) * E, :])


def inside_kernel(len_ref, q_ref, k_ref, v_ref, w_ref, att_ref):
    mask = pair_mask(bounds(len_ref))
    for p in range(PAIRS):
        lanes = slice(p * PAIR, (p + 1) * PAIR)
        q2 = heads(q_ref[0, :, lanes])
        weights = pick(mask, dot_nt(q2, k_ref[0, :, lanes])).astype(bf16)
        w_ref[p] = weights
        att_ref[:, lanes] = dot(beside(weights), heads(v_ref[0, :, lanes]))


def attend_kernel(
    len_ref, q_ref, g_ref, gain_ref, att_ref, mine_ref, other_ref,
    out_ref, ga_ref, keep_ref, send_ref, part_ref,
):
    core, _, _, _ = place()
    before = before_mask(bounds(len_ref))
    same = (lax.broadcasted_iota(i32, (PAIR, PAIR), 0) < E) == left_lanes(PAIR)
    ones = jnp.where(same, 1.0 / E, 0.0).astype(bf16)
    ones2 = jnp.concatenate([ones, ones], axis=0)
    for i, pair, lanes in local_pairs(core):
        gain = gain_ref[:, lanes]
        qb = pick(before, q_ref[0, :, lanes])
        att = att_ref[:, lanes] + dot(qb, state_of(i, mine_ref, other_ref))
        dy = g_ref[0, :, lanes].astype(f32)
        d = dy * gain
        means = dot(
            jnp.concatenate(split(jnp.concatenate([att * att, d * att], axis=0)), axis=1), ones2
        )
        r = lax.rsqrt(means[:BLK] + eps)
        normed = att * r
        out_ref[0, :, lanes] = (gain * normed).astype(bf16)
        ga = ((d - normed * (means[BLK:] * r)) * r).astype(bf16)
        ga_ref[:, lanes] = ga
        part_ref[pl.ds(pair, 1), :] = jnp.sum(dy * normed, axis=0, keepdims=True)
        ref = keep_ref if i < HALF else send_ref
        ref[i % HALF * E : (i % HALF + 1) * E, :] = fold(dot_tn(qb, ga)).astype(bf16)
    high, low = split(part_ref[...])
    send_ref[ROWS : ROWS + PAIRS] = high
    send_ref[ROWS + PAIRS :] = low


def grads_kernel(
    len_ref, q_ref, k_ref, v_ref, w_ref, ga_ref, mine_ref, other_ref, gq_ref, pk_ref, pv_ref
):
    core, _, _, _ = place()
    begins = bounds(len_ref)
    mask, before = pair_mask(begins), before_mask(begins)
    for i, pair, lanes in local_pairs(core):
        ga = ga_ref[:, lanes]
        ga2 = heads(ga)
        gw = pick(mask, dot_nt(ga2, v_ref[0, :, lanes])).astype(bf16)
        gq = dot(beside(gw), heads(k_ref[0, :, lanes]))
        gq = gq + dot_nt(pick(before, ga), state_of(i, mine_ref, other_ref))
        gq_ref[0, :, lanes] = gq.astype(bf16)
        pk_ref[:, lanes] = dot_tn(gw, heads(q_ref[0, :, lanes]))
        pv_ref[:, lanes] = dot_tn(w_ref[pair], ga2)


def last_kernel(
    len_ref, k_ref, v_ref, pk_ref, pv_ref, mine_ref, other_ref, gk_ref, gv_ref
):
    core, _, _, _ = place()
    after = after_mask(bounds(len_ref))
    for i, _, lanes in local_pairs(core):
        k = pick(after, k_ref[0, :, lanes])
        v = pick(after, v_ref[0, :, lanes])
        carried = state_of(i, mine_ref, other_ref)
        gk_ref[0, :, lanes] = (pk_ref[:, lanes] + dot_nt(v, carried)).astype(bf16)
        gv_ref[0, :, lanes] = (pv_ref[:, lanes] + dot(k, carried)).astype(bf16)


def call(kernel, outs, n_in, name, scratch=()):
    vmem = pl.BlockSpec(memory_space=pltpu.VMEM)
    smem = pl.BlockSpec(memory_space=pltpu.SMEM)
    return pl.pallas_call(
        kernel,
        out_shape=outs,
        in_specs=[smem] + [vmem] * n_in,
        out_specs=jax.tree.map(lambda _: vmem, outs),
        scratch_shapes=list(scratch),
        compiler_params=pltpu.CompilerParams(vmem_limit_bytes=48 << 20),
        name=name,
    )


def moves(to):
    pairs = []
    for y in range(NY):
        for x in range(NX):
            for core in range(CORES):
                y2, x2, core2 = to(y, x, core)
                pairs.append(
                    ((y * NX + x) * CORES + core, (y2 % NY * NX + x2 % NX) * CORES + core2)
                )
    return pairs


def across(a):
    return lax.ppermute(a, "ctx", moves(lambda y, x, core: (y, x, 1 - core)))


def along_x(arrays):
    return [arrays[0]] + [
        lax.ppermute(arrays[o], "ctx", moves(lambda y, x, core: (y, x + o, core)))
        for o in range(1, NX)
    ]


def along_y(a, o):
    return lax.ppermute(a, "ctx", moves(lambda y, x, core: (y + o, x, core)))


def chain(lengths, keep, send, back, part=None):
    shape = jax.ShapeDtypeStruct
    rows = SLICE + TILE if back else SLICE
    wide, narrow = shape((rows, PAIR), bf16), shape((SLICE, PAIR), bf16)
    half = shape((ROWS, PAIR), bf16)
    name = "back" if back else "ahead"
    stage = pltpu.VMEM((NX, rows, PAIR), bf16)
    moved = pltpu.VMEM((NX, SLICE, PAIR), bf16)
    got = across(send)
    extra = (part,) if back else ()
    totals = call(chip_kernel(back), (wide,) * NX, 2 + len(extra), name + "_chip")(
        lengths, keep, got, *extra
    )
    totals = along_x(totals)
    row = call(row_kernel(back), wide, NX, name + "_row", [stage])(lengths, *totals)
    step = -1 if back else 1
    near, far = along_y(row, step), along_y(row, 2 * step)
    gains = None
    if back:
        rest = along_y(row[SLICE:], 3 * step)
        *out, gains = call(
            carry_kernel(back),
            (narrow,) * NX + (shape((PAIRS, PAIR), f32),),
            NX + 4,
            name + "_carry",
            [stage, moved, pltpu.VMEM((NY, PAIRS, PAIR), f32)],
        )(lengths, *totals, near, far, row, rest)
    else:
        out = call(carry_kernel(back), (narrow,) * NX, NX + 2, name + "_carry", [stage, moved])(
            lengths, *totals, near, far
        )
    out = along_x(out)
    mine, other = call(spread_kernel(back), (half, half), NX + 2, name + "_spread")(
        lengths, *out, keep, got
    )
    return mine, across(other), gains


def over_dp(gains):
    count = lax.axis_size("dp")
    step = 1
    while step < count:
        gains = gains + lax.ppermute(gains, "dp", [(i, i ^ step) for i in range(count)])
        step *= 2
    return gains


def per_device(queries, keys, values, grad_output, out_gain, doc_lengths):
    shape = jax.ShapeDtypeStruct
    full = shape(queries.shape, bf16)
    plain = shape((BLK, H * E), f32)
    half = shape((ROWS, PAIR), bf16)
    gain = out_gain.reshape(1, H * E)
    keep, send = call(own_state_kernel, (half, half), 2, "own_state")(doc_lengths, keys, values)
    weights, inside = call(
        inside_kernel, (shape((PAIRS, 2 * BLK, BLK), bf16), plain), 3, "inside"
    )(doc_lengths, queries, keys, values)
    mine, other, _ = chain(doc_lengths, keep, send, False)
    output, grad_att, keep, send, part = call(
        attend_kernel,
        (
            full,
            shape((BLK, H * E), bf16),
            half,
            shape((ROWS + TILE, PAIR), bf16),
            shape((PAIRS, PAIR), f32),
        ),
        6,
        "attend",
    )(doc_lengths, queries, grad_output, gain, inside, mine, other)
    grad_q, part_k, part_v = call(grads_kernel, (full, plain, plain), 7, "grads")(
        doc_lengths, queries, keys, values, weights, grad_att, mine, other
    )
    mine, other, gains = chain(doc_lengths, keep, send, True, part)
    grad_k, grad_v = call(last_kernel, (full, full), 6, "last")(
        doc_lengths, keys, values, part_k, part_v, mine, other
    )
    total_tokens = lax.axis_size("dp") * BLK * lax.axis_size("ctx")
    grad_gain = over_dp(gains).reshape(H * E) / math.sqrt(total_tokens)
    return (output, grad_q, grad_k, grad_v, grad_gain)


def solution(mesh):
    spread = P("dp", "ctx", None)
    return jax.shard_map(
        per_device,
        mesh=mesh,
        in_specs=(spread, spread, spread, spread, P(), P("dp", None)),
        out_specs=(spread, spread, spread, spread, P()),
        check_vma=False,
    )
```

time: 98.1 us -> 89.4 us (0.911)
  blocking collectives: 75.7 us -> 0 us
  starting transfers between devices: 0 us -> 38.2 us
  waiting for transfers between devices: 0 us -> 24.3 us
  Pallas kernels: 18 us -> 21.8 us
    all_to_all x4 -> x0, blocking collectives: 55.4 us -> none  [swap(): return lax.all_to_all(a, 'ctx', 0, 0, tiled=True)]
    ppermute x0 -> x24, starting transfers between devices: none -> 38.2 us  [the longest x12 20.4 us: along_x(): lax.ppermute(arrays[o], 'ctx', moves(lambda y, x, core: (y, x + o, core)))]
    ppermute x0 -> x24, waiting for transfers between devices: none -> 24.3 us  [the longest x5 9.13 us: along_y(): return lax.ppermute(a, 'ctx', moves(lambda y, x, core: (y + o, x, core)))]
    psum x1 -> x0, blocking collectives: 20.2 us -> none  [per_device(): lax.psum(gain_terms.reshape(H * E), 'dp') / math.sqrt(total_tokens)]
    pallas_call x5 -> x13, Pallas kernels: 18 us -> 21.8 us  [the longest x1 6.66 us: per_device(): call(attend_kernel, (full, shape((BLK, H * E), bf16), half, shape((ROWS +...]
  transfers between devices with their start and end apart: 0 -> 24, of which waited for: 0 -> 14; matrix products, arithmetic and copies ran while one was open for 0% -> 1% of each run, Pallas kernels for 0% -> 8%
where the time goes in v2:
time: 89.4 us; the launch traced here: 88.6 us
  starting transfers between devices  38.2 us (43%)
  waiting for transfers between devices  24.3 us (27%)
  Pallas kernels  21.8 us (24%)
  local copies, waits for them, and re-layouts  2.76 us (3%)
    ppermute x12, starting transfers between devices, along_x(): lax.ppermute(arrays[o], 'ctx', moves(lambda y, x, core: (y, x + o, core)))  20.4 us
    ppermute x3, starting transfers between devices, over_dp(): lax.ppermute(gains, 'dp', [(i, i ^ step) for i in range(count)])  12 us
    ppermute x5, waiting for transfers between devices, along_y(): return lax.ppermute(a, 'ctx', moves(lambda y, x, core: (y + o, x, core)))  9.13 us
    ppermute x12, waiting for transfers between devices, along_x(): lax.ppermute(arrays[o], 'ctx', moves(lambda y, x, core: (y, x + o, core)))  8.74 us
    pallas_call x1, Pallas kernels, per_device(): call(attend_kernel, (full, shape((BLK, H * E), bf16), half, shape((ROWS +...  6.66 us
    pallas_call x1, Pallas kernels, per_device(): call(grads_kernel, (full, plain, plain), 7, 'grads')  5.07 us
    ppermute x5, starting transfers between devices, along_y(): return lax.ppermute(a, 'ctx', moves(lambda y, x, core: (y + o, x, core)))  5.03 us
    ppermute x3, waiting for transfers between devices, over_dp(): lax.ppermute(gains, 'dp', [(i, i ^ step) for i in range(count)])  3.36 us
  transfers between devices with their start and end apart: 24, of which 14 were waited for; matrix products, arithmetic and copies ran while one was open for 1% of the time, Pallas kernels for 8%

profile of v2, /device:TPU:2, one launch (start us, length us, event | category | flops | bytes accessed | tf_op | source)
XLA Modules:
  0.0 88.6 jit_solution(8588845904462644876)
XLA Ops:
  6.5 1.6 %collective-permute-start.1 = (bf16[128,128]{1,0:T(8,128)(2,1)S(1)}, bf16[128,128]{1,0:T(8,128)(2,1)S(1)}, u32[]{:S(2)}, u32[]{:S(2)}) collective-permute-start(bf16[128,128]{1,0:T(8,128)(2,1)S(1)} %get-tuple-element.44), channel_id=1, source_target_pairs={{0,2},{1,3},{2,4},{3,5},{4,6},{5,7},{6,0},{7,1},{8,10},{9,11},{10,... | collective-permute-start | bytes 98312 | tf_op jit(solution)/shard_map/ppermute | solution.py:355
  8.1 2.8 %collective-permute-start.2 = (bf16[128,128]{1,0:T(8,128)(2,1)S(1)}, bf16[128,128]{1,0:T(8,128)(2,1)S(1)}, u32[]{:S(2)}, u32[]{:S(2)}) collective-permute-start(bf16[128,128]{1,0:T(8,128)(2,1)S(1)} %get-tuple-element.45), channel_id=1, source_target_pairs={{0,4},{1,5},{2,6},{3,7},{4,0},{5,1},{6,2},{7,3},{8,12},{9,13},{10,... | collective-permute-start | bytes 98312 | tf_op jit(solution)/shard_map/ppermute | solution.py:355
  11.3 2.3 %collective-permute-done.2.r2 = bf16[128,128]{1,0:T(8,128)(2,1)S(1)} collective-permute-done((bf16[128,128]{1,0:T(8,128)(2,1)S(1)}, bf16[128,128]{1,0:T(8,128)(2,1)S(1)}, u32[]{:S(2)}, u32[]{:S(2)}) %collective-permute-start.2) | collective-permute-done | bytes 32800 | tf_op jit(solution)/shard_map/ppermute | solution.py:355
  15.5 1.9 %collective-permute-start.5 = (bf16[128,128]{1,0:T(8,128)(2,1)S(1)}, bf16[128,128]{1,0:T(8,128)(2,1)S(1)}, u32[]{:S(2)}, u32[]{:S(2)}) collective-permute-start(bf16[128,128]{1,0:T(8,128)(2,1)S(1)} %ahead_row.1), channel_id=1, source_target_pairs={{0,16},{1,17},{2,18},{3,19},{4,20},{5,21},{6,22},{7,23},{8,24},{9,... | collective-permute-start | bytes 98312 | tf_op jit(solution)/shard_map/ppermute | solution.py:361
  18.2 2.9 %collective-permute-done.5.a2_ref = bf16[128,128]{1,0:T(8,128)(2,1)S(1)} collective-permute-done((bf16[128,128]{1,0:T(8,128)(2,1)S(1)}, bf16[128,128]{1,0:T(8,128)(2,1)S(1)}, u32[]{:S(2)}, u32[]{:S(2)}) %collective-permute-start.5) | collective-permute-done | bytes 32800 | tf_op jit(solution)/shard_map/ppermute | solution.py:361
  21.0 1.6 %collective-permute-done.4.a1_ref = bf16[128,128]{1,0:T(8,128)(2,1)S(1)} collective-permute-done((bf16[128,128]{1,0:T(8,128)(2,1)S(1)}, bf16[128,128]{1,0:T(8,128)(2,1)S(1)}, u32[]{:S(2)}, u32[]{:S(2)}) %collective-permute-start.4) | collective-permute-done | bytes 32800 | tf_op jit(solution)/shard_map/ppermute | solution.py:361
  24.6 2.6 %collective-permute-start.7 = (bf16[128,128]{1,0:T(8,128)(2,1)S(1)}, bf16[128,128]{1,0:T(8,128)(2,1)S(1)}, u32[]{:S(2)}, u32[]{:S(2)}) collective-permute-start(bf16[128,128]{1,0:T(8,128)(2,1)S(1)} %get-tuple-element.49), channel_id=1, source_target_pairs={{0,4},{1,5},{2,6},{3,7},{4,0},{5,1},{6,2},{7,3},{8,12},{9,13},{10,... | collective-permute-start | bytes 98312 | tf_op jit(solution)/shard_map/ppermute | solution.py:355
  27.2 2.0 %collective-permute-start.8 = (bf16[128,128]{1,0:T(8,128)(2,1)S(1)}, bf16[128,128]{1,0:T(8,128)(2,1)S(1)}, u32[]{:S(2)}, u32[]{:S(2)}) collective-permute-start(bf16[128,128]{1,0:T(8,128)(2,1)S(1)} %get-tuple-element.50), channel_id=1, source_target_pairs={{0,6},{1,7},{2,0},{3,1},{4,2},{5,3},{6,4},{7,5},{8,14},{9,15},{10,... | collective-permute-start | bytes 98312 | tf_op jit(solution)/shard_map/ppermute | solution.py:355
  31.9 1.5 %inside.1 = (bf16[16,256,128]{2,1,0:T(8,128)(2,1)S(1)}, f32[128,2048]{1,0:T(8,128)S(1)}) custom-call(s32[1,12]{1,0:T(1,128)S(1)} %copy-done.6, bf16[1,128,2048]{2,1,0:T(8,128)(2,1)S(1)} %copy-done.4, bf16[1,128,2048]{2,1,0:T(8,128)(2,1)S(1)} %copy-done.1, bf16[1,128,2048]{2,1,0:T(8,128)(2,1)S(1)} %copy-done.3), custom_call_target="tpu_custom_call" | custom-call | tf_op jit(solution)/shard_map/inside/pallas_call | solution.py:418
  33.5 6.7 %attend.1 = (bf16[1,128,2048]{2,1,0:T(8,128)(2,1)}, bf16[128,2048]{1,0:T(8,128)(2,1)S(1)}, bf16[512,128]{1,0:T(8,128)(2,1)S(1)}, bf16[544,128]{1,0:T(8,128)(2,1)S(1)}, f32[16,128]{1,0:T(8,128)S(1)}) custom-call(s32[1,12]{1,0:T(1,128)S(1)} %copy-done.6, bf16[1,128,2048]{2,1,0:T(8,128)(2,1)S(1)} %copy-done.4, bf16[1,128,2048]{2,1,0:T(8,128)(2,1)S(1)} %copy-done.5, ...), custom_call_target="tpu_custom_call" | custom-call | tf_op jit(solution)/shard_map/attend/pallas_call | solution.py:422
  42.2 1.6 %collective-permute-start.11 = (bf16[160,128]{1,0:T(8,128)(2,1)S(1)}, bf16[160,128]{1,0:T(8,128)(2,1)S(1)}, u32[]{:S(2)}, u32[]{:S(2)}) collective-permute-start(bf16[160,128]{1,0:T(8,128)(2,1)S(1)} %get-tuple-element.63), channel_id=1, source_target_pairs={{0,2},{1,3},{2,4},{3,5},{4,6},{5,7},{6,0},{7,1},{8,10},{9,11},{10,... | collective-permute-start | bytes 122888 | tf_op jit(solution)/shard_map/ppermute | solution.py:355
  43.8 2.6 %collective-permute-start.12 = (bf16[160,128]{1,0:T(8,128)(2,1)S(1)}, bf16[160,128]{1,0:T(8,128)(2,1)S(1)}, u32[]{:S(2)}, u32[]{:S(2)}) collective-permute-start(bf16[160,128]{1,0:T(8,128)(2,1)S(1)} %get-tuple-element.64), channel_id=1, source_target_pairs={{0,4},{1,5},{2,6},{3,7},{4,0},{5,1},{6,2},{7,3},{8,12},{9,13},{10,... | collective-permute-start | bytes 122888 | tf_op jit(solution)/shard_map/ppermute | solution.py:355
  47.1 2.3 %collective-permute-done.12.r2 = bf16[160,128]{1,0:T(8,128)(2,1)S(1)} collective-permute-done((bf16[160,128]{1,0:T(8,128)(2,1)S(1)}, bf16[160,128]{1,0:T(8,128)(2,1)S(1)}, u32[]{:S(2)}, u32[]{:S(2)}) %collective-permute-start.12) | collective-permute-done | bytes 40992 | tf_op jit(solution)/shard_map/ppermute | solution.py:355
  51.5 1.8 %collective-permute-start.14 = (bf16[160,128]{1,0:T(8,128)(2,1)S(1)}, bf16[160,128]{1,0:T(8,128)(2,1)S(1)}, u32[]{:S(2)}, u32[]{:S(2)}) collective-permute-start(bf16[160,128]{1,0:T(8,128)(2,1)S(1)} %back_row.1.refs_0_), channel_id=1, source_target_pairs={{0,24},{1,25},{2,26},{3,27},{4,28},{5,29},{6,30},{7,31},{8,0},{9,1... | collective-permute-start | bytes 122888 | tf_op jit(solution)/shard_map/ppermute | solution.py:361
  53.5 4.7 %collective-permute-done.16.refs_1_ = bf16[32,128]{1,0:T(8,128)(2,1)S(1)} collective-permute-done((bf16[32,128]{1,0:T(8,128)(2,1)S(1)}, bf16[32,128]{1,0:T(8,128)(2,1)S(1)}, u32[]{:S(2)}, u32[]{:S(2)}) %collective-permute-start.16) | collective-permute-done | bytes 8224 | tf_op jit(solution)/shard_map/ppermute | solution.py:361
  59.1 2.6 %collective-permute-start.18 = (bf16[128,128]{1,0:T(8,128)(2,1)S(1)}, bf16[128,128]{1,0:T(8,128)(2,1)S(1)}, u32[]{:S(2)}, u32[]{:S(2)}) collective-permute-start(bf16[128,128]{1,0:T(8,128)(2,1)S(1)} %get-tuple-element.68), channel_id=1, source_target_pairs={{0,4},{1,5},{2,6},{3,7},{4,0},{5,1},{6,2},{7,3},{8,12},{9,13},{10,... | collective-permute-start | bytes 98312 | tf_op jit(solution)/shard_map/ppermute | solution.py:355
  61.7 2.0 %collective-permute-start.19 = (bf16[128,128]{1,0:T(8,128)(2,1)S(1)}, bf16[128,128]{1,0:T(8,128)(2,1)S(1)}, u32[]{:S(2)}, u32[]{:S(2)}) collective-permute-start(bf16[128,128]{1,0:T(8,128)(2,1)S(1)} %get-tuple-element.69), channel_id=1, source_target_pairs={{0,6},{1,7},{2,0},{3,1},{4,2},{5,3},{6,4},{7,5},{8,14},{9,15},{10,... | collective-permute-start | bytes 98312 | tf_op jit(solution)/shard_map/ppermute | solution.py:355
  63.7 1.9 %collective-permute-start.21 = (f32[16,128]{1,0:T(8,128)S(1)}, f32[16,128]{1,0:T(8,128)S(1)}, u32[]{:S(2)}, u32[]{:S(2)}) collective-permute-start(f32[16,128]{1,0:T(8,128)S(1)} %get-tuple-element.74), channel_id=1, source_target_pairs={{0,32},{32,0},{64,96},{96,64},{128,160},{160,128},{192,224},{224,1... | collective-permute-start | bytes 24584 | tf_op jit(solution)/shard_map/ppermute | solution.py:406
  65.7 1.7 %collective-permute-done.21 = f32[16,128]{1,0:T(8,128)S(1)} collective-permute-done((f32[16,128]{1,0:T(8,128)S(1)}, f32[16,128]{1,0:T(8,128)S(1)}, u32[]{:S(2)}, u32[]{:S(2)}) %collective-permute-start.21) | collective-permute-done | bytes 8224 | tf_op jit(solution)/shard_map/ppermute | solution.py:406
  67.4 3.3 %collective-permute-start.22 = (f32[16,128]{1,0:T(8,128)S(1)}, f32[16,128]{1,0:T(8,128)S(1)}, u32[]{:S(2)}, u32[]{:S(2)}) collective-permute-start(f32[16,128]{1,0:T(8,128)S(1)} %add.9), channel_id=1, source_target_pairs={{0,64},{32,96},{64,0},{96,32},{128,192},{160,224},{192,128},{224,1... | collective-permute-start | bytes 24584 | tf_op jit(solution)/shard_map/ppermute | solution.py:406
  70.7 1.6 %collective-permute-done.22 = f32[16,128]{1,0:T(8,128)S(1)} collective-permute-done((f32[16,128]{1,0:T(8,128)S(1)}, f32[16,128]{1,0:T(8,128)S(1)}, u32[]{:S(2)}, u32[]{:S(2)}) %collective-permute-start.22) | collective-permute-done | bytes 8224 | tf_op jit(solution)/shard_map/ppermute | solution.py:406
  72.3 6.8 %collective-permute-start.23 = (f32[16,128]{1,0:T(8,128)S(1)}, f32[16,128]{1,0:T(8,128)S(1)}, u32[]{:S(2)}, u32[]{:S(2)}) collective-permute-start(f32[16,128]{1,0:T(8,128)S(1)} %add.10), channel_id=1, source_target_pairs={{0,128},{32,160},{64,192},{96,224},{128,0},{160,32},{192,64},{224,... | collective-permute-start | bytes 24584 | tf_op jit(solution)/shard_map/ppermute | solution.py:406
  79.2 5.1 %grads.1 = (bf16[1,128,2048]{2,1,0:T(8,128)(2,1)}, f32[128,2048]{1,0:T(8,128)S(1)}, f32[128,2048]{1,0:T(8,128)S(1)}) custom-call(s32[1,12]{1,0:T(1,128)S(1)} %copy-done.6, bf16[1,128,2048]{2,1,0:T(8,128)(2,1)S(1)} %copy-done.4, bf16[1,128,2048]{2,1,0:T(8,128)(2,1)S(1)} %copy-done.1, bf16[1,128,2048]{2,1,0:T(8,128)(2,1)S(1)} %copy-done.3, ...), custom_call_target="tpu_custom_call" | custom-call | tf_op jit(solution)/shard_map/grads/pallas_call | solution.py:434
  86.3 2.2 %last.1 = (bf16[1,128,2048]{2,1,0:T(8,128)(2,1)}, bf16[1,128,2048]{2,1,0:T(8,128)(2,1)}) custom-call(s32[1,12]{1,0:T(1,128)S(1)} %copy-done.6, bf16[1,128,2048]{2,1,0:T(8,128)(2,1)S(1)} %copy-done.1, bf16[1,128,2048]{2,1,0:T(8,128)(2,1)S(1)} %copy-done.3, f32[128,2048]{1,0:T(8,128)S(1)} %get-tuple-element.57.pk_ref, ...), custom_call_target="tpu_custom_call" | custom-call | tf_op jit(solution)/shard_map/last/pallas_call | solution.py:438
  (57 shorter events, 21.4 us)
Async XLA Ops:
  4.4 1.4 %collective-permute-start = (bf16[512,128]{1,0:T(8,128)(2,1)S(1)}, bf16[512,128]{1,0:T(8,128)(2,1)S(1)}, u32[]{:S(2)}, u32[]{:S(2)}) collective-permute-start(bf16[512,128]{1,0:T(8,128)(2,1)S(1)} %get-tuple-element.42), channel_id=1, source_target_pairs={{0,1},{1,0},{2,3},{3,2},{4,5},{5,4},{6,7},{7,6},{8,9},{9,8},{10,11... | collective-permute-start | bytes 393224 | tf_op jit(solution)/shard_map/ppermute | solution.py:350
  6.5 4.8 %collective-permute-start.1 = (bf16[128,128]{1,0:T(8,128)(2,1)S(1)}, bf16[128,128]{1,0:T(8,128)(2,1)S(1)}, u32[]{:S(2)}, u32[]{:S(2)}) collective-permute-start(bf16[128,128]{1,0:T(8,128)(2,1)S(1)} %get-tuple-element.44), channel_id=1, source_target_pairs={{0,2},{1,3},{2,4},{3,5},{4,6},{5,7},{6,0},{7,1},{8,10},{9,11},{10,... | collective-permute-start | bytes 98312 | tf_op jit(solution)/shard_map/ppermute | solution.py:355
  8.1 5.5 %collective-permute-start.2 = (bf16[128,128]{1,0:T(8,128)(2,1)S(1)}, bf16[128,128]{1,0:T(8,128)(2,1)S(1)}, u32[]{:S(2)}, u32[]{:S(2)}) collective-permute-start(bf16[128,128]{1,0:T(8,128)(2,1)S(1)} %get-tuple-element.45), channel_id=1, source_target_pairs={{0,4},{1,5},{2,6},{3,7},{4,0},{5,1},{6,2},{7,3},{8,12},{9,13},{10,... | collective-permute-start | bytes 98312 | tf_op jit(solution)/shard_map/ppermute | solution.py:355
  10.9 3.9 %collective-permute-start.3 = (bf16[128,128]{1,0:T(8,128)(2,1)S(1)}, bf16[128,128]{1,0:T(8,128)(2,1)S(1)}, u32[]{:S(2)}, u32[]{:S(2)}) collective-permute-start(bf16[128,128]{1,0:T(8,128)(2,1)S(1)} %get-tuple-element.46), channel_id=1, source_target_pairs={{0,6},{1,7},{2,0},{3,1},{4,2},{5,3},{6,4},{7,5},{8,14},{9,15},{10,... | collective-permute-start | bytes 98312 | tf_op jit(solution)/shard_map/ppermute | solution.py:355
  15.5 5.5 %collective-permute-start.5 = (bf16[128,128]{1,0:T(8,128)(2,1)S(1)}, bf16[128,128]{1,0:T(8,128)(2,1)S(1)}, u32[]{:S(2)}, u32[]{:S(2)}) collective-permute-start(bf16[128,128]{1,0:T(8,128)(2,1)S(1)} %ahead_row.1), channel_id=1, source_target_pairs={{0,16},{1,17},{2,18},{3,19},{4,20},{5,21},{6,22},{7,23},{8,24},{9,... | collective-permute-start | bytes 98312 | tf_op jit(solution)/shard_map/ppermute | solution.py:361
  17.5 5.1 %collective-permute-start.4 = (bf16[128,128]{1,0:T(8,128)(2,1)S(1)}, bf16[128,128]{1,0:T(8,128)(2,1)S(1)}, u32[]{:S(2)}, u32[]{:S(2)}) collective-permute-start(bf16[128,128]{1,0:T(8,128)(2,1)S(1)} %ahead_row.1), channel_id=1, source_target_pairs={{0,8},{1,9},{2,10},{3,11},{4,12},{5,13},{6,14},{7,15},{8,16},{9,17... | collective-permute-start | bytes 98312 | tf_op jit(solution)/shard_map/ppermute | solution.py:361
  23.3 5.9 %collective-permute-start.6 = (bf16[128,128]{1,0:T(8,128)(2,1)S(1)}, bf16[128,128]{1,0:T(8,128)(2,1)S(1)}, u32[]{:S(2)}, u32[]{:S(2)}) collective-permute-start(bf16[128,128]{1,0:T(8,128)(2,1)S(1)} %get-tuple-element.48), channel_id=1, source_target_pairs={{0,2},{1,3},{2,4},{3,5},{4,6},{5,7},{6,0},{7,1},{8,10},{9,11},{10,... | collective-permute-start | bytes 98312 | tf_op jit(solution)/shard_map/ppermute | solution.py:355
  24.6 5.4 %collective-permute-start.7 = (bf16[128,128]{1,0:T(8,128)(2,1)S(1)}, bf16[128,128]{1,0:T(8,128)(2,1)S(1)}, u32[]{:S(2)}, u32[]{:S(2)}) collective-permute-start(bf16[128,128]{1,0:T(8,128)(2,1)S(1)} %get-tuple-element.49), channel_id=1, source_target_pairs={{0,4},{1,5},{2,6},{3,7},{4,0},{5,1},{6,2},{7,3},{8,12},{9,13},{10,... | collective-permute-start | bytes 98312 | tf_op jit(solution)/shard_map/ppermute | solution.py:355
  27.2 3.9 %collective-permute-start.8 = (bf16[128,128]{1,0:T(8,128)(2,1)S(1)}, bf16[128,128]{1,0:T(8,128)(2,1)S(1)}, u32[]{:S(2)}, u32[]{:S(2)}) collective-permute-start(bf16[128,128]{1,0:T(8,128)(2,1)S(1)} %get-tuple-element.50), channel_id=1, source_target_pairs={{0,6},{1,7},{2,0},{3,1},{4,2},{5,3},{6,4},{7,5},{8,14},{9,15},{10,... | collective-permute-start | bytes 98312 | tf_op jit(solution)/shard_map/ppermute | solution.py:355
  31.8 1.7 %collective-permute-start.9 = (bf16[512,128]{1,0:T(8,128)(2,1)S(1)}, bf16[512,128]{1,0:T(8,128)(2,1)S(1)}, u32[]{:S(2)}, u32[]{:S(2)}) collective-permute-start(bf16[512,128]{1,0:T(8,128)(2,1)S(1)} %get-tuple-element.52), channel_id=1, source_target_pairs={{0,1},{1,0},{2,3},{3,2},{4,5},{5,4},{6,7},{7,6},{8,9},{9,8},{10,11... | collective-permute-start | bytes 393224 | tf_op jit(solution)/shard_map/ppermute | solution.py:350
  40.1 1.5 %collective-permute-start.10 = (bf16[544,128]{1,0:T(8,128)(2,1)S(1)}, bf16[544,128]{1,0:T(8,128)(2,1)S(1)}, u32[]{:S(2)}, u32[]{:S(2)}) collective-permute-start(bf16[544,128]{1,0:T(8,128)(2,1)S(1)} %get-tuple-element.60), channel_id=1, source_target_pairs={{0,1},{1,0},{2,3},{3,2},{4,5},{5,4},{6,7},{7,6},{8,9},{9,8},{10,11... | collective-permute-start | bytes 417800 | tf_op jit(solution)/shard_map/ppermute | solution.py:350
  42.2 4.8 %collective-permute-start.11 = (bf16[160,128]{1,0:T(8,128)(2,1)S(1)}, bf16[160,128]{1,0:T(8,128)(2,1)S(1)}, u32[]{:S(2)}, u32[]{:S(2)}) collective-permute-start(bf16[160,128]{1,0:T(8,128)(2,1)S(1)} %get-tuple-element.63), channel_id=1, source_target_pairs={{0,2},{1,3},{2,4},{3,5},{4,6},{5,7},{6,0},{7,1},{8,10},{9,11},{10,... | collective-permute-start | bytes 122888 | tf_op jit(solution)/shard_map/ppermute | solution.py:355
  43.8 5.6 %collective-permute-start.12 = (bf16[160,128]{1,0:T(8,128)(2,1)S(1)}, bf16[160,128]{1,0:T(8,128)(2,1)S(1)}, u32[]{:S(2)}, u32[]{:S(2)}) collective-permute-start(bf16[160,128]{1,0:T(8,128)(2,1)S(1)} %get-tuple-element.64), channel_id=1, source_target_pairs={{0,4},{1,5},{2,6},{3,7},{4,0},{5,1},{6,2},{7,3},{8,12},{9,13},{10,... | collective-permute-start | bytes 122888 | tf_op jit(solution)/shard_map/ppermute | solution.py:355
  46.4 4.0 %collective-permute-start.13 = (bf16[160,128]{1,0:T(8,128)(2,1)S(1)}, bf16[160,128]{1,0:T(8,128)(2,1)S(1)}, u32[]{:S(2)}, u32[]{:S(2)}) collective-permute-start(bf16[160,128]{1,0:T(8,128)(2,1)S(1)} %get-tuple-element.65), channel_id=1, source_target_pairs={{0,6},{1,7},{2,0},{3,1},{4,2},{5,3},{6,4},{7,5},{8,14},{9,15},{10,... | collective-permute-start | bytes 122888 | tf_op jit(solution)/shard_map/ppermute | solution.py:355
  51.1 7.1 %collective-permute-start.15 = (bf16[160,128]{1,0:T(8,128)(2,1)S(1)}, bf16[160,128]{1,0:T(8,128)(2,1)S(1)}, u32[]{:S(2)}, u32[]{:S(2)}) collective-permute-start(bf16[160,128]{1,0:T(8,128)(2,1)S(1)} %back_row.1.refs_0_), channel_id=1, source_target_pairs={{0,16},{1,17},{2,18},{3,19},{4,20},{5,21},{6,22},{7,23},{8,24},{9,... | collective-permute-start | bytes 122888 | tf_op jit(solution)/shard_map/ppermute | solution.py:361
  51.5 6.7 %collective-permute-start.14 = (bf16[160,128]{1,0:T(8,128)(2,1)S(1)}, bf16[160,128]{1,0:T(8,128)(2,1)S(1)}, u32[]{:S(2)}, u32[]{:S(2)}) collective-permute-start(bf16[160,128]{1,0:T(8,128)(2,1)S(1)} %back_row.1.refs_0_), channel_id=1, source_target_pairs={{0,24},{1,25},{2,26},{3,27},{4,28},{5,29},{6,30},{7,31},{8,0},{9,1... | collective-permute-start | bytes 122888 | tf_op jit(solution)/shard_map/ppermute | solution.py:361
  53.4 4.9 %collective-permute-start.16 = (bf16[32,128]{1,0:T(8,128)(2,1)S(1)}, bf16[32,128]{1,0:T(8,128)(2,1)S(1)}, u32[]{:S(2)}, u32[]{:S(2)}) collective-permute-start(bf16[32,128]{1,0:T(8,128)(2,1)S(1)} %slice.4), channel_id=1, source_target_pairs={{0,8},{1,9},{2,10},{3,11},{4,12},{5,13},{6,14},{7,15},{8,16},{9,17... | collective-permute-start | bytes 24584 | tf_op jit(solution)/shard_map/ppermute | solution.py:361
  58.9 25.3 %collective-permute-start.17 = (bf16[128,128]{1,0:T(8,128)(2,1)S(1)}, bf16[128,128]{1,0:T(8,128)(2,1)S(1)}, u32[]{:S(2)}, u32[]{:S(2)}) collective-permute-start(bf16[128,128]{1,0:T(8,128)(2,1)S(1)} %get-tuple-element.67), channel_id=1, source_target_pairs={{0,2},{1,3},{2,4},{3,5},{4,6},{5,7},{6,0},{7,1},{8,10},{9,11},{10,... | collective-permute-start | bytes 98312 | tf_op jit(solution)/shard_map/ppermute | solution.py:355
  59.1 25.1 %collective-permute-start.18 = (bf16[128,128]{1,0:T(8,128)(2,1)S(1)}, bf16[128,128]{1,0:T(8,128)(2,1)S(1)}, u32[]{:S(2)}, u32[]{:S(2)}) collective-permute-start(bf16[128,128]{1,0:T(8,128)(2,1)S(1)} %get-tuple-element.68), channel_id=1, source_target_pairs={{0,4},{1,5},{2,6},{3,7},{4,0},{5,1},{6,2},{7,3},{8,12},{9,13},{10,... | collective-permute-start | bytes 98312 | tf_op jit(solution)/shard_map/ppermute | solution.py:355
  61.7 22.5 %collective-permute-start.19 = (bf16[128,128]{1,0:T(8,128)(2,1)S(1)}, bf16[128,128]{1,0:T(8,128)(2,1)S(1)}, u32[]{:S(2)}, u32[]{:S(2)}) collective-permute-start(bf16[128,128]{1,0:T(8,128)(2,1)S(1)} %get-tuple-element.69), channel_id=1, source_target_pairs={{0,6},{1,7},{2,0},{3,1},{4,2},{5,3},{6,4},{7,5},{8,14},{9,15},{10,... | collective-permute-start | bytes 98312 | tf_op jit(solution)/shard_map/ppermute | solution.py:355
  63.7 3.7 %collective-permute-start.21 = (f32[16,128]{1,0:T(8,128)S(1)}, f32[16,128]{1,0:T(8,128)S(1)}, u32[]{:S(2)}, u32[]{:S(2)}) collective-permute-start(f32[16,128]{1,0:T(8,128)S(1)} %get-tuple-element.74), channel_id=1, source_target_pairs={{0,32},{32,0},{64,96},{96,64},{128,160},{160,128},{192,224},{224,1... | collective-permute-start | bytes 24584 | tf_op jit(solution)/shard_map/ppermute | solution.py:406
  67.4 4.9 %collective-permute-start.22 = (f32[16,128]{1,0:T(8,128)S(1)}, f32[16,128]{1,0:T(8,128)S(1)}, u32[]{:S(2)}, u32[]{:S(2)}) collective-permute-start(f32[16,128]{1,0:T(8,128)S(1)} %add.9), channel_id=1, source_target_pairs={{0,64},{32,96},{64,0},{96,32},{128,192},{160,224},{192,128},{224,1... | collective-permute-start | bytes 24584 | tf_op jit(solution)/shard_map/ppermute | solution.py:406
  72.3 12.7 %collective-permute-start.23 = (f32[16,128]{1,0:T(8,128)S(1)}, f32[16,128]{1,0:T(8,128)S(1)}, u32[]{:S(2)}, u32[]{:S(2)}) collective-permute-start(f32[16,128]{1,0:T(8,128)S(1)} %add.10), channel_id=1, source_target_pairs={{0,128},{32,160},{64,192},{96,224},{128,0},{160,32},{192,64},{224,... | collective-permute-start | bytes 24584 | tf_op jit(solution)/shard_map/ppermute | solution.py:406
  84.9 1.4 %collective-permute-start.20 = (bf16[512,128]{1,0:T(8,128)(2,1)S(1)}, bf16[512,128]{1,0:T(8,128)(2,1)S(1)}, u32[]{:S(2)}, u32[]{:S(2)}) collective-permute-start(bf16[512,128]{1,0:T(8,128)(2,1)S(1)} %get-tuple-element.71), channel_id=1, source_target_pairs={{0,1},{1,0},{2,3},{3,2},{4,5},{5,4},{6,7},{7,6},{8,9},{9,8},{10,11... | collective-permute-start | bytes 393224 | tf_op jit(solution)/shard_map/ppermute | solution.py:350
  (8 other events, 90.5 us)

commit v3 on v2

v3 whole, which is shorter than its diff:
```python
import math

import jax
import jax.numpy as jnp
from jax import lax
from jax.experimental import pallas as pl
from jax.experimental.pallas import tpu as pltpu
from jax.sharding import PartitionSpec as P

H = 32
E = 64
PAIR = 2 * E
PAIRS = H // 2
DOCS = 12
BLK = 128
GROUP = 4
SHARE = PAIRS // GROUP
ROWS = SHARE * E
TILE = 2 * PAIRS
REACH = 3

eps = 1e-05
f32 = jnp.float32
bf16 = jnp.bfloat16
i32 = jnp.int32


def dot(a, b):
    return lax.dot_general(a, b, (((1,), (0,)), ((), ())), preferred_element_type=f32)


def dot_nt(a, b):
    return lax.dot_general(a, b, (((1,), (1,)), ((), ())), preferred_element_type=f32)


def dot_tn(a, b):
    return lax.dot_general(a, b, (((0,), (0,)), ((), ())), preferred_element_type=f32)


def place():
    index = lax.axis_index("ctx")
    return index % GROUP, index // GROUP


def bounds(len_ref):
    begins, total = [], jnp.int32(0)
    for k in range(DOCS):
        begins.append(total)
        total = total + len_ref[0, k]
    return begins


def clear(begins, low, size):
    found = jnp.bool_(False)
    for begin in begins:
        found = jnp.logical_or(found, jnp.logical_and(begin >= low, begin < low + size))
    return jnp.where(found, 0.0, 1.0).astype(f32)


def doc_ids(begins, positions):
    ids = jnp.zeros(positions.shape, i32)
    for begin in begins:
        ids = ids + (positions >= begin).astype(i32)
    return ids


def started(begins, end):
    count = jnp.int32(0)
    for begin in begins:
        count = count + (begin < end).astype(i32)
    return count


def positions(dim):
    return lax.broadcasted_iota(i32, (BLK, BLK), dim) + lax.axis_index("ctx") * BLK


def before_mask(begins):
    return doc_ids(begins, positions(0)) == started(begins, lax.axis_index("ctx") * BLK)


def after_mask(begins):
    return doc_ids(begins, positions(0)) == started(begins, (lax.axis_index("ctx") + 1) * BLK)


def pair_mask(begins):
    row, col = positions(0), positions(1)
    mask = jnp.logical_and(row >= col, doc_ids(begins, row) == doc_ids(begins, col))
    return jnp.concatenate([mask, mask], axis=0)


def left_lanes(rows):
    return lax.broadcasted_iota(i32, (rows, PAIR), 1) < E


def pick(cond, a):
    return jnp.where(cond, a, jnp.zeros_like(a))


def heads(a):
    left = left_lanes(a.shape[0])
    return jnp.concatenate([pick(left, a), pick(jnp.logical_not(left), a)], axis=0)


def fold(full):
    return jnp.where(left_lanes(E), full[:E], full[E:])


def beside(a):
    return jnp.concatenate([a[:BLK], a[BLK:]], axis=1)


def split(a):
    high = a.astype(bf16)
    return high, (a - high.astype(f32)).astype(bf16)


def local_pairs(r):
    for o in range(GROUP):
        for i in range(SHARE):
            pair = (r ^ o) * SHARE + i
            yield o, slice(i * E, (i + 1) * E), pair, pl.ds(pl.multiple_of(pair * PAIR, PAIR), PAIR)


def own_state_kernel(len_ref, k_ref, v_ref, *state_refs):
    r, _ = place()
    after = after_mask(bounds(len_ref))
    for o, rows, _, lanes in local_pairs(r):
        k = pick(after, k_ref[0, :, lanes])
        state_refs[o][rows, :] = fold(dot_tn(k, v_ref[0, :, lanes])).astype(bf16)


def block_keeps(begins, group):
    return [clear(begins, (group * GROUP + b) * BLK, BLK) for b in range(GROUP)]


def order(back):
    return range(GROUP - 1, -1, -1) if back else range(GROUP)


def joined(tile):
    return tile[:PAIRS].astype(f32) + tile[PAIRS:].astype(f32)


def total_kernel(back):
    def kernel(len_ref, *refs):
        r, group = place()
        states = refs[:GROUP]
        if back:
            part_ref, out_ref, gain_ref, scratch = refs[GROUP:]
        else:
            out_ref, scratch = refs[GROUP:]
        keep = block_keeps(bounds(len_ref), group)
        for o, ref in enumerate(states):
            scratch[r ^ o] = ref[:ROWS]
        total = scratch[order(back)[0]].astype(f32)
        for b in order(back)[1:]:
            total = scratch[b].astype(f32) + keep[b] * total
        out_ref[...] = total.astype(bf16)
        if back:
            high, low = split(part_ref[...])
            own = high.astype(f32) + low.astype(f32)
            g1, g2, g3 = (joined(ref[ROWS:]) for ref in states[1:])
            gain_ref[...] = (own + g1) + (g2 + g3)

    return kernel


def carry_kernel(back):
    def kernel(len_ref, *refs):
        r, group = place()
        begins = bounds(len_ref)
        states, far, outs = refs[:GROUP], refs[GROUP : GROUP + REACH], refs[GROUP + REACH : -2]
        scratch, moved = refs[-2:]
        keep = block_keeps(begins, group)
        for o, ref in enumerate(states):
            scratch[r ^ o] = ref[:ROWS]
        carry = jnp.zeros((ROWS, PAIR), f32)
        for d in range(REACH, 0, -1):
            source = group + d if back else group - d
            inside = (source < lax.axis_size("ctx") // GROUP) if back else (source >= 0)
            through = clear(begins, source * GROUP * BLK, GROUP * BLK)
            carry = through * carry + jnp.where(inside, 1.0, 0.0) * far[d - 1][...].astype(f32)
        for b in order(back):
            moved[b] = carry.astype(bf16)
            carry = scratch[b].astype(f32) + keep[b] * carry
        for o, out in enumerate(outs):
            out[...] = moved[r ^ o]

    return kernel


def inside_kernel(len_ref, q_ref, k_ref, v_ref, w_ref, att_ref):
    mask = pair_mask(bounds(len_ref))
    for p in range(PAIRS):
        lanes = slice(p * PAIR, (p + 1) * PAIR)
        q2 = heads(q_ref[0, :, lanes])
        weights = pick(mask, dot_nt(q2, k_ref[0, :, lanes])).astype(bf16)
        w_ref[p] = weights
        att_ref[:, lanes] = dot(beside(weights), heads(v_ref[0, :, lanes]))


def attend_kernel(len_ref, q_ref, g_ref, gain_ref, att_ref, *refs):
    c_refs, (out_ref, ga_ref), state_refs = refs[:GROUP], refs[GROUP : GROUP + 2], refs[GROUP + 2 : -1]
    part_ref = refs[-1]
    r, _ = place()
    before = before_mask(bounds(len_ref))
    same = (lax.broadcasted_iota(i32, (PAIR, PAIR), 0) < E) == left_lanes(PAIR)
    ones = jnp.where(same, 1.0 / E, 0.0).astype(bf16)
    ones2 = jnp.concatenate([ones, ones], axis=0)
    for o, rows, pair, lanes in local_pairs(r):
        gain = gain_ref[:, lanes]
        qb = pick(before, q_ref[0, :, lanes])
        att = att_ref[:, lanes] + dot(qb, heads(c_refs[o][rows, :]))
        dy = g_ref[0, :, lanes].astype(f32)
        d = dy * gain
        means = dot(
            jnp.concatenate(split(jnp.concatenate([att * att, d * att], axis=0)), axis=1), ones2
        )
        root = lax.rsqrt(means[:BLK] + eps)
        normed = att * root
        out_ref[0, :, lanes] = (gain * normed).astype(bf16)
        ga = ((d - normed * (means[BLK:] * root)) * root).astype(bf16)
        ga_ref[:, lanes] = ga
        part_ref[pl.ds(pair, 1), :] = jnp.sum(dy * normed, axis=0, keepdims=True)
        state_refs[o][rows, :] = fold(dot_tn(qb, ga)).astype(bf16)
    tile = jnp.concatenate(split(part_ref[...]), axis=0)
    for ref in state_refs[1:]:
        ref[ROWS:] = tile


def grads_kernel(len_ref, q_ref, k_ref, v_ref, w_ref, ga_ref, *refs):
    c_refs, (gq_ref, pk_ref, pv_ref) = refs[:GROUP], refs[GROUP:]
    r, _ = place()
    begins = bounds(len_ref)
    mask, before = pair_mask(begins), before_mask(begins)
    for o, rows, pair, lanes in local_pairs(r):
        ga = ga_ref[:, lanes]
        ga2 = heads(ga)
        gw = pick(mask, dot_nt(ga2, v_ref[0, :, lanes])).astype(bf16)
        gq = dot(beside(gw), heads(k_ref[0, :, lanes]))
        gq = gq + dot_nt(pick(before, ga), heads(c_refs[o][rows, :]))
        gq_ref[0, :, lanes] = gq.astype(bf16)
        pk_ref[:, lanes] = dot_tn(gw, heads(q_ref[0, :, lanes]))
        pv_ref[:, lanes] = dot_tn(w_ref[pair], ga2)


def last_kernel(len_ref, k_ref, v_ref, pk_ref, pv_ref, *refs):
    c_refs, (gk_ref, gv_ref) = refs[:GROUP], refs[GROUP:]
    r, _ = place()
    after = after_mask(bounds(len_ref))
    for o, rows, _, lanes in local_pairs(r):
        k = pick(after, k_ref[0, :, lanes])
        v = pick(after, v_ref[0, :, lanes])
        carried = heads(c_refs[o][rows, :])
        gk_ref[0, :, lanes] = (pk_ref[:, lanes] + dot_nt(v, carried)).astype(bf16)
        gv_ref[0, :, lanes] = (pv_ref[:, lanes] + dot(k, carried)).astype(bf16)


def call(kernel, outs, n_in, name, scratch=()):
    vmem = pl.BlockSpec(memory_space=pltpu.VMEM)
    smem = pl.BlockSpec(memory_space=pltpu.SMEM)
    return pl.pallas_call(
        kernel,
        out_shape=outs,
        in_specs=[smem] + [vmem] * n_in,
        out_specs=jax.tree.map(lambda _: vmem, outs),
        scratch_shapes=list(scratch),
        compiler_params=pltpu.CompilerParams(vmem_limit_bytes=48 << 20),
        name=name,
    )


def exchange(arrays):
    count = lax.axis_size("ctx")
    got = [
        lax.ppermute(arrays[o], "ctx", [(i, i ^ o) for i in range(count)])
        for o in range(GROUP - 1, 0, -1)
    ]
    return [arrays[0]] + got[::-1]


def among(terms, first, second):
    count = lax.axis_size(("dp", "ctx"))
    a, b, c = (
        lax.ppermute(terms, ("dp", "ctx"), [(i, i ^ bits) for i in range(count)])
        for bits in (first, second, first | second)
    )
    return (terms + a) + (b + c)


def chain(lengths, states, back, part=None):
    shape = jax.ShapeDtypeStruct
    share = shape((ROWS, PAIR), bf16)
    terms = shape((PAIRS, PAIR), f32)
    name = "back" if back else "ahead"
    stage = pltpu.VMEM((GROUP, ROWS, PAIR), bf16)
    count = lax.axis_size("ctx")
    states = exchange(states)
    gains = None
    if back:
        total, gains = call(total_kernel(True), (share, terms), GROUP + 1, name + "_total", [stage])(
            lengths, *states, part
        )
    else:
        total = call(total_kernel(False), share, GROUP, name + "_total", [stage])(lengths, *states)
    step = -GROUP if back else GROUP
    far = [
        lax.ppermute(total, "ctx", [(i, (i + d * step) % count) for i in range(count)])
        for d in range(REACH, 0, -1)
    ][::-1]
    if back:
        gains, *far = lax.optimization_barrier((among(gains, 32, 64), *far))
    outs = call(carry_kernel(back), (share,) * GROUP, GROUP + REACH, name + "_carry", [stage, stage])(
        lengths, *states, *far
    )
    carried = exchange(outs)
    if back:
        gains, *carried = lax.optimization_barrier((among(gains, 8, 16), *carried))
    return carried, gains


def per_device(queries, keys, values, grad_output, out_gain, doc_lengths):
    shape = jax.ShapeDtypeStruct
    full = shape(queries.shape, bf16)
    plain = shape((BLK, H * E), f32)
    share = shape((ROWS, PAIR), bf16)
    wide = shape((ROWS + TILE, PAIR), bf16)
    gain = out_gain.reshape(1, H * E)
    states = call(own_state_kernel, (share,) * GROUP, 2, "own_state")(doc_lengths, keys, values)
    weights, inside = call(
        inside_kernel, (shape((PAIRS, 2 * BLK, BLK), bf16), plain), 3, "inside"
    )(doc_lengths, queries, keys, values)
    carried, _ = chain(doc_lengths, states, False)
    output, grad_att, *states, part = call(
        attend_kernel,
        (full, shape((BLK, H * E), bf16), share, wide, wide, wide, shape((PAIRS, PAIR), f32)),
        4 + GROUP,
        "attend",
    )(doc_lengths, queries, grad_output, gain, inside, *carried)
    grad_q, part_k, part_v = call(grads_kernel, (full, plain, plain), 5 + GROUP, "grads")(
        doc_lengths, queries, keys, values, weights, grad_att, *carried
    )
    carried, gains = chain(doc_lengths, states, True, part)
    grad_k, grad_v = call(last_kernel, (full, full), 4 + GROUP, "last")(
        doc_lengths, keys, values, part_k, part_v, *carried
    )
    total_tokens = lax.axis_size("dp") * BLK * lax.axis_size("ctx")
    grad_gain = among(gains, 4, 128).reshape(H * E) / math.sqrt(total_tokens)
    return (output, grad_q, grad_k, grad_v, grad_gain)


def solution(mesh):
    spread = P("dp", "ctx", None)
    return jax.shard_map(
        per_device,
        mesh=mesh,
        in_specs=(spread, spread, spread, spread, P(), P("dp", None)),
        out_specs=(spread, spread, spread, spread, P()),
        check_vma=False,
    )
```

time: 89.4 us -> 85.7 us (0.959)
  Pallas kernels: 21.8 us -> 19.4 us
  waiting for transfers between devices: 24.3 us -> 22.3 us
    pallas_call x12 -> x8, Pallas kernels: 20.3 us -> 17.9 us  [the longest x1 6.68 us: per_device(): call(attend_kernel, (full, shape((BLK, H * E), bf16), share, wide, wide,...]
    ppermute x24 -> x27, waiting for transfers between devices: 24.3 us -> 22.3 us  [the longest x12 14.5 us: exchange(): lax.ppermute(arrays[o], 'ctx', [(i, i ^ o) for i in range(count)])]
    ppermute x24 -> x27, starting transfers between devices: 38.2 us -> 38.2 us  [the longest x9 18.7 us: among(): lax.ppermute(terms, ('dp', 'ctx'), [(i, i ^ bits) for i in range(count)])]
  transfers between devices with their start and end apart: 24 -> 27, of which waited for: 14 -> 14; matrix products, arithmetic and copies ran while one was open for 1% -> 0% of each run, Pallas kernels for 8% -> 11%
where the time goes in v3:
time: 85.7 us; the launch traced here: 84.1 us
  starting transfers between devices  38.2 us (45%)
  waiting for transfers between devices  22.3 us (26%)
  Pallas kernels  19.4 us (23%)
  local copies, waits for them, and re-layouts  2.75 us (3%)
    ppermute x9, starting transfers between devices, among(): lax.ppermute(terms, ('dp', 'ctx'), [(i, i ^ bits) for i in range(count)])  18.7 us
    ppermute x12, waiting for transfers between devices, exchange(): lax.ppermute(arrays[o], 'ctx', [(i, i ^ o) for i in range(count)])  14.5 us
    ppermute x6, starting transfers between devices, chain(): lax.ppermute(total, 'ctx', [(i, (i + d * step) % count) for i in range(co...  11 us
    ppermute x12, starting transfers between devices, exchange(): lax.ppermute(arrays[o], 'ctx', [(i, i ^ o) for i in range(count)])  8.45 us
    ppermute x6, waiting for transfers between devices, chain(): lax.ppermute(total, 'ctx', [(i, (i + d * step) % count) for i in range(co...  7.64 us
    pallas_call x1, Pallas kernels, per_device(): call(attend_kernel, (full, shape((BLK, H * E), bf16), share, wide, wide,...  6.68 us
    pallas_call x1, Pallas kernels, per_device(): call(grads_kernel, (full, plain, plain), 5 + GROUP, 'grads')  5.06 us
    unnamed x16, local copies, waits for them, and re-layouts  2.75 us
  transfers between devices with their start and end apart: 27, of which 14 were waited for; matrix products, arithmetic and copies ran while one was open for 0% of the time, Pallas kernels for 11%

profile of v3, /device:TPU:2, one launch (start us, length us, event | category | flops | bytes accessed | tf_op | source)
XLA Modules:
  0.0 84.1 jit_solution(2777229225617188903)
XLA Ops:
  4.6 2.4 %collective-permute-start.1 = (bf16[256,128]{1,0:T(8,128)(2,1)S(1)}, bf16[256,128]{1,0:T(8,128)(2,1)S(1)}, u32[]{:S(2)}, u32[]{:S(2)}) collective-permute-start(bf16[256,128]{1,0:T(8,128)(2,1)S(1)} %get-tuple-element.45), channel_id=1, source_target_pairs={{0,2},{1,3},{2,0},{3,1},{4,6},{5,7},{6,4},{7,5},{8,10},{9,11},{10,... | collective-permute-start | bytes 196616 | tf_op jit(solution)/shard_map/ppermute | solution.py:277
  7.0 2.6 %collective-permute-done.1.refs_2_ = bf16[256,128]{1,0:T(8,128)(2,1)S(1)} collective-permute-done((bf16[256,128]{1,0:T(8,128)(2,1)S(1)}, bf16[256,128]{1,0:T(8,128)(2,1)S(1)}, u32[]{:S(2)}, u32[]{:S(2)}) %collective-permute-start.1) | collective-permute-done | bytes 65568 | tf_op jit(solution)/shard_map/ppermute | solution.py:277
  9.6 1.4 %collective-permute-done.2.refs_3_ = bf16[256,128]{1,0:T(8,128)(2,1)S(1)} collective-permute-done((bf16[256,128]{1,0:T(8,128)(2,1)S(1)}, bf16[256,128]{1,0:T(8,128)(2,1)S(1)}, u32[]{:S(2)}, u32[]{:S(2)}) %collective-permute-start.2) | collective-permute-done | bytes 65568 | tf_op jit(solution)/shard_map/ppermute | solution.py:277
  11.6 2.2 %collective-permute-start.5 = (bf16[256,128]{1,0:T(8,128)(2,1)S(1)}, bf16[256,128]{1,0:T(8,128)(2,1)S(1)}, u32[]{:S(2)}, u32[]{:S(2)}) collective-permute-start(bf16[256,128]{1,0:T(8,128)(2,1)S(1)} %ahead_total.1), channel_id=1, source_target_pairs={{0,12},{1,13},{2,14},{3,15},{4,16},{5,17},{6,18},{7,19},{8,20},{9,... | collective-permute-start | bytes 196616 | tf_op jit(solution)/shard_map/ppermute | solution.py:309
  13.9 1.6 %collective-permute-start.4 = (bf16[256,128]{1,0:T(8,128)(2,1)S(1)}, bf16[256,128]{1,0:T(8,128)(2,1)S(1)}, u32[]{:S(2)}, u32[]{:S(2)}) collective-permute-start(bf16[256,128]{1,0:T(8,128)(2,1)S(1)} %ahead_total.1), channel_id=1, source_target_pairs={{0,8},{1,9},{2,10},{3,11},{4,12},{5,13},{6,14},{7,15},{8,16},{9,17... | collective-permute-start | bytes 196616 | tf_op jit(solution)/shard_map/ppermute | solution.py:309
  15.5 2.1 %collective-permute-start.3 = (bf16[256,128]{1,0:T(8,128)(2,1)S(1)}, bf16[256,128]{1,0:T(8,128)(2,1)S(1)}, u32[]{:S(2)}, u32[]{:S(2)}) collective-permute-start(bf16[256,128]{1,0:T(8,128)(2,1)S(1)} %ahead_total.1), channel_id=1, source_target_pairs={{0,4},{1,5},{2,6},{3,7},{4,8},{5,9},{6,10},{7,11},{8,12},{9,13},{1... | collective-permute-start | bytes 196616 | tf_op jit(solution)/shard_map/ppermute | solution.py:309
  17.6 2.4 %collective-permute-done.5.refs_6_ = bf16[256,128]{1,0:T(8,128)(2,1)S(1)} collective-permute-done((bf16[256,128]{1,0:T(8,128)(2,1)S(1)}, bf16[256,128]{1,0:T(8,128)(2,1)S(1)}, u32[]{:S(2)}, u32[]{:S(2)}) %collective-permute-start.5) | collective-permute-done | bytes 65568 | tf_op jit(solution)/shard_map/ppermute | solution.py:309
  20.5 2.8 %collective-permute-done.3.refs_4_ = bf16[256,128]{1,0:T(8,128)(2,1)S(1)} collective-permute-done((bf16[256,128]{1,0:T(8,128)(2,1)S(1)}, bf16[256,128]{1,0:T(8,128)(2,1)S(1)}, u32[]{:S(2)}, u32[]{:S(2)}) %collective-permute-start.3) | collective-permute-done | bytes 65568 | tf_op jit(solution)/shard_map/ppermute | solution.py:309
  24.2 1.7 %collective-permute-start.7 = (bf16[256,128]{1,0:T(8,128)(2,1)S(1)}, bf16[256,128]{1,0:T(8,128)(2,1)S(1)}, u32[]{:S(2)}, u32[]{:S(2)}) collective-permute-start(bf16[256,128]{1,0:T(8,128)(2,1)S(1)} %get-tuple-element.49), channel_id=1, source_target_pairs={{0,2},{1,3},{2,0},{3,1},{4,6},{5,7},{6,4},{7,5},{8,10},{9,11},{10,... | collective-permute-start | bytes 196616 | tf_op jit(solution)/shard_map/ppermute | solution.py:277
  26.1 1.5 %inside.1 = (bf16[16,256,128]{2,1,0:T(8,128)(2,1)S(1)}, f32[128,2048]{1,0:T(8,128)S(1)}) custom-call(s32[1,12]{1,0:T(1,128)S(1)} %copy-done.6, bf16[1,128,2048]{2,1,0:T(8,128)(2,1)S(1)} %copy-done.4, bf16[1,128,2048]{2,1,0:T(8,128)(2,1)S(1)} %copy-done.1, bf16[1,128,2048]{2,1,0:T(8,128)(2,1)S(1)} %copy-done.3), custom_call_target="tpu_custom_call" | custom-call | tf_op jit(solution)/shard_map/inside/pallas_call | solution.py:331
  30.0 6.7 %attend.1 = (bf16[1,128,2048]{2,1,0:T(8,128)(2,1)}, bf16[128,2048]{1,0:T(8,128)(2,1)S(1)}, bf16[256,128]{1,0:T(8,128)(2,1)S(1)}, bf16[288,128]{1,0:T(8,128)(2,1)...) custom-call(s32[1,12]{1,0:T(1,128)S(1)} %copy-done.6, ...), custom_call_target="tpu_custom_call" | custom-call | tf_op jit(solution)/shard_map/attend/pallas_call | solution.py:335
  36.8 1.4 %collective-permute-start.10 = (bf16[288,128]{1,0:T(8,128)(2,1)S(1)}, bf16[288,128]{1,0:T(8,128)(2,1)S(1)}, u32[]{:S(2)}, u32[]{:S(2)}) collective-permute-start(bf16[288,128]{1,0:T(8,128)(2,1)S(1)} %get-tuple-element.59), channel_id=1, source_target_pairs={{0,2},{1,3},{2,0},{3,1},{4,6},{5,7},{6,4},{7,5},{8,10},{9,11},{10,... | collective-permute-start | bytes 221192 | tf_op jit(solution)/shard_map/ppermute | solution.py:277
  38.5 2.9 %collective-permute-done.10.refs_2_ = bf16[288,128]{1,0:T(8,128)(2,1)S(1)} collective-permute-done((bf16[288,128]{1,0:T(8,128)(2,1)S(1)}, bf16[288,128]{1,0:T(8,128)(2,1)S(1)}, u32[]{:S(2)}, u32[]{:S(2)}) %collective-permute-start.10) | collective-permute-done | bytes 73760 | tf_op jit(solution)/shard_map/ppermute | solution.py:277
  41.5 1.3 %collective-permute-done.11.refs_3_ = bf16[288,128]{1,0:T(8,128)(2,1)S(1)} collective-permute-done((bf16[288,128]{1,0:T(8,128)(2,1)S(1)}, bf16[288,128]{1,0:T(8,128)(2,1)S(1)}, u32[]{:S(2)}, u32[]{:S(2)}) %collective-permute-start.11) | collective-permute-done | bytes 73760 | tf_op jit(solution)/shard_map/ppermute | solution.py:277
  43.5 4.7 %collective-permute-start.14 = (f32[16,128]{1,0:T(8,128)S(1)}, f32[16,128]{1,0:T(8,128)S(1)}, u32[]{:S(2)}, u32[]{:S(2)}) collective-permute-start(f32[16,128]{1,0:T(8,128)S(1)} %get-tuple-element.62), channel_id=1, source_target_pairs={{0,96},{1,97},{2,98},{3,99},{4,100},{5,101},{6,102},{7,103},{8,104... | collective-permute-start | bytes 24584 | tf_op jit(solution)/shard_map/ppermute | solution.py:286
  50.0 3.9 %collective-permute-start.15 = (bf16[256,128]{1,0:T(8,128)(2,1)S(1)}, bf16[256,128]{1,0:T(8,128)(2,1)S(1)}, u32[]{:S(2)}, u32[]{:S(2)}) collective-permute-start(bf16[256,128]{1,0:T(8,128)(2,1)S(1)} %get-tuple-element.63), channel_id=1, source_target_pairs={{0,28},{1,29},{2,30},{3,31},{4,0},{5,1},{6,2},{7,3},{8,4},{9,5},{1... | collective-permute-start | bytes 196616 | tf_op jit(solution)/shard_map/ppermute | solution.py:309
  54.0 1.6 %collective-permute-done.17.refs_6_ = bf16[256,128]{1,0:T(8,128)(2,1)S(1)} collective-permute-done((bf16[256,128]{1,0:T(8,128)(2,1)S(1)}, bf16[256,128]{1,0:T(8,128)(2,1)S(1)}, u32[]{:S(2)}, u32[]{:S(2)}) %collective-permute-start.17) | collective-permute-done | bytes 65568 | tf_op jit(solution)/shard_map/ppermute | solution.py:309
  55.8 1.9 %collective-permute-start.20 = (f32[16,128]{1,0:T(8,128)S(1)}, f32[16,128]{1,0:T(8,128)S(1)}, u32[]{:S(2)}, u32[]{:S(2)}) collective-permute-start(f32[16,128]{1,0:T(8,128)S(1)} %add_add_fusion.1), channel_id=1, source_target_pairs={{0,24},{1,25},{2,26},{3,27},{4,28},{5,29},{6,30},{7,31},{8,16},{9,... | collective-permute-start | bytes 24584 | tf_op jit(solution)/shard_map/ppermute | solution.py:286
  60.8 2.0 %collective-permute-start.22 = (bf16[256,128]{1,0:T(8,128)(2,1)S(1)}, bf16[256,128]{1,0:T(8,128)(2,1)S(1)}, u32[]{:S(2)}, u32[]{:S(2)}) collective-permute-start(bf16[256,128]{1,0:T(8,128)(2,1)S(1)} %get-tuple-element.70), channel_id=1, source_target_pairs={{0,2},{1,3},{2,0},{3,1},{4,6},{5,7},{6,4},{7,5},{8,10},{9,11},{10,... | collective-permute-start | bytes 196616 | tf_op jit(solution)/shard_map/ppermute | solution.py:277
  63.0 2.5 %collective-permute-done.22.refs_2_ = bf16[256,128]{1,0:T(8,128)(2,1)S(1)} collective-permute-done((bf16[256,128]{1,0:T(8,128)(2,1)S(1)}, bf16[256,128]{1,0:T(8,128)(2,1)S(1)}, u32[]{:S(2)}, u32[]{:S(2)}) %collective-permute-start.22) | collective-permute-done | bytes 65568 | tf_op jit(solution)/shard_map/ppermute | solution.py:277
  65.5 1.4 %collective-permute-done.23.refs_3_ = bf16[256,128]{1,0:T(8,128)(2,1)S(1)} collective-permute-done((bf16[256,128]{1,0:T(8,128)(2,1)S(1)}, bf16[256,128]{1,0:T(8,128)(2,1)S(1)}, u32[]{:S(2)}, u32[]{:S(2)}) %collective-permute-start.23) | collective-permute-done | bytes 65568 | tf_op jit(solution)/shard_map/ppermute | solution.py:277
  66.9 8.6 %collective-permute-start.26 = (f32[16,128]{1,0:T(8,128)S(1)}, f32[16,128]{1,0:T(8,128)S(1)}, u32[]{:S(2)}, u32[]{:S(2)}) collective-permute-start(f32[16,128]{1,0:T(8,128)S(1)} %add_add_fusion), channel_id=1, source_target_pairs={{0,132},{1,133},{2,134},{3,135},{4,128},{5,129},{6,130},{7,131},{8... | collective-permute-start | bytes 24584 | tf_op jit(solution)/shard_map/ppermute | solution.py:286
  76.1 5.1 %grads.1 = (bf16[1,128,2048]{2,1,0:T(8,128)(2,1)}, f32[128,2048]{1,0:T(8,128)S(1)}, f32[128,2048]{1,0:T(8,128)S(1)}) custom-call(s32[1,12]{1,0:T(1,128)S(1)} %copy-done.6, bf16[1,128,2048]{2,1,0:T(8,128)(2,1)S(1)} %copy-done.4, bf16[1,128,2048]{2,1,0:T(8,128)(2,1)S(1)} %copy-done.1, bf16[1,128,2048]{2,1,0:T(8,128)(2,1)S(1)} %copy-done.3, ...), custom_call_target="tpu_custom_call" | custom-call | tf_op jit(solution)/shard_map/grads/pallas_call | solution.py:341
  81.2 2.2 %last.1 = (bf16[1,128,2048]{2,1,0:T(8,128)(2,1)}, bf16[1,128,2048]{2,1,0:T(8,128)(2,1)}) custom-call(s32[1,12]{1,0:T(1,128)S(1)} %copy-done.6, bf16[1,128,2048]{2,1,0:T(8,128)(2,1)S(1)} %copy-done.1, bf16[1,128,2048]{2,1,0:T(8,128)(2,1)S(1)} %copy-done.3, f32[128,2048]{1,0:T(8,128)S(1)} %get-tuple-element.55.pk_ref, ...), custom_call_target="tpu_custom_call" | custom-call | tf_op jit(solution)/shard_map/last/pallas_call | solution.py:345
  (58 shorter events, 16.2 us)
Async XLA Ops:
  4.6 5.0 %collective-permute-start.1 = (bf16[256,128]{1,0:T(8,128)(2,1)S(1)}, bf16[256,128]{1,0:T(8,128)(2,1)S(1)}, u32[]{:S(2)}, u32[]{:S(2)}) collective-permute-start(bf16[256,128]{1,0:T(8,128)(2,1)S(1)} %get-tuple-element.45), channel_id=1, source_target_pairs={{0,2},{1,3},{2,0},{3,1},{4,6},{5,7},{6,4},{7,5},{8,10},{9,11},{10,... | collective-permute-start | bytes 196616 | tf_op jit(solution)/shard_map/ppermute | solution.py:277
  6.9 4.1 %collective-permute-start.2 = (bf16[256,128]{1,0:T(8,128)(2,1)S(1)}, bf16[256,128]{1,0:T(8,128)(2,1)S(1)}, u32[]{:S(2)}, u32[]{:S(2)}) collective-permute-start(bf16[256,128]{1,0:T(8,128)(2,1)S(1)} %get-tuple-element.46), channel_id=1, source_target_pairs={{0,3},{1,2},{2,1},{3,0},{4,7},{5,6},{6,5},{7,4},{8,11},{9,10},{10,... | collective-permute-start | bytes 196616 | tf_op jit(solution)/shard_map/ppermute | solution.py:277
  11.6 8.3 %collective-permute-start.5 = (bf16[256,128]{1,0:T(8,128)(2,1)S(1)}, bf16[256,128]{1,0:T(8,128)(2,1)S(1)}, u32[]{:S(2)}, u32[]{:S(2)}) collective-permute-start(bf16[256,128]{1,0:T(8,128)(2,1)S(1)} %ahead_total.1), channel_id=1, source_target_pairs={{0,12},{1,13},{2,14},{3,15},{4,16},{5,17},{6,18},{7,19},{8,20},{9,... | collective-permute-start | bytes 196616 | tf_op jit(solution)/shard_map/ppermute | solution.py:309
  13.9 6.6 %collective-permute-start.4 = (bf16[256,128]{1,0:T(8,128)(2,1)S(1)}, bf16[256,128]{1,0:T(8,128)(2,1)S(1)}, u32[]{:S(2)}, u32[]{:S(2)}) collective-permute-start(bf16[256,128]{1,0:T(8,128)(2,1)S(1)} %ahead_total.1), channel_id=1, source_target_pairs={{0,8},{1,9},{2,10},{3,11},{4,12},{5,13},{6,14},{7,15},{8,16},{9,17... | collective-permute-start | bytes 196616 | tf_op jit(solution)/shard_map/ppermute | solution.py:309
  15.5 7.9 %collective-permute-start.3 = (bf16[256,128]{1,0:T(8,128)(2,1)S(1)}, bf16[256,128]{1,0:T(8,128)(2,1)S(1)}, u32[]{:S(2)}, u32[]{:S(2)}) collective-permute-start(bf16[256,128]{1,0:T(8,128)(2,1)S(1)} %ahead_total.1), channel_id=1, source_target_pairs={{0,4},{1,5},{2,6},{3,7},{4,8},{5,9},{6,10},{7,11},{8,12},{9,13},{1... | collective-permute-start | bytes 196616 | tf_op jit(solution)/shard_map/ppermute | solution.py:309
  24.1 3.5 %collective-permute-start.6 = (bf16[256,128]{1,0:T(8,128)(2,1)S(1)}, bf16[256,128]{1,0:T(8,128)(2,1)S(1)}, u32[]{:S(2)}, u32[]{:S(2)}) collective-permute-start(bf16[256,128]{1,0:T(8,128)(2,1)S(1)} %get-tuple-element.48), channel_id=1, source_target_pairs={{0,1},{1,0},{2,3},{3,2},{4,5},{5,4},{6,7},{7,6},{8,9},{9,8},{10,11... | collective-permute-start | bytes 196616 | tf_op jit(solution)/shard_map/ppermute | solution.py:277
  24.2 4.5 %collective-permute-start.7 = (bf16[256,128]{1,0:T(8,128)(2,1)S(1)}, bf16[256,128]{1,0:T(8,128)(2,1)S(1)}, u32[]{:S(2)}, u32[]{:S(2)}) collective-permute-start(bf16[256,128]{1,0:T(8,128)(2,1)S(1)} %get-tuple-element.49), channel_id=1, source_target_pairs={{0,2},{1,3},{2,0},{3,1},{4,6},{5,7},{6,4},{7,5},{8,10},{9,11},{10,... | collective-permute-start | bytes 196616 | tf_op jit(solution)/shard_map/ppermute | solution.py:277
  25.9 4.1 %collective-permute-start.8 = (bf16[256,128]{1,0:T(8,128)(2,1)S(1)}, bf16[256,128]{1,0:T(8,128)(2,1)S(1)}, u32[]{:S(2)}, u32[]{:S(2)}) collective-permute-start(bf16[256,128]{1,0:T(8,128)(2,1)S(1)} %get-tuple-element.50), channel_id=1, source_target_pairs={{0,3},{1,2},{2,1},{3,0},{4,7},{5,6},{6,5},{7,4},{8,11},{9,10},{10,... | collective-permute-start | bytes 196616 | tf_op jit(solution)/shard_map/ppermute | solution.py:277
  36.8 4.7 %collective-permute-start.10 = (bf16[288,128]{1,0:T(8,128)(2,1)S(1)}, bf16[288,128]{1,0:T(8,128)(2,1)S(1)}, u32[]{:S(2)}, u32[]{:S(2)}) collective-permute-start(bf16[288,128]{1,0:T(8,128)(2,1)S(1)} %get-tuple-element.59), channel_id=1, source_target_pairs={{0,2},{1,3},{2,0},{3,1},{4,6},{5,7},{6,4},{7,5},{8,10},{9,11},{10,... | collective-permute-start | bytes 221192 | tf_op jit(solution)/shard_map/ppermute | solution.py:277
  38.2 4.5 %collective-permute-start.11 = (bf16[288,128]{1,0:T(8,128)(2,1)S(1)}, bf16[288,128]{1,0:T(8,128)(2,1)S(1)}, u32[]{:S(2)}, u32[]{:S(2)}) collective-permute-start(bf16[288,128]{1,0:T(8,128)(2,1)S(1)} %get-tuple-element.60), channel_id=1, source_target_pairs={{0,3},{1,2},{2,1},{3,0},{4,7},{5,6},{6,5},{7,4},{8,11},{9,10},{10,... | collective-permute-start | bytes 221192 | tf_op jit(solution)/shard_map/ppermute | solution.py:277
  43.5 6.6 %collective-permute-start.14 = (f32[16,128]{1,0:T(8,128)S(1)}, f32[16,128]{1,0:T(8,128)S(1)}, u32[]{:S(2)}, u32[]{:S(2)}) collective-permute-start(f32[16,128]{1,0:T(8,128)S(1)} %get-tuple-element.62), channel_id=1, source_target_pairs={{0,96},{1,97},{2,98},{3,99},{4,100},{5,101},{6,102},{7,103},{8,104... | collective-permute-start | bytes 24584 | tf_op jit(solution)/shard_map/ppermute | solution.py:286
  48.2 5.8 %collective-permute-start.13 = (f32[16,128]{1,0:T(8,128)S(1)}, f32[16,128]{1,0:T(8,128)S(1)}, u32[]{:S(2)}, u32[]{:S(2)}) collective-permute-start(f32[16,128]{1,0:T(8,128)S(1)} %get-tuple-element.62), channel_id=1, source_target_pairs={{0,64},{1,65},{2,66},{3,67},{4,68},{5,69},{6,70},{7,71},{8,72},{9,... | collective-permute-start | bytes 24584 | tf_op jit(solution)/shard_map/ppermute | solution.py:286
  48.2 5.8 %collective-permute-start.12 = (f32[16,128]{1,0:T(8,128)S(1)}, f32[16,128]{1,0:T(8,128)S(1)}, u32[]{:S(2)}, u32[]{:S(2)}) collective-permute-start(f32[16,128]{1,0:T(8,128)S(1)} %get-tuple-element.62), channel_id=1, source_target_pairs={{0,32},{1,33},{2,34},{3,35},{4,36},{5,37},{6,38},{7,39},{8,40},{9,... | collective-permute-start | bytes 24584 | tf_op jit(solution)/shard_map/ppermute | solution.py:286
  48.8 6.8 %collective-permute-start.17 = (bf16[256,128]{1,0:T(8,128)(2,1)S(1)}, bf16[256,128]{1,0:T(8,128)(2,1)S(1)}, u32[]{:S(2)}, u32[]{:S(2)}) collective-permute-start(bf16[256,128]{1,0:T(8,128)(2,1)S(1)} %get-tuple-element.63), channel_id=1, source_target_pairs={{0,20},{1,21},{2,22},{3,23},{4,24},{5,25},{6,26},{7,27},{8,28},{9,... | collective-permute-start | bytes 196616 | tf_op jit(solution)/shard_map/ppermute | solution.py:309
  49.2 6.4 %collective-permute-start.16 = (bf16[256,128]{1,0:T(8,128)(2,1)S(1)}, bf16[256,128]{1,0:T(8,128)(2,1)S(1)}, u32[]{:S(2)}, u32[]{:S(2)}) collective-permute-start(bf16[256,128]{1,0:T(8,128)(2,1)S(1)} %get-tuple-element.63), channel_id=1, source_target_pairs={{0,24},{1,25},{2,26},{3,27},{4,28},{5,29},{6,30},{7,31},{8,0},{9,1... | collective-permute-start | bytes 196616 | tf_op jit(solution)/shard_map/ppermute | solution.py:309
  50.0 5.8 %collective-permute-start.15 = (bf16[256,128]{1,0:T(8,128)(2,1)S(1)}, bf16[256,128]{1,0:T(8,128)(2,1)S(1)}, u32[]{:S(2)}, u32[]{:S(2)}) collective-permute-start(bf16[256,128]{1,0:T(8,128)(2,1)S(1)} %get-tuple-element.63), channel_id=1, source_target_pairs={{0,28},{1,29},{2,30},{3,31},{4,0},{5,1},{6,2},{7,3},{8,4},{9,5},{1... | collective-permute-start | bytes 196616 | tf_op jit(solution)/shard_map/ppermute | solution.py:309
  55.8 7.0 %collective-permute-start.20 = (f32[16,128]{1,0:T(8,128)S(1)}, f32[16,128]{1,0:T(8,128)S(1)}, u32[]{:S(2)}, u32[]{:S(2)}) collective-permute-start(f32[16,128]{1,0:T(8,128)S(1)} %add_add_fusion.1), channel_id=1, source_target_pairs={{0,24},{1,25},{2,26},{3,27},{4,28},{5,29},{6,30},{7,31},{8,16},{9,... | collective-permute-start | bytes 24584 | tf_op jit(solution)/shard_map/ppermute | solution.py:286
  57.8 5.2 %collective-permute-start.19 = (f32[16,128]{1,0:T(8,128)S(1)}, f32[16,128]{1,0:T(8,128)S(1)}, u32[]{:S(2)}, u32[]{:S(2)}) collective-permute-start(f32[16,128]{1,0:T(8,128)S(1)} %add_add_fusion.1), channel_id=1, source_target_pairs={{0,16},{1,17},{2,18},{3,19},{4,20},{5,21},{6,22},{7,23},{8,24},{9,... | collective-permute-start | bytes 24584 | tf_op jit(solution)/shard_map/ppermute | solution.py:286
  59.1 3.9 %collective-permute-start.18 = (f32[16,128]{1,0:T(8,128)S(1)}, f32[16,128]{1,0:T(8,128)S(1)}, u32[]{:S(2)}, u32[]{:S(2)}) collective-permute-start(f32[16,128]{1,0:T(8,128)S(1)} %add_add_fusion.1), channel_id=1, source_target_pairs={{0,8},{1,9},{2,10},{3,11},{4,12},{5,13},{6,14},{7,15},{8,0},{9,1},... | collective-permute-start | bytes 24584 | tf_op jit(solution)/shard_map/ppermute | solution.py:286
  60.8 4.7 %collective-permute-start.22 = (bf16[256,128]{1,0:T(8,128)(2,1)S(1)}, bf16[256,128]{1,0:T(8,128)(2,1)S(1)}, u32[]{:S(2)}, u32[]{:S(2)}) collective-permute-start(bf16[256,128]{1,0:T(8,128)(2,1)S(1)} %get-tuple-element.70), channel_id=1, source_target_pairs={{0,2},{1,3},{2,0},{3,1},{4,6},{5,7},{6,4},{7,5},{8,10},{9,11},{10,... | collective-permute-start | bytes 196616 | tf_op jit(solution)/shard_map/ppermute | solution.py:277
  62.8 4.1 %collective-permute-start.23 = (bf16[256,128]{1,0:T(8,128)(2,1)S(1)}, bf16[256,128]{1,0:T(8,128)(2,1)S(1)}, u32[]{:S(2)}, u32[]{:S(2)}) collective-permute-start(bf16[256,128]{1,0:T(8,128)(2,1)S(1)} %get-tuple-element.71), channel_id=1, source_target_pairs={{0,3},{1,2},{2,1},{3,0},{4,7},{5,6},{6,5},{7,4},{8,11},{9,10},{10,... | collective-permute-start | bytes 196616 | tf_op jit(solution)/shard_map/ppermute | solution.py:277
  66.9 16.6 %collective-permute-start.26 = (f32[16,128]{1,0:T(8,128)S(1)}, f32[16,128]{1,0:T(8,128)S(1)}, u32[]{:S(2)}, u32[]{:S(2)}) collective-permute-start(f32[16,128]{1,0:T(8,128)S(1)} %add_add_fusion), channel_id=1, source_target_pairs={{0,132},{1,133},{2,134},{3,135},{4,128},{5,129},{6,130},{7,131},{8... | collective-permute-start | bytes 24584 | tf_op jit(solution)/shard_map/ppermute | solution.py:286
  75.5 7.9 %collective-permute-start.25 = (f32[16,128]{1,0:T(8,128)S(1)}, f32[16,128]{1,0:T(8,128)S(1)}, u32[]{:S(2)}, u32[]{:S(2)}) collective-permute-start(f32[16,128]{1,0:T(8,128)S(1)} %add_add_fusion), channel_id=1, source_target_pairs={{0,128},{1,129},{2,130},{3,131},{4,132},{5,133},{6,134},{7,135},{8... | collective-permute-start | bytes 24584 | tf_op jit(solution)/shard_map/ppermute | solution.py:286
  75.5 7.9 %collective-permute-start.24 = (f32[16,128]{1,0:T(8,128)S(1)}, f32[16,128]{1,0:T(8,128)S(1)}, u32[]{:S(2)}, u32[]{:S(2)}) collective-permute-start(f32[16,128]{1,0:T(8,128)S(1)} %add_add_fusion), channel_id=1, source_target_pairs={{0,4},{1,5},{2,6},{3,7},{4,0},{5,1},{6,2},{7,3},{8,12},{9,13},{10,... | collective-permute-start | bytes 24584 | tf_op jit(solution)/shard_map/ppermute | solution.py:286
  (11 other events, 84.4 us)

commit v4 on v3

--- a/solution.py
+++ b/solution.py
@@ -147,7 +147,7 @@
         r, group = place()
         states = refs[:GROUP]
         if back:
-            part_ref, out_ref, gain_ref, scratch = refs[GROUP:]
+            part_ref, out_ref, scratch = refs[GROUP:]
         else:
             out_ref, scratch = refs[GROUP:]
         keep = block_keeps(bounds(len_ref), group)
@@ -156,12 +156,12 @@
         total = scratch[order(back)[0]].astype(f32)
         for b in order(back)[1:]:
             total = scratch[b].astype(f32) + keep[b] * total
-        out_ref[...] = total.astype(bf16)
+        out_ref[:ROWS] = total.astype(bf16)
         if back:
             high, low = split(part_ref[...])
             own = high.astype(f32) + low.astype(f32)
             g1, g2, g3 = (joined(ref[ROWS:]) for ref in states[1:])
-            gain_ref[...] = (own + g1) + (g2 + g3)
+            out_ref[ROWS:] = jnp.concatenate(split((own + g1) + (g2 + g3)), axis=0)
 
     return kernel
 
@@ -170,8 +170,13 @@
     def kernel(len_ref, *refs):
         r, group = place()
         begins = bounds(len_ref)
-        states, far, outs = refs[:GROUP], refs[GROUP : GROUP + REACH], refs[GROUP + REACH : -2]
-        scratch, moved = refs[-2:]
+        states, far, refs = refs[:GROUP], refs[GROUP : GROUP + REACH], refs[GROUP + REACH :]
+        if back:
+            own_ref, *outs, terms_ref, scratch, moved = refs
+            for d, ref in enumerate((own_ref, *far)):
+                terms_ref[d * PAIRS : (d + 1) * PAIRS] = joined(ref[ROWS:])
+        else:
+            *outs, scratch, moved = refs
         keep = block_keeps(begins, group)
         for o, ref in enumerate(states):
             scratch[r ^ o] = ref[:ROWS]
@@ -180,7 +185,7 @@
             source = group + d if back else group - d
             inside = (source < lax.axis_size("ctx") // GROUP) if back else (source >= 0)
             through = clear(begins, source * GROUP * BLK, GROUP * BLK)
-            carry = through * carry + jnp.where(inside, 1.0, 0.0) * far[d - 1][...].astype(f32)
+            carry = through * carry + jnp.where(inside, 1.0, 0.0) * far[d - 1][:ROWS].astype(f32)
         for b in order(back):
             moved[b] = carry.astype(bf16)
             carry = scratch[b].astype(f32) + keep[b] * carry
@@ -188,6 +193,18 @@
             out[...] = moved[r ^ o]
 
     return kernel
+
+
+def gather_kernel(_, mine_ref, theirs_ref, out_ref, scratch):
+    _, group = place()
+    groups = scratch.shape[0]
+    for d in range(groups):
+        ref = mine_ref if d < GROUP else theirs_ref
+        scratch[(group + d) % groups] = ref[d % GROUP * PAIRS : (d % GROUP + 1) * PAIRS]
+    total = scratch[0]
+    for g in range(1, groups):
+        total = total + scratch[g]
+    out_ref[...] = total
 
 
 def inside_kernel(len_ref, q_ref, k_ref, v_ref, w_ref, att_ref):
@@ -280,44 +297,48 @@
     return [arrays[0]] + got[::-1]
 
 
-def among(terms, first, second):
-    count = lax.axis_size(("dp", "ctx"))
-    a, b, c = (
-        lax.ppermute(terms, ("dp", "ctx"), [(i, i ^ bits) for i in range(count)])
-        for bits in (first, second, first | second)
-    )
-    return (terms + a) + (b + c)
-
-
-def chain(lengths, states, back, part=None):
+def chain(lengths, states, back, part=None, beside=()):
     shape = jax.ShapeDtypeStruct
-    share = shape((ROWS, PAIR), bf16)
-    terms = shape((PAIRS, PAIR), f32)
+    share, wide = shape((ROWS, PAIR), bf16), shape((ROWS + TILE, PAIR), bf16)
+    terms, four = shape((PAIRS, PAIR), f32), shape((GROUP * PAIRS, PAIR), f32)
     name = "back" if back else "ahead"
     stage = pltpu.VMEM((GROUP, ROWS, PAIR), bf16)
     count = lax.axis_size("ctx")
     states = exchange(states)
-    gains = None
-    if back:
-        total, gains = call(total_kernel(True), (share, terms), GROUP + 1, name + "_total", [stage])(
-            lengths, *states, part
-        )
-    else:
-        total = call(total_kernel(False), share, GROUP, name + "_total", [stage])(lengths, *states)
+    extra = (part,) if back else ()
+    total = call(
+        total_kernel(back), wide if back else share, GROUP + len(extra), name + "_total", [stage]
+    )(lengths, *states, *extra)
     step = -GROUP if back else GROUP
     far = [
         lax.ppermute(total, "ctx", [(i, (i + d * step) % count) for i in range(count)])
         for d in range(REACH, 0, -1)
     ][::-1]
-    if back:
-        gains, *far = lax.optimization_barrier((among(gains, 32, 64), *far))
-    outs = call(carry_kernel(back), (share,) * GROUP, GROUP + REACH, name + "_carry", [stage, stage])(
-        lengths, *states, *far
-    )
-    carried = exchange(outs)
-    if back:
-        gains, *carried = lax.optimization_barrier((among(gains, 8, 16), *carried))
-    return carried, gains
+    if not back:
+        outs = call(carry_kernel(False), (share,) * GROUP, GROUP + REACH, name + "_carry", [stage] * 2)(
+            lengths, *states, *far
+        )
+        return exchange(outs), None, beside
+    far, beside = lax.optimization_barrier((far, beside))
+    *outs, mine = call(
+        carry_kernel(True), (share,) * GROUP + (four,), GROUP + REACH + 1, name + "_carry", [stage] * 2
+    )(lengths, *states, *far, total)
+    theirs = lax.ppermute(mine, "ctx", [(i, (i + count // 2) % count) for i in range(count)])
+    gains = call(
+        gather_kernel, terms, 2, "gather", [pltpu.VMEM((count // GROUP, PAIRS, PAIR), f32)]
+    )(lengths, mine, theirs)
+    outs = exchange(outs)
+    gains, *outs = lax.optimization_barrier((gains, *outs))
+    return outs, gains, beside
+
+
+def over_dp(gains):
+    count = lax.axis_size("dp")
+    step = 1
+    while step < count:
+        gains = gains + lax.ppermute(gains, "dp", [(i, i ^ step) for i in range(count)])
+        step *= 2
+    return gains
 
 
 def per_device(queries, keys, values, grad_output, out_gain, doc_lengths):
@@ -331,22 +352,23 @@
     weights, inside = call(
         inside_kernel, (shape((PAIRS, 2 * BLK, BLK), bf16), plain), 3, "inside"
     )(doc_lengths, queries, keys, values)
-    carried, _ = chain(doc_lengths, states, False)
+    carried, _, _ = chain(doc_lengths, states, False)
     output, grad_att, *states, part = call(
         attend_kernel,
         (full, shape((BLK, H * E), bf16), share, wide, wide, wide, shape((PAIRS, PAIR), f32)),
         4 + GROUP,
         "attend",
     )(doc_lengths, queries, grad_output, gain, inside, *carried)
-    grad_q, part_k, part_v = call(grads_kernel, (full, plain, plain), 5 + GROUP, "grads")(
+    parts = call(grads_kernel, (full, plain, plain), 5 + GROUP, "grads")(
         doc_lengths, queries, keys, values, weights, grad_att, *carried
     )
-    carried, gains = chain(doc_lengths, states, True, part)
+    carried, gains, parts = chain(doc_lengths, states, True, part, parts)
+    grad_q, part_k, part_v = parts
     grad_k, grad_v = call(last_kernel, (full, full), 4 + GROUP, "last")(
         doc_lengths, keys, values, part_k, part_v, *carried
     )
     total_tokens = lax.axis_size("dp") * BLK * lax.axis_size("ctx")
-    grad_gain = among(gains, 4, 128).reshape(H * E) / math.sqrt(total_tokens)
+    grad_gain = over_dp(gains).reshape(H * E) / math.sqrt(total_tokens)
     return (output, grad_q, grad_k, grad_v, grad_gain)
 
 

time: 85.7 us -> 81.5 us (0.951); the launches traced: 84.1 us -> 81.3 us
  starting transfers between devices: 38.2 us -> 34.9 us
    ppermute x9 -> x4, waiting for transfers between devices: 0.12 us -> 7.24 us  [the longest x1 3.87 us: chain(): lax.ppermute(mine, 'ctx', [(i, (i + count // 2) % count) for i in range(c...]
    ppermute x9 -> x4, starting transfers between devices: 18.7 us -> 13.7 us  [the longest x3 12.1 us: over_dp(): lax.ppermute(gains, 'dp', [(i, i ^ step) for i in range(count)])]
    ppermute x12, waiting for transfers between devices: 14.5 us -> 10 us  [exchange(): lax.ppermute(arrays[o], 'ctx', [(i, i ^ o) for i in range(count)])]
    ppermute x6, waiting for transfers between devices: 7.64 us -> 5.04 us  [chain(): lax.ppermute(total, 'ctx', [(i, (i + d * step) % count) for i in range(co...]
    ppermute x6, starting transfers between devices: 11 us -> 12.6 us  [chain(): lax.ppermute(total, 'ctx', [(i, (i + d * step) % count) for i in range(co...]
    pallas_call x4 -> x5, Pallas kernels: 2.85 us -> 3.45 us  [the longest x2 1.33 us: chain(): call(total_kernel(back), wide if back else share, GROUP + len(extra), nam...]
  transfers between devices with their start and end apart: 27 -> 22, of which waited for: 14 -> 12; matrix products, arithmetic and copies ran while one was open for 0% -> 0% of each run, Pallas kernels for 11% -> 12%
where the time goes in v4:
time: 81.5 us; the launch traced here: 81.3 us
  starting transfers between devices  34.9 us (43%)
  waiting for transfers between devices  22.3 us (27%)
  Pallas kernels  20 us (25%)
  local copies, waits for them, and re-layouts  2.75 us (3%)
    ppermute x6, starting transfers between devices, chain(): lax.ppermute(total, 'ctx', [(i, (i + d * step) % count) for i in range(co...  12.6 us
    ppermute x3, starting transfers between devices, over_dp(): lax.ppermute(gains, 'dp', [(i, i ^ step) for i in range(count)])  12.1 us
    ppermute x12, waiting for transfers between devices, exchange(): lax.ppermute(arrays[o], 'ctx', [(i, i ^ o) for i in range(count)])  10 us
    ppermute x12, starting transfers between devices, exchange(): lax.ppermute(arrays[o], 'ctx', [(i, i ^ o) for i in range(count)])  8.56 us
    pallas_call x1, Pallas kernels, per_device(): call(attend_kernel, (full, shape((BLK, H * E), bf16), share, wide, wide,...  6.68 us
    pallas_call x1, Pallas kernels, per_device(): call(grads_kernel, (full, plain, plain), 5 + GROUP, 'grads')  5.06 us
    ppermute x6, waiting for transfers between devices, chain(): lax.ppermute(total, 'ctx', [(i, (i + d * step) % count) for i in range(co...  5.04 us
    ppermute x1, waiting for transfers between devices, chain(): lax.ppermute(mine, 'ctx', [(i, (i + count // 2) % count) for i in range(c...  3.87 us
  transfers between devices with their start and end apart: 22, of which 12 were waited for; matrix products, arithmetic and copies ran while one was open for 0% of the time, Pallas kernels for 12%

profile of v4, /device:TPU:2, one launch (start us, length us, event | category | flops | bytes accessed | tf_op | source)
XLA Modules:
  0.0 81.3 jit_solution(3290722241519226515)
XLA Ops:
  4.6 2.4 %collective-permute-start.1 = (bf16[256,128]{1,0:T(8,128)(2,1)S(1)}, bf16[256,128]{1,0:T(8,128)(2,1)S(1)}, u32[]{:S(2)}, u32[]{:S(2)}) collective-permute-start(bf16[256,128]{1,0:T(8,128)(2,1)S(1)} %get-tuple-element.46), channel_id=1, source_target_pairs={{0,2},{1,3},{2,0},{3,1},{4,6},{5,7},{6,4},{7,5},{8,10},{9,11},{10,... | collective-permute-start | bytes 196616 | tf_op jit(solution)/shard_map/ppermute | solution.py:294
  7.0 2.6 %collective-permute-done.1.refs_2_ = bf16[256,128]{1,0:T(8,128)(2,1)S(1)} collective-permute-done((bf16[256,128]{1,0:T(8,128)(2,1)S(1)}, bf16[256,128]{1,0:T(8,128)(2,1)S(1)}, u32[]{:S(2)}, u32[]{:S(2)}) %collective-permute-start.1) | collective-permute-done | bytes 65568 | tf_op jit(solution)/shard_map/ppermute | solution.py:294
  9.6 1.4 %collective-permute-done.2.refs_3_ = bf16[256,128]{1,0:T(8,128)(2,1)S(1)} collective-permute-done((bf16[256,128]{1,0:T(8,128)(2,1)S(1)}, bf16[256,128]{1,0:T(8,128)(2,1)S(1)}, u32[]{:S(2)}, u32[]{:S(2)}) %collective-permute-start.2) | collective-permute-done | bytes 65568 | tf_op jit(solution)/shard_map/ppermute | solution.py:294
  12.9 1.6 %collective-permute-start.4 = (bf16[256,128]{1,0:T(8,128)(2,1)S(1)}, bf16[256,128]{1,0:T(8,128)(2,1)S(1)}, u32[]{:S(2)}, u32[]{:S(2)}) collective-permute-start(bf16[256,128]{1,0:T(8,128)(2,1)S(1)} %ahead_total.1), channel_id=1, source_target_pairs={{0,8},{1,9},{2,10},{3,11},{4,12},{5,13},{6,14},{7,15},{8,16},{9,17... | collective-permute-start | bytes 196616 | tf_op jit(solution)/shard_map/ppermute | solution.py:314
  14.4 3.1 %collective-permute-start.5 = (bf16[256,128]{1,0:T(8,128)(2,1)S(1)}, bf16[256,128]{1,0:T(8,128)(2,1)S(1)}, u32[]{:S(2)}, u32[]{:S(2)}) collective-permute-start(bf16[256,128]{1,0:T(8,128)(2,1)S(1)} %ahead_total.1), channel_id=1, source_target_pairs={{0,12},{1,13},{2,14},{3,15},{4,16},{5,17},{6,18},{7,19},{8,20},{9,... | collective-permute-start | bytes 196616 | tf_op jit(solution)/shard_map/ppermute | solution.py:314
  17.6 2.1 %collective-permute-done.3.refs_4_ = bf16[256,128]{1,0:T(8,128)(2,1)S(1)} collective-permute-done((bf16[256,128]{1,0:T(8,128)(2,1)S(1)}, bf16[256,128]{1,0:T(8,128)(2,1)S(1)}, u32[]{:S(2)}, u32[]{:S(2)}) %collective-permute-start.3) | collective-permute-done | bytes 65568 | tf_op jit(solution)/shard_map/ppermute | solution.py:314
  19.8 2.9 %collective-permute-done.5.refs_6_ = bf16[256,128]{1,0:T(8,128)(2,1)S(1)} collective-permute-done((bf16[256,128]{1,0:T(8,128)(2,1)S(1)}, bf16[256,128]{1,0:T(8,128)(2,1)S(1)}, u32[]{:S(2)}, u32[]{:S(2)}) %collective-permute-start.5) | collective-permute-done | bytes 65568 | tf_op jit(solution)/shard_map/ppermute | solution.py:314
  23.5 1.7 %collective-permute-start.7 = (bf16[256,128]{1,0:T(8,128)(2,1)S(1)}, bf16[256,128]{1,0:T(8,128)(2,1)S(1)}, u32[]{:S(2)}, u32[]{:S(2)}) collective-permute-start(bf16[256,128]{1,0:T(8,128)(2,1)S(1)} %get-tuple-element.50), channel_id=1, source_target_pairs={{0,2},{1,3},{2,0},{3,1},{4,6},{5,7},{6,4},{7,5},{8,10},{9,11},{10,... | collective-permute-start | bytes 196616 | tf_op jit(solution)/shard_map/ppermute | solution.py:294
  25.4 1.5 %inside.1 = (bf16[16,256,128]{2,1,0:T(8,128)(2,1)S(1)}, f32[128,2048]{1,0:T(8,128)S(1)}) custom-call(s32[1,12]{1,0:T(1,128)S(1)} %copy-done.6, bf16[1,128,2048]{2,1,0:T(8,128)(2,1)S(1)} %copy-done.4, bf16[1,128,2048]{2,1,0:T(8,128)(2,1)S(1)} %copy-done.1, bf16[1,128,2048]{2,1,0:T(8,128)(2,1)S(1)} %copy-done.3), custom_call_target="tpu_custom_call" | custom-call | tf_op jit(solution)/shard_map/inside/pallas_call | solution.py:352
  29.3 6.7 %attend.1 = (bf16[1,128,2048]{2,1,0:T(8,128)(2,1)}, bf16[128,2048]{1,0:T(8,128)(2,1)S(1)}, bf16[256,128]{1,0:T(8,128)(2,1)S(1)}, bf16[288,128]{1,0:T(8,128)(2,1)...) custom-call(s32[1,12]{1,0:T(1,128)S(1)} %copy-done.6, ...), custom_call_target="tpu_custom_call" | custom-call | tf_op jit(solution)/shard_map/attend/pallas_call | solution.py:356
  38.1 2.3 %collective-permute-done.10.refs_2_ = bf16[288,128]{1,0:T(8,128)(2,1)S(1)} collective-permute-done((bf16[288,128]{1,0:T(8,128)(2,1)S(1)}, bf16[288,128]{1,0:T(8,128)(2,1)S(1)}, u32[]{:S(2)}, u32[]{:S(2)}) %collective-permute-start.10) | collective-permute-done | bytes 73760 | tf_op jit(solution)/shard_map/ppermute | solution.py:294
  40.4 1.3 %collective-permute-done.11.refs_3_ = bf16[288,128]{1,0:T(8,128)(2,1)S(1)} collective-permute-done((bf16[288,128]{1,0:T(8,128)(2,1)S(1)}, bf16[288,128]{1,0:T(8,128)(2,1)S(1)}, u32[]{:S(2)}, u32[]{:S(2)}) %collective-permute-start.11) | collective-permute-done | bytes 73760 | tf_op jit(solution)/shard_map/ppermute | solution.py:294
  42.4 1.4 %collective-permute-start.12 = (bf16[288,128]{1,0:T(8,128)(2,1)S(1)}, bf16[288,128]{1,0:T(8,128)(2,1)S(1)}, u32[]{:S(2)}, u32[]{:S(2)}) collective-permute-start(bf16[288,128]{1,0:T(8,128)(2,1)S(1)} %back_total.1.refs_7_), channel_id=1, source_target_pairs={{0,28},{1,29},{2,30},{3,31},{4,0},{5,1},{6,2},{7,3},{8,4},{9,5},{1... | collective-permute-start | bytes 221192 | tf_op jit(solution)/shard_map/ppermute | solution.py:314
  43.8 1.5 %collective-permute-start.13 = (bf16[288,128]{1,0:T(8,128)(2,1)S(1)}, bf16[288,128]{1,0:T(8,128)(2,1)S(1)}, u32[]{:S(2)}, u32[]{:S(2)}) collective-permute-start(bf16[288,128]{1,0:T(8,128)(2,1)S(1)} %back_total.1.refs_7_), channel_id=1, source_target_pairs={{0,24},{1,25},{2,26},{3,27},{4,28},{5,29},{6,30},{7,31},{8,0},{9,1... | collective-permute-start | bytes 221192 | tf_op jit(solution)/shard_map/ppermute | solution.py:314
  45.3 3.8 %collective-permute-start.14 = (bf16[288,128]{1,0:T(8,128)(2,1)S(1)}, bf16[288,128]{1,0:T(8,128)(2,1)S(1)}, u32[]{:S(2)}, u32[]{:S(2)}) collective-permute-start(bf16[288,128]{1,0:T(8,128)(2,1)S(1)} %back_total.1.refs_7_), channel_id=1, source_target_pairs={{0,20},{1,21},{2,22},{3,23},{4,24},{5,25},{6,26},{7,27},{8,28},{9,... | collective-permute-start | bytes 221192 | tf_op jit(solution)/shard_map/ppermute | solution.py:314
  49.1 5.1 %grads.1 = (bf16[1,128,2048]{2,1,0:T(8,128)(2,1)}, f32[128,2048]{1,0:T(8,128)S(1)}, f32[128,2048]{1,0:T(8,128)S(1)}) custom-call(s32[1,12]{1,0:T(1,128)S(1)} %copy-done.6, bf16[1,128,2048]{2,1,0:T(8,128)(2,1)S(1)} %copy-done.4, bf16[1,128,2048]{2,1,0:T(8,128)(2,1)S(1)} %copy-done.1, bf16[1,128,2048]{2,1,0:T(8,128)(2,1)S(1)} %copy-done.3, ...), custom_call_target="tpu_custom_call" | custom-call | tf_op jit(solution)/shard_map/grads/pallas_call | solution.py:362
  56.9 1.6 %collective-permute-start.15 = (f32[64,128]{1,0:T(8,128)S(1)}, f32[64,128]{1,0:T(8,128)S(1)}, u32[]{:S(2)}, u32[]{:S(2)}) collective-permute-start(f32[64,128]{1,0:T(8,128)S(1)} %get-tuple-element.69.mine_ref), channel_id=1, source_target_pairs={{0,16},{1,17},{2,18},{3,19},{4,20},{5,21},{6,22},{7,23},{8,24},{9,... | collective-permute-start | bytes 98312 | tf_op jit(solution)/shard_map/ppermute | solution.py:326
  58.5 3.9 %collective-permute-done.15.theirs_ref = f32[64,128]{1,0:T(8,128)S(1)} collective-permute-done((f32[64,128]{1,0:T(8,128)S(1)}, f32[64,128]{1,0:T(8,128)S(1)}, u32[]{:S(2)}, u32[]{:S(2)}) %collective-permute-start.15) | collective-permute-done | bytes 32800 | tf_op jit(solution)/shard_map/ppermute | solution.py:326
  63.0 2.0 %collective-permute-start.19 = (f32[16,128]{1,0:T(8,128)S(1)}, f32[16,128]{1,0:T(8,128)S(1)}, u32[]{:S(2)}, u32[]{:S(2)}) collective-permute-start(f32[16,128]{1,0:T(8,128)S(1)} %gather.1), channel_id=1, source_target_pairs={{0,32},{32,0},{64,96},{96,64},{128,160},{160,128},{192,224},{224,1... | collective-permute-start | bytes 24584 | tf_op jit(solution)/shard_map/ppermute | solution.py:339
  65.0 1.7 %collective-permute-done.19 = f32[16,128]{1,0:T(8,128)S(1)} collective-permute-done((f32[16,128]{1,0:T(8,128)S(1)}, f32[16,128]{1,0:T(8,128)S(1)}, u32[]{:S(2)}, u32[]{:S(2)}) %collective-permute-start.19) | collective-permute-done | bytes 8224 | tf_op jit(solution)/shard_map/ppermute | solution.py:339
  66.7 3.3 %collective-permute-start.20 = (f32[16,128]{1,0:T(8,128)S(1)}, f32[16,128]{1,0:T(8,128)S(1)}, u32[]{:S(2)}, u32[]{:S(2)}) collective-permute-start(f32[16,128]{1,0:T(8,128)S(1)} %add.9), channel_id=1, source_target_pairs={{0,64},{32,96},{64,0},{96,32},{128,192},{160,224},{192,128},{224,1... | collective-permute-start | bytes 24584 | tf_op jit(solution)/shard_map/ppermute | solution.py:339
  70.0 1.6 %collective-permute-done.20 = f32[16,128]{1,0:T(8,128)S(1)} collective-permute-done((f32[16,128]{1,0:T(8,128)S(1)}, f32[16,128]{1,0:T(8,128)S(1)}, u32[]{:S(2)}, u32[]{:S(2)}) %collective-permute-start.20) | collective-permute-done | bytes 8224 | tf_op jit(solution)/shard_map/ppermute | solution.py:339
  71.6 6.8 %collective-permute-start.21 = (f32[16,128]{1,0:T(8,128)S(1)}, f32[16,128]{1,0:T(8,128)S(1)}, u32[]{:S(2)}, u32[]{:S(2)}) collective-permute-start(f32[16,128]{1,0:T(8,128)S(1)} %add.10), channel_id=1, source_target_pairs={{0,128},{32,160},{64,192},{96,224},{128,0},{160,32},{192,64},{224,... | collective-permute-start | bytes 24584 | tf_op jit(solution)/shard_map/ppermute | solution.py:339
  78.5 2.2 %last.1 = (bf16[1,128,2048]{2,1,0:T(8,128)(2,1)}, bf16[1,128,2048]{2,1,0:T(8,128)(2,1)}) custom-call(s32[1,12]{1,0:T(1,128)S(1)} %copy-done.6, bf16[1,128,2048]{2,1,0:T(8,128)(2,1)S(1)} %copy-done.1, bf16[1,128,2048]{2,1,0:T(8,128)(2,1)S(1)} %copy-done.3, f32[128,2048]{1,0:T(8,128)S(1)} %get-tuple-element.64.pk_ref, ...), custom_call_target="tpu_custom_call" | custom-call | tf_op jit(solution)/shard_map/last/pallas_call | solution.py:367
  (49 shorter events, 16.1 us)
Async XLA Ops:
  3.4 22.0 %copy-start.3 = (bf16[1,128,2048]{2,1,0:T(8,128)(2,1)S(1)}, bf16[1,128,2048]{2,1,0:T(8,128)(2,1)}, u32[]{:S(2)}) copy-start(bf16[1,128,2048]{2,1,0:T(8,128)(2,1)} %v_ref.7) | copy-start | bytes 1572868
  3.4 22.0 %copy-start.4 = (bf16[1,128,2048]{2,1,0:T(8,128)(2,1)S(1)}, bf16[1,128,2048]{2,1,0:T(8,128)(2,1)}, u32[]{:S(2)}) copy-start(bf16[1,128,2048]{2,1,0:T(8,128)(2,1)} %q_ref.5) | copy-start | bytes 1572868
  4.5 2.5 %collective-permute-start = (bf16[256,128]{1,0:T(8,128)(2,1)S(1)}, bf16[256,128]{1,0:T(8,128)(2,1)S(1)}, u32[]{:S(2)}, u32[]{:S(2)}) collective-permute-start(bf16[256,128]{1,0:T(8,128)(2,1)S(1)} %get-tuple-element.45), channel_id=1, source_target_pairs={{0,1},{1,0},{2,3},{3,2},{4,5},{5,4},{6,7},{7,6},{8,9},{9,8},{10,11... | collective-permute-start | bytes 196616 | tf_op jit(solution)/shard_map/ppermute | solution.py:294
  4.6 5.0 %collective-permute-start.1 = (bf16[256,128]{1,0:T(8,128)(2,1)S(1)}, bf16[256,128]{1,0:T(8,128)(2,1)S(1)}, u32[]{:S(2)}, u32[]{:S(2)}) collective-permute-start(bf16[256,128]{1,0:T(8,128)(2,1)S(1)} %get-tuple-element.46), channel_id=1, source_target_pairs={{0,2},{1,3},{2,0},{3,1},{4,6},{5,7},{6,4},{7,5},{8,10},{9,11},{10,... | collective-permute-start | bytes 196616 | tf_op jit(solution)/shard_map/ppermute | solution.py:294
  6.9 4.1 %collective-permute-start.2 = (bf16[256,128]{1,0:T(8,128)(2,1)S(1)}, bf16[256,128]{1,0:T(8,128)(2,1)S(1)}, u32[]{:S(2)}, u32[]{:S(2)}) collective-permute-start(bf16[256,128]{1,0:T(8,128)(2,1)S(1)} %get-tuple-element.47), channel_id=1, source_target_pairs={{0,3},{1,2},{2,1},{3,0},{4,7},{5,6},{6,5},{7,4},{8,11},{9,10},{10,... | collective-permute-start | bytes 196616 | tf_op jit(solution)/shard_map/ppermute | solution.py:294
  11.6 8.0 %collective-permute-start.3 = (bf16[256,128]{1,0:T(8,128)(2,1)S(1)}, bf16[256,128]{1,0:T(8,128)(2,1)S(1)}, u32[]{:S(2)}, u32[]{:S(2)}) collective-permute-start(bf16[256,128]{1,0:T(8,128)(2,1)S(1)} %ahead_total.1), channel_id=1, source_target_pairs={{0,4},{1,5},{2,6},{3,7},{4,8},{5,9},{6,10},{7,11},{8,12},{9,13},{1... | collective-permute-start | bytes 196616 | tf_op jit(solution)/shard_map/ppermute | solution.py:314
  12.9 6.9 %collective-permute-start.4 = (bf16[256,128]{1,0:T(8,128)(2,1)S(1)}, bf16[256,128]{1,0:T(8,128)(2,1)S(1)}, u32[]{:S(2)}, u32[]{:S(2)}) collective-permute-start(bf16[256,128]{1,0:T(8,128)(2,1)S(1)} %ahead_total.1), channel_id=1, source_target_pairs={{0,8},{1,9},{2,10},{3,11},{4,12},{5,13},{6,14},{7,15},{8,16},{9,17... | collective-permute-start | bytes 196616 | tf_op jit(solution)/shard_map/ppermute | solution.py:314
  14.4 8.2 %collective-permute-start.5 = (bf16[256,128]{1,0:T(8,128)(2,1)S(1)}, bf16[256,128]{1,0:T(8,128)(2,1)S(1)}, u32[]{:S(2)}, u32[]{:S(2)}) collective-permute-start(bf16[256,128]{1,0:T(8,128)(2,1)S(1)} %ahead_total.1), channel_id=1, source_target_pairs={{0,12},{1,13},{2,14},{3,15},{4,16},{5,17},{6,18},{7,19},{8,20},{9,... | collective-permute-start | bytes 196616 | tf_op jit(solution)/shard_map/ppermute | solution.py:314
  23.4 3.5 %collective-permute-start.6 = (bf16[256,128]{1,0:T(8,128)(2,1)S(1)}, bf16[256,128]{1,0:T(8,128)(2,1)S(1)}, u32[]{:S(2)}, u32[]{:S(2)}) collective-permute-start(bf16[256,128]{1,0:T(8,128)(2,1)S(1)} %get-tuple-element.49), channel_id=1, source_target_pairs={{0,1},{1,0},{2,3},{3,2},{4,5},{5,4},{6,7},{7,6},{8,9},{9,8},{10,11... | collective-permute-start | bytes 196616 | tf_op jit(solution)/shard_map/ppermute | solution.py:294
  23.5 4.5 %collective-permute-start.7 = (bf16[256,128]{1,0:T(8,128)(2,1)S(1)}, bf16[256,128]{1,0:T(8,128)(2,1)S(1)}, u32[]{:S(2)}, u32[]{:S(2)}) collective-permute-start(bf16[256,128]{1,0:T(8,128)(2,1)S(1)} %get-tuple-element.50), channel_id=1, source_target_pairs={{0,2},{1,3},{2,0},{3,1},{4,6},{5,7},{6,4},{7,5},{8,10},{9,11},{10,... | collective-permute-start | bytes 196616 | tf_op jit(solution)/shard_map/ppermute | solution.py:294
  25.2 4.1 %collective-permute-start.8 = (bf16[256,128]{1,0:T(8,128)(2,1)S(1)}, bf16[256,128]{1,0:T(8,128)(2,1)S(1)}, u32[]{:S(2)}, u32[]{:S(2)}) collective-permute-start(bf16[256,128]{1,0:T(8,128)(2,1)S(1)} %get-tuple-element.51), channel_id=1, source_target_pairs={{0,3},{1,2},{2,1},{3,0},{4,7},{5,6},{6,5},{7,4},{8,11},{9,10},{10,... | collective-permute-start | bytes 196616 | tf_op jit(solution)/shard_map/ppermute | solution.py:294
  35.9 4.5 %collective-permute-start.10 = (bf16[288,128]{1,0:T(8,128)(2,1)S(1)}, bf16[288,128]{1,0:T(8,128)(2,1)S(1)}, u32[]{:S(2)}, u32[]{:S(2)}) collective-permute-start(bf16[288,128]{1,0:T(8,128)(2,1)S(1)} %get-tuple-element.55), channel_id=1, source_target_pairs={{0,2},{1,3},{2,0},{3,1},{4,6},{5,7},{6,4},{7,5},{8,10},{9,11},{10,... | collective-permute-start | bytes 221192 | tf_op jit(solution)/shard_map/ppermute | solution.py:294
  37.2 4.5 %collective-permute-start.11 = (bf16[288,128]{1,0:T(8,128)(2,1)S(1)}, bf16[288,128]{1,0:T(8,128)(2,1)S(1)}, u32[]{:S(2)}, u32[]{:S(2)}) collective-permute-start(bf16[288,128]{1,0:T(8,128)(2,1)S(1)} %get-tuple-element.56), channel_id=1, source_target_pairs={{0,3},{1,2},{2,1},{3,0},{4,7},{5,6},{6,5},{7,4},{8,11},{9,10},{10,... | collective-permute-start | bytes 221192 | tf_op jit(solution)/shard_map/ppermute | solution.py:294
  37.4 4.3 %collective-permute-start.9 = (bf16[288,128]{1,0:T(8,128)(2,1)S(1)}, bf16[288,128]{1,0:T(8,128)(2,1)S(1)}, u32[]{:S(2)}, u32[]{:S(2)}) collective-permute-start(bf16[288,128]{1,0:T(8,128)(2,1)S(1)} %get-tuple-element.54), channel_id=1, source_target_pairs={{0,1},{1,0},{2,3},{3,2},{4,5},{5,4},{6,7},{7,6},{8,9},{9,8},{10,11... | collective-permute-start | bytes 221192 | tf_op jit(solution)/shard_map/ppermute | solution.py:294
  42.4 11.8 %collective-permute-start.12 = (bf16[288,128]{1,0:T(8,128)(2,1)S(1)}, bf16[288,128]{1,0:T(8,128)(2,1)S(1)}, u32[]{:S(2)}, u32[]{:S(2)}) collective-permute-start(bf16[288,128]{1,0:T(8,128)(2,1)S(1)} %back_total.1.refs_7_), channel_id=1, source_target_pairs={{0,28},{1,29},{2,30},{3,31},{4,0},{5,1},{6,2},{7,3},{8,4},{9,5},{1... | collective-permute-start | bytes 221192 | tf_op jit(solution)/shard_map/ppermute | solution.py:314
  43.8 10.4 %collective-permute-start.13 = (bf16[288,128]{1,0:T(8,128)(2,1)S(1)}, bf16[288,128]{1,0:T(8,128)(2,1)S(1)}, u32[]{:S(2)}, u32[]{:S(2)}) collective-permute-start(bf16[288,128]{1,0:T(8,128)(2,1)S(1)} %back_total.1.refs_7_), channel_id=1, source_target_pairs={{0,24},{1,25},{2,26},{3,27},{4,28},{5,29},{6,30},{7,31},{8,0},{9,1... | collective-permute-start | bytes 221192 | tf_op jit(solution)/shard_map/ppermute | solution.py:314
  45.3 8.9 %collective-permute-start.14 = (bf16[288,128]{1,0:T(8,128)(2,1)S(1)}, bf16[288,128]{1,0:T(8,128)(2,1)S(1)}, u32[]{:S(2)}, u32[]{:S(2)}) collective-permute-start(bf16[288,128]{1,0:T(8,128)(2,1)S(1)} %back_total.1.refs_7_), channel_id=1, source_target_pairs={{0,20},{1,21},{2,22},{3,23},{4,24},{5,25},{6,26},{7,27},{8,28},{9,... | collective-permute-start | bytes 221192 | tf_op jit(solution)/shard_map/ppermute | solution.py:314
  55.0 8.0 %collective-permute-start.16 = (bf16[256,128]{1,0:T(8,128)(2,1)S(1)}, bf16[256,128]{1,0:T(8,128)(2,1)S(1)}, u32[]{:S(2)}, u32[]{:S(2)}) collective-permute-start(bf16[256,128]{1,0:T(8,128)(2,1)S(1)} %get-tuple-element.71), channel_id=1, source_target_pairs={{0,1},{1,0},{2,3},{3,2},{4,5},{5,4},{6,7},{7,6},{8,9},{9,8},{10,11... | collective-permute-start | bytes 196616 | tf_op jit(solution)/shard_map/ppermute | solution.py:294
  55.1 7.9 %collective-permute-start.17 = (bf16[256,128]{1,0:T(8,128)(2,1)S(1)}, bf16[256,128]{1,0:T(8,128)(2,1)S(1)}, u32[]{:S(2)}, u32[]{:S(2)}) collective-permute-start(bf16[256,128]{1,0:T(8,128)(2,1)S(1)} %get-tuple-element.72), channel_id=1, source_target_pairs={{0,2},{1,3},{2,0},{3,1},{4,6},{5,7},{6,4},{7,5},{8,10},{9,11},{10,... | collective-permute-start | bytes 196616 | tf_op jit(solution)/shard_map/ppermute | solution.py:294
  56.1 6.9 %collective-permute-start.18 = (bf16[256,128]{1,0:T(8,128)(2,1)S(1)}, bf16[256,128]{1,0:T(8,128)(2,1)S(1)}, u32[]{:S(2)}, u32[]{:S(2)}) collective-permute-start(bf16[256,128]{1,0:T(8,128)(2,1)S(1)} %get-tuple-element.73), channel_id=1, source_target_pairs={{0,3},{1,2},{2,1},{3,0},{4,7},{5,6},{6,5},{7,4},{8,11},{9,10},{10,... | collective-permute-start | bytes 196616 | tf_op jit(solution)/shard_map/ppermute | solution.py:294
  56.9 5.4 %collective-permute-start.15 = (f32[64,128]{1,0:T(8,128)S(1)}, f32[64,128]{1,0:T(8,128)S(1)}, u32[]{:S(2)}, u32[]{:S(2)}) collective-permute-start(f32[64,128]{1,0:T(8,128)S(1)} %get-tuple-element.69.mine_ref), channel_id=1, source_target_pairs={{0,16},{1,17},{2,18},{3,19},{4,20},{5,21},{6,22},{7,23},{8,24},{9,... | collective-permute-start | bytes 98312 | tf_op jit(solution)/shard_map/ppermute | solution.py:326
  63.0 3.7 %collective-permute-start.19 = (f32[16,128]{1,0:T(8,128)S(1)}, f32[16,128]{1,0:T(8,128)S(1)}, u32[]{:S(2)}, u32[]{:S(2)}) collective-permute-start(f32[16,128]{1,0:T(8,128)S(1)} %gather.1), channel_id=1, source_target_pairs={{0,32},{32,0},{64,96},{96,64},{128,160},{160,128},{192,224},{224,1... | collective-permute-start | bytes 24584 | tf_op jit(solution)/shard_map/ppermute | solution.py:339
  66.7 4.9 %collective-permute-start.20 = (f32[16,128]{1,0:T(8,128)S(1)}, f32[16,128]{1,0:T(8,128)S(1)}, u32[]{:S(2)}, u32[]{:S(2)}) collective-permute-start(f32[16,128]{1,0:T(8,128)S(1)} %add.9), channel_id=1, source_target_pairs={{0,64},{32,96},{64,0},{96,32},{128,192},{160,224},{192,128},{224,1... | collective-permute-start | bytes 24584 | tf_op jit(solution)/shard_map/ppermute | solution.py:339
  71.6 9.1 %collective-permute-start.21 = (f32[16,128]{1,0:T(8,128)S(1)}, f32[16,128]{1,0:T(8,128)S(1)}, u32[]{:S(2)}, u32[]{:S(2)}) collective-permute-start(f32[16,128]{1,0:T(8,128)S(1)} %add.10), channel_id=1, source_target_pairs={{0,128},{32,160},{64,192},{96,224},{128,0},{160,32},{192,64},{224,... | collective-permute-start | bytes 24584 | tf_op jit(solution)/shard_map/ppermute | solution.py:339
  (6 other events, 31.6 us)

commit v5 on v4

--- a/solution.py
+++ b/solution.py
@@ -17,6 +17,7 @@
 SHARE = PAIRS // GROUP
 ROWS = SHARE * E
 TILE = 2 * PAIRS
+BATCHED = 4
 REACH = 3
 
 eps = 1e-05
@@ -225,22 +226,32 @@
     same = (lax.broadcasted_iota(i32, (PAIR, PAIR), 0) < E) == left_lanes(PAIR)
     ones = jnp.where(same, 1.0 / E, 0.0).astype(bf16)
     ones2 = jnp.concatenate([ones, ones], axis=0)
-    for o, rows, pair, lanes in local_pairs(r):
-        gain = gain_ref[:, lanes]
-        qb = pick(before, q_ref[0, :, lanes])
-        att = att_ref[:, lanes] + dot(qb, heads(c_refs[o][rows, :]))
-        dy = g_ref[0, :, lanes].astype(f32)
-        d = dy * gain
-        means = dot(
-            jnp.concatenate(split(jnp.concatenate([att * att, d * att], axis=0)), axis=1), ones2
-        )
-        root = lax.rsqrt(means[:BLK] + eps)
-        normed = att * root
-        out_ref[0, :, lanes] = (gain * normed).astype(bf16)
-        ga = ((d - normed * (means[BLK:] * root)) * root).astype(bf16)
-        ga_ref[:, lanes] = ga
-        part_ref[pl.ds(pair, 1), :] = jnp.sum(dy * normed, axis=0, keepdims=True)
-        state_refs[o][rows, :] = fold(dot_tn(qb, ga)).astype(bf16)
+    todo = list(local_pairs(r))
+    for first in range(0, PAIRS, BATCHED):
+        some = todo[first : first + BATCHED]
+        qbs = [pick(before, q_ref[0, :, lanes]) for _, _, _, lanes in some]
+        atts = [
+            att_ref[:, lanes] + dot(qb, heads(c_refs[o][rows, :]))
+            for qb, (o, rows, _, lanes) in zip(qbs, some)
+        ]
+        dys = [g_ref[0, :, lanes].astype(f32) for _, _, _, lanes in some]
+        ds = [dy * gain_ref[:, lanes] for dy, (_, _, _, lanes) in zip(dys, some)]
+        means = [
+            dot(jnp.concatenate(split(jnp.concatenate([att * att, d * att], axis=0)), axis=1), ones2)
+            for att, d in zip(atts, ds)
+        ]
+        gas = []
+        for att, dy, d, mean, (_, _, pair, lanes) in zip(atts, dys, ds, means, some):
+            root = lax.rsqrt(mean[:BLK] + eps)
+            normed = att * root
+            out_ref[0, :, lanes] = (gain_ref[:, lanes] * normed).astype(bf16)
+            ga = ((d - normed * (mean[BLK:] * root)) * root).astype(bf16)
+            ga_ref[:, lanes] = ga
+            part_ref[pl.ds(pair, 1), :] = jnp.sum(dy * normed, axis=0, keepdims=True)
+            gas.append(ga)
+        fulls = [dot_tn(qb, ga) for qb, ga in zip(qbs, gas)]
+        for full, (o, rows, _, _) in zip(fulls, some):
+            state_refs[o][rows, :] = fold(full).astype(bf16)
     tile = jnp.concatenate(split(part_ref[...]), axis=0)
     for ref in state_refs[1:]:
         ref[ROWS:] = tile
@@ -251,15 +262,22 @@
     r, _ = place()
     begins = bounds(len_ref)
     mask, before = pair_mask(begins), before_mask(begins)
-    for o, rows, pair, lanes in local_pairs(r):
-        ga = ga_ref[:, lanes]
-        ga2 = heads(ga)
-        gw = pick(mask, dot_nt(ga2, v_ref[0, :, lanes])).astype(bf16)
-        gq = dot(beside(gw), heads(k_ref[0, :, lanes]))
-        gq = gq + dot_nt(pick(before, ga), heads(c_refs[o][rows, :]))
-        gq_ref[0, :, lanes] = gq.astype(bf16)
-        pk_ref[:, lanes] = dot_tn(gw, heads(q_ref[0, :, lanes]))
-        pv_ref[:, lanes] = dot_tn(w_ref[pair], ga2)
+    todo = list(local_pairs(r))
+    for first in range(0, PAIRS, BATCHED):
+        some = todo[first : first + BATCHED]
+        ga2s = [heads(ga_ref[:, lanes]) for _, _, _, lanes in some]
+        gws = [
+            pick(mask, dot_nt(ga2, v_ref[0, :, pair[3]])).astype(bf16) for ga2, pair in zip(ga2s, some)
+        ]
+        gqs = [
+            dot(beside(gw), heads(k_ref[0, :, lanes]))
+            + dot_nt(pick(before, ga_ref[:, lanes]), heads(c_refs[o][rows, :]))
+            for gw, (o, rows, _, lanes) in zip(gws, some)
+        ]
+        for gq, gw, ga2, (_, _, pair, lanes) in zip(gqs, gws, ga2s, some):
+            gq_ref[0, :, lanes] = gq.astype(bf16)
+            pk_ref[:, lanes] = dot_tn(gw, heads(q_ref[0, :, lanes]))
+            pv_ref[:, lanes] = dot_tn(w_ref[pair], ga2)
 
 
 def last_kernel(len_ref, k_ref, v_ref, pk_ref, pv_ref, *refs):

time: 81.5 us -> 77.7 us (0.953)
  the two profiles are of different devices: /device:TPU:2 before, /device:TPU:6 now
where the time goes in v5:
time: 77.7 us; the launch traced here: 77.5 us
  starting transfers between devices  35 us (45%)
  waiting for transfers between devices  23.9 us (31%)
  Pallas kernels  14.4 us (19%)
  local copies, waits for them, and re-layouts  2.75 us (4%)
  between operations  0.79 us (1%)
    ppermute x6, starting transfers between devices, chain(): lax.ppermute(total, 'ctx', [(i, (i + d * step) % count) for i in range(co...  12.9 us
    ppermute x3, starting transfers between devices, over_dp(): lax.ppermute(gains, 'dp', [(i, i ^ step) for i in range(count)])  12.1 us
    ppermute x12, waiting for transfers between devices, exchange(): lax.ppermute(arrays[o], 'ctx', [(i, i ^ o) for i in range(count)])  8.87 us
    ppermute x6, waiting for transfers between devices, chain(): lax.ppermute(total, 'ctx', [(i, (i + d * step) % count) for i in range(co...  8.18 us
    ppermute x12, starting transfers between devices, exchange(): lax.ppermute(arrays[o], 'ctx', [(i, i ^ o) for i in range(count)])  8.02 us
    ppermute x1, waiting for transfers between devices, chain(): lax.ppermute(mine, 'ctx', [(i, (i + count // 2) % count) for i in range(c...  3.44 us
    ppermute x3, waiting for transfers between devices, over_dp(): lax.ppermute(gains, 'dp', [(i, i ^ step) for i in range(count)])  3.38 us
    pallas_call x1, Pallas kernels, per_device(): call(attend_kernel, (full, shape((BLK, H * E), bf16), share, wide, wide,...  3.23 us
  transfers between devices with their start and end apart: 22, of which 12 were waited for; matrix products, arithmetic and copies ran while one was open for 0% of the time, Pallas kernels for 9%

profile of v5, /device:TPU:6, one launch (start us, length us, event | category | flops | bytes accessed | tf_op | source)
XLA Modules:
  0.0 77.5 jit_solution(2695466343795549113)
XLA Ops:
  6.4 3.1 %collective-permute-done.1.refs_2_ = bf16[256,128]{1,0:T(8,128)(2,1)S(1)} collective-permute-done((bf16[256,128]{1,0:T(8,128)(2,1)S(1)}, bf16[256,128]{1,0:T(8,128)(2,1)S(1)}, u32[]{:S(2)}, u32[]{:S(2)}) %collective-permute-start.1) | collective-permute-done | bytes 65568 | tf_op jit(solution)/shard_map/ppermute | solution.py:312
  10.7 2.5 %collective-permute-start.3 = (bf16[256,128]{1,0:T(8,128)(2,1)S(1)}, bf16[256,128]{1,0:T(8,128)(2,1)S(1)}, u32[]{:S(2)}, u32[]{:S(2)}) collective-permute-start(bf16[256,128]{1,0:T(8,128)(2,1)S(1)} %ahead_total.1), channel_id=1, source_target_pairs={{0,4},{1,5},{2,6},{3,7},{4,8},{5,9},{6,10},{7,11},{8,12},{9,13},{1... | collective-permute-start | bytes 196616 | tf_op jit(solution)/shard_map/ppermute | solution.py:332
  13.2 1.6 %collective-permute-start.4 = (bf16[256,128]{1,0:T(8,128)(2,1)S(1)}, bf16[256,128]{1,0:T(8,128)(2,1)S(1)}, u32[]{:S(2)}, u32[]{:S(2)}) collective-permute-start(bf16[256,128]{1,0:T(8,128)(2,1)S(1)} %ahead_total.1), channel_id=1, source_target_pairs={{0,8},{1,9},{2,10},{3,11},{4,12},{5,13},{6,14},{7,15},{8,16},{9,17... | collective-permute-start | bytes 196616 | tf_op jit(solution)/shard_map/ppermute | solution.py:332
  14.7 3.4 %collective-permute-start.5 = (bf16[256,128]{1,0:T(8,128)(2,1)S(1)}, bf16[256,128]{1,0:T(8,128)(2,1)S(1)}, u32[]{:S(2)}, u32[]{:S(2)}) collective-permute-start(bf16[256,128]{1,0:T(8,128)(2,1)S(1)} %ahead_total.1), channel_id=1, source_target_pairs={{0,12},{1,13},{2,14},{3,15},{4,16},{5,17},{6,18},{7,19},{8,20},{9,... | collective-permute-start | bytes 196616 | tf_op jit(solution)/shard_map/ppermute | solution.py:332
  18.6 4.0 %collective-permute-done.5.refs_6_ = bf16[256,128]{1,0:T(8,128)(2,1)S(1)} collective-permute-done((bf16[256,128]{1,0:T(8,128)(2,1)S(1)}, bf16[256,128]{1,0:T(8,128)(2,1)S(1)}, u32[]{:S(2)}, u32[]{:S(2)}) %collective-permute-start.5) | collective-permute-done | bytes 65568 | tf_op jit(solution)/shard_map/ppermute | solution.py:332
  23.7 1.6 %collective-permute-start.8 = (bf16[256,128]{1,0:T(8,128)(2,1)S(1)}, bf16[256,128]{1,0:T(8,128)(2,1)S(1)}, u32[]{:S(2)}, u32[]{:S(2)}) collective-permute-start(bf16[256,128]{1,0:T(8,128)(2,1)S(1)} %get-tuple-element.51), channel_id=1, source_target_pairs={{0,3},{1,2},{2,1},{3,0},{4,7},{5,6},{6,5},{7,4},{8,11},{9,10},{10,... | collective-permute-start | bytes 196616 | tf_op jit(solution)/shard_map/ppermute | solution.py:312
  25.4 1.5 %inside.1 = (bf16[16,256,128]{2,1,0:T(8,128)(2,1)S(1)}, f32[128,2048]{1,0:T(8,128)S(1)}) custom-call(s32[1,12]{1,0:T(1,128)S(1)} %copy-done.6, bf16[1,128,2048]{2,1,0:T(8,128)(2,1)S(1)} %copy-done.4, bf16[1,128,2048]{2,1,0:T(8,128)(2,1)S(1)} %copy-done.1, bf16[1,128,2048]{2,1,0:T(8,128)(2,1)S(1)} %copy-done.3), custom_call_target="tpu_custom_call" | custom-call | tf_op jit(solution)/shard_map/inside/pallas_call | solution.py:370
  26.9 1.6 %collective-permute-done.7.refs_2_ = bf16[256,128]{1,0:T(8,128)(2,1)S(1)} collective-permute-done((bf16[256,128]{1,0:T(8,128)(2,1)S(1)}, bf16[256,128]{1,0:T(8,128)(2,1)S(1)}, u32[]{:S(2)}, u32[]{:S(2)}) %collective-permute-start.7) | collective-permute-done | bytes 65568 | tf_op jit(solution)/shard_map/ppermute | solution.py:312
  28.9 3.2 %attend.1 = (bf16[1,128,2048]{2,1,0:T(8,128)(2,1)}, bf16[128,2048]{1,0:T(8,128)(2,1)S(1)}, bf16[256,128]{1,0:T(8,128)(2,1)S(1)}, bf16[288,128]{1,0:T(8,128)(2,1)...) custom-call(s32[1,12]{1,0:T(1,128)S(1)} %copy-done.6, ...), custom_call_target="tpu_custom_call" | custom-call | tf_op jit(solution)/shard_map/attend/pallas_call | solution.py:374
  34.3 3.0 %collective-permute-done.10.refs_2_ = bf16[288,128]{1,0:T(8,128)(2,1)S(1)} collective-permute-done((bf16[288,128]{1,0:T(8,128)(2,1)S(1)}, bf16[288,128]{1,0:T(8,128)(2,1)S(1)}, u32[]{:S(2)}, u32[]{:S(2)}) %collective-permute-start.10) | collective-permute-done | bytes 73760 | tf_op jit(solution)/shard_map/ppermute | solution.py:312
  38.2 2.2 %collective-permute-start.12 = (bf16[288,128]{1,0:T(8,128)(2,1)S(1)}, bf16[288,128]{1,0:T(8,128)(2,1)S(1)}, u32[]{:S(2)}, u32[]{:S(2)}) collective-permute-start(bf16[288,128]{1,0:T(8,128)(2,1)S(1)} %back_total.1.refs_7_), channel_id=1, source_target_pairs={{0,28},{1,29},{2,30},{3,31},{4,0},{5,1},{6,2},{7,3},{8,4},{9,5},{1... | collective-permute-start | bytes 221192 | tf_op jit(solution)/shard_map/ppermute | solution.py:332
  40.4 1.7 %collective-permute-start.13 = (bf16[288,128]{1,0:T(8,128)(2,1)S(1)}, bf16[288,128]{1,0:T(8,128)(2,1)S(1)}, u32[]{:S(2)}, u32[]{:S(2)}) collective-permute-start(bf16[288,128]{1,0:T(8,128)(2,1)S(1)} %back_total.1.refs_7_), channel_id=1, source_target_pairs={{0,24},{1,25},{2,26},{3,27},{4,28},{5,29},{6,30},{7,31},{8,0},{9,1... | collective-permute-start | bytes 221192 | tf_op jit(solution)/shard_map/ppermute | solution.py:332
  42.1 1.5 %collective-permute-start.14 = (bf16[288,128]{1,0:T(8,128)(2,1)S(1)}, bf16[288,128]{1,0:T(8,128)(2,1)S(1)}, u32[]{:S(2)}, u32[]{:S(2)}) collective-permute-start(bf16[288,128]{1,0:T(8,128)(2,1)S(1)} %back_total.1.refs_7_), channel_id=1, source_target_pairs={{0,20},{1,21},{2,22},{3,23},{4,24},{5,25},{6,26},{7,27},{8,28},{9,... | collective-permute-start | bytes 221192 | tf_op jit(solution)/shard_map/ppermute | solution.py:332
  43.6 3.0 %grads.1 = (bf16[1,128,2048]{2,1,0:T(8,128)(2,1)}, f32[128,2048]{1,0:T(8,128)S(1)}, f32[128,2048]{1,0:T(8,128)S(1)}) custom-call(s32[1,12]{1,0:T(1,128)S(1)} %copy-done.6, bf16[1,128,2048]{2,1,0:T(8,128)(2,1)S(1)} %copy-done.4, bf16[1,128,2048]{2,1,0:T(8,128)(2,1)S(1)} %copy-done.1, bf16[1,128,2048]{2,1,0:T(8,128)(2,1)S(1)} %copy-done.3, ...), custom_call_target="tpu_custom_call" | custom-call | tf_op jit(solution)/shard_map/grads/pallas_call | solution.py:380
  46.6 3.8 %collective-permute-done.14.refs_6_ = bf16[288,128]{1,0:T(8,128)(2,1)S(1)} collective-permute-done((bf16[288,128]{1,0:T(8,128)(2,1)S(1)}, bf16[288,128]{1,0:T(8,128)(2,1)S(1)}, u32[]{:S(2)}, u32[]{:S(2)}) %collective-permute-start.14) | collective-permute-done | bytes 73760 | tf_op jit(solution)/shard_map/ppermute | solution.py:332
  51.6 1.5 %collective-permute-start.18 = (bf16[256,128]{1,0:T(8,128)(2,1)S(1)}, bf16[256,128]{1,0:T(8,128)(2,1)S(1)}, u32[]{:S(2)}, u32[]{:S(2)}) collective-permute-start(bf16[256,128]{1,0:T(8,128)(2,1)S(1)} %get-tuple-element.73), channel_id=1, source_target_pairs={{0,3},{1,2},{2,1},{3,0},{4,7},{5,6},{6,5},{7,4},{8,11},{9,10},{10,... | collective-permute-start | bytes 196616 | tf_op jit(solution)/shard_map/ppermute | solution.py:312
  53.1 2.0 %collective-permute-start.15 = (f32[64,128]{1,0:T(8,128)S(1)}, f32[64,128]{1,0:T(8,128)S(1)}, u32[]{:S(2)}, u32[]{:S(2)}) collective-permute-start(f32[64,128]{1,0:T(8,128)S(1)} %get-tuple-element.69.mine_ref), channel_id=1, source_target_pairs={{0,16},{1,17},{2,18},{3,19},{4,20},{5,21},{6,22},{7,23},{8,24},{9,... | collective-permute-start | bytes 98312 | tf_op jit(solution)/shard_map/ppermute | solution.py:344
  55.1 3.4 %collective-permute-done.15.theirs_ref = f32[64,128]{1,0:T(8,128)S(1)} collective-permute-done((f32[64,128]{1,0:T(8,128)S(1)}, f32[64,128]{1,0:T(8,128)S(1)}, u32[]{:S(2)}, u32[]{:S(2)}) %collective-permute-start.15) | collective-permute-done | bytes 32800 | tf_op jit(solution)/shard_map/ppermute | solution.py:344
  59.2 2.0 %collective-permute-start.19 = (f32[16,128]{1,0:T(8,128)S(1)}, f32[16,128]{1,0:T(8,128)S(1)}, u32[]{:S(2)}, u32[]{:S(2)}) collective-permute-start(f32[16,128]{1,0:T(8,128)S(1)} %gather.1), channel_id=1, source_target_pairs={{0,32},{32,0},{64,96},{96,64},{128,160},{160,128},{192,224},{224,1... | collective-permute-start | bytes 24584 | tf_op jit(solution)/shard_map/ppermute | solution.py:357
  61.2 1.7 %collective-permute-done.19 = f32[16,128]{1,0:T(8,128)S(1)} collective-permute-done((f32[16,128]{1,0:T(8,128)S(1)}, f32[16,128]{1,0:T(8,128)S(1)}, u32[]{:S(2)}, u32[]{:S(2)}) %collective-permute-start.19) | collective-permute-done | bytes 8224 | tf_op jit(solution)/shard_map/ppermute | solution.py:357
  62.9 3.3 %collective-permute-start.20 = (f32[16,128]{1,0:T(8,128)S(1)}, f32[16,128]{1,0:T(8,128)S(1)}, u32[]{:S(2)}, u32[]{:S(2)}) collective-permute-start(f32[16,128]{1,0:T(8,128)S(1)} %add.9), channel_id=1, source_target_pairs={{0,64},{32,96},{64,0},{96,32},{128,192},{160,224},{192,128},{224,1... | collective-permute-start | bytes 24584 | tf_op jit(solution)/shard_map/ppermute | solution.py:357
  66.2 1.6 %collective-permute-done.20 = f32[16,128]{1,0:T(8,128)S(1)} collective-permute-done((f32[16,128]{1,0:T(8,128)S(1)}, f32[16,128]{1,0:T(8,128)S(1)}, u32[]{:S(2)}, u32[]{:S(2)}) %collective-permute-start.20) | collective-permute-done | bytes 8224 | tf_op jit(solution)/shard_map/ppermute | solution.py:357
  67.8 6.8 %collective-permute-start.21 = (f32[16,128]{1,0:T(8,128)S(1)}, f32[16,128]{1,0:T(8,128)S(1)}, u32[]{:S(2)}, u32[]{:S(2)}) collective-permute-start(f32[16,128]{1,0:T(8,128)S(1)} %add.10), channel_id=1, source_target_pairs={{0,128},{32,160},{64,192},{96,224},{128,0},{160,32},{192,64},{224,... | collective-permute-start | bytes 24584 | tf_op jit(solution)/shard_map/ppermute | solution.py:357
  74.7 2.2 %last.1 = (bf16[1,128,2048]{2,1,0:T(8,128)(2,1)}, bf16[1,128,2048]{2,1,0:T(8,128)(2,1)}) custom-call(s32[1,12]{1,0:T(1,128)S(1)} %copy-done.6, bf16[1,128,2048]{2,1,0:T(8,128)(2,1)S(1)} %copy-done.1, bf16[1,128,2048]{2,1,0:T(8,128)(2,1)S(1)} %copy-done.3, f32[128,2048]{1,0:T(8,128)S(1)} %get-tuple-element.64.pk_ref, ...), custom_call_target="tpu_custom_call" | custom-call | tf_op jit(solution)/shard_map/last/pallas_call | solution.py:385
  (49 shorter events, 14.4 us)
Async XLA Ops:
  3.4 22.0 %copy-start.3 = (bf16[1,128,2048]{2,1,0:T(8,128)(2,1)S(1)}, bf16[1,128,2048]{2,1,0:T(8,128)(2,1)}, u32[]{:S(2)}) copy-start(bf16[1,128,2048]{2,1,0:T(8,128)(2,1)} %v_ref.7) | copy-start | bytes 1572868
  3.4 22.0 %copy-start.4 = (bf16[1,128,2048]{2,1,0:T(8,128)(2,1)S(1)}, bf16[1,128,2048]{2,1,0:T(8,128)(2,1)}, u32[]{:S(2)}) copy-start(bf16[1,128,2048]{2,1,0:T(8,128)(2,1)} %q_ref.5) | copy-start | bytes 1572868
  4.5 2.0 %collective-permute-start = (bf16[256,128]{1,0:T(8,128)(2,1)S(1)}, bf16[256,128]{1,0:T(8,128)(2,1)S(1)}, u32[]{:S(2)}, u32[]{:S(2)}) collective-permute-start(bf16[256,128]{1,0:T(8,128)(2,1)S(1)} %get-tuple-element.45), channel_id=1, source_target_pairs={{0,1},{1,0},{2,3},{3,2},{4,5},{5,4},{6,7},{7,6},{8,9},{9,8},{10,11... | collective-permute-start | bytes 196616 | tf_op jit(solution)/shard_map/ppermute | solution.py:312
  4.6 5.0 %collective-permute-start.1 = (bf16[256,128]{1,0:T(8,128)(2,1)S(1)}, bf16[256,128]{1,0:T(8,128)(2,1)S(1)}, u32[]{:S(2)}, u32[]{:S(2)}) collective-permute-start(bf16[256,128]{1,0:T(8,128)(2,1)S(1)} %get-tuple-element.46), channel_id=1, source_target_pairs={{0,2},{1,3},{2,0},{3,1},{4,6},{5,7},{6,4},{7,5},{8,10},{9,11},{10,... | collective-permute-start | bytes 196616 | tf_op jit(solution)/shard_map/ppermute | solution.py:312
  5.5 4.5 %collective-permute-start.2 = (bf16[256,128]{1,0:T(8,128)(2,1)S(1)}, bf16[256,128]{1,0:T(8,128)(2,1)S(1)}, u32[]{:S(2)}, u32[]{:S(2)}) collective-permute-start(bf16[256,128]{1,0:T(8,128)(2,1)S(1)} %get-tuple-element.47), channel_id=1, source_target_pairs={{0,3},{1,2},{2,1},{3,0},{4,7},{5,6},{6,5},{7,4},{8,11},{9,10},{10,... | collective-permute-start | bytes 196616 | tf_op jit(solution)/shard_map/ppermute | solution.py:312
  10.7 7.5 %collective-permute-start.3 = (bf16[256,128]{1,0:T(8,128)(2,1)S(1)}, bf16[256,128]{1,0:T(8,128)(2,1)S(1)}, u32[]{:S(2)}, u32[]{:S(2)}) collective-permute-start(bf16[256,128]{1,0:T(8,128)(2,1)S(1)} %ahead_total.1), channel_id=1, source_target_pairs={{0,4},{1,5},{2,6},{3,7},{4,8},{5,9},{6,10},{7,11},{8,12},{9,13},{1... | collective-permute-start | bytes 196616 | tf_op jit(solution)/shard_map/ppermute | solution.py:332
  13.2 5.5 %collective-permute-start.4 = (bf16[256,128]{1,0:T(8,128)(2,1)S(1)}, bf16[256,128]{1,0:T(8,128)(2,1)S(1)}, u32[]{:S(2)}, u32[]{:S(2)}) collective-permute-start(bf16[256,128]{1,0:T(8,128)(2,1)S(1)} %ahead_total.1), channel_id=1, source_target_pairs={{0,8},{1,9},{2,10},{3,11},{4,12},{5,13},{6,14},{7,15},{8,16},{9,17... | collective-permute-start | bytes 196616 | tf_op jit(solution)/shard_map/ppermute | solution.py:332
  14.7 7.9 %collective-permute-start.5 = (bf16[256,128]{1,0:T(8,128)(2,1)S(1)}, bf16[256,128]{1,0:T(8,128)(2,1)S(1)}, u32[]{:S(2)}, u32[]{:S(2)}) collective-permute-start(bf16[256,128]{1,0:T(8,128)(2,1)S(1)} %ahead_total.1), channel_id=1, source_target_pairs={{0,12},{1,13},{2,14},{3,15},{4,16},{5,17},{6,18},{7,19},{8,20},{9,... | collective-permute-start | bytes 196616 | tf_op jit(solution)/shard_map/ppermute | solution.py:332
  23.4 3.5 %collective-permute-start.6 = (bf16[256,128]{1,0:T(8,128)(2,1)S(1)}, bf16[256,128]{1,0:T(8,128)(2,1)S(1)}, u32[]{:S(2)}, u32[]{:S(2)}) collective-permute-start(bf16[256,128]{1,0:T(8,128)(2,1)S(1)} %get-tuple-element.49), channel_id=1, source_target_pairs={{0,1},{1,0},{2,3},{3,2},{4,5},{5,4},{6,7},{7,6},{8,9},{9,8},{10,11... | collective-permute-start | bytes 196616 | tf_op jit(solution)/shard_map/ppermute | solution.py:312
  23.5 5.0 %collective-permute-start.7 = (bf16[256,128]{1,0:T(8,128)(2,1)S(1)}, bf16[256,128]{1,0:T(8,128)(2,1)S(1)}, u32[]{:S(2)}, u32[]{:S(2)}) collective-permute-start(bf16[256,128]{1,0:T(8,128)(2,1)S(1)} %get-tuple-element.50), channel_id=1, source_target_pairs={{0,2},{1,3},{2,0},{3,1},{4,6},{5,7},{6,4},{7,5},{8,10},{9,11},{10,... | collective-permute-start | bytes 196616 | tf_op jit(solution)/shard_map/ppermute | solution.py:312
  23.7 5.2 %collective-permute-start.8 = (bf16[256,128]{1,0:T(8,128)(2,1)S(1)}, bf16[256,128]{1,0:T(8,128)(2,1)S(1)}, u32[]{:S(2)}, u32[]{:S(2)}) collective-permute-start(bf16[256,128]{1,0:T(8,128)(2,1)S(1)} %get-tuple-element.51), channel_id=1, source_target_pairs={{0,3},{1,2},{2,1},{3,0},{4,7},{5,6},{6,5},{7,4},{8,11},{9,10},{10,... | collective-permute-start | bytes 196616 | tf_op jit(solution)/shard_map/ppermute | solution.py:312
  32.2 5.1 %collective-permute-start.10 = (bf16[288,128]{1,0:T(8,128)(2,1)S(1)}, bf16[288,128]{1,0:T(8,128)(2,1)S(1)}, u32[]{:S(2)}, u32[]{:S(2)}) collective-permute-start(bf16[288,128]{1,0:T(8,128)(2,1)S(1)} %get-tuple-element.55), channel_id=1, source_target_pairs={{0,2},{1,3},{2,0},{3,1},{4,6},{5,7},{6,4},{7,5},{8,10},{9,11},{10,... | collective-permute-start | bytes 221192 | tf_op jit(solution)/shard_map/ppermute | solution.py:312
  32.9 4.7 %collective-permute-start.11 = (bf16[288,128]{1,0:T(8,128)(2,1)S(1)}, bf16[288,128]{1,0:T(8,128)(2,1)S(1)}, u32[]{:S(2)}, u32[]{:S(2)}) collective-permute-start(bf16[288,128]{1,0:T(8,128)(2,1)S(1)} %get-tuple-element.56), channel_id=1, source_target_pairs={{0,3},{1,2},{2,1},{3,0},{4,7},{5,6},{6,5},{7,4},{8,11},{9,10},{10,... | collective-permute-start | bytes 221192 | tf_op jit(solution)/shard_map/ppermute | solution.py:312
  33.8 3.8 %collective-permute-start.9 = (bf16[288,128]{1,0:T(8,128)(2,1)S(1)}, bf16[288,128]{1,0:T(8,128)(2,1)S(1)}, u32[]{:S(2)}, u32[]{:S(2)}) collective-permute-start(bf16[288,128]{1,0:T(8,128)(2,1)S(1)} %get-tuple-element.54), channel_id=1, source_target_pairs={{0,1},{1,0},{2,3},{3,2},{4,5},{5,4},{6,7},{7,6},{8,9},{9,8},{10,11... | collective-permute-start | bytes 221192 | tf_op jit(solution)/shard_map/ppermute | solution.py:312
  38.2 8.4 %collective-permute-start.12 = (bf16[288,128]{1,0:T(8,128)(2,1)S(1)}, bf16[288,128]{1,0:T(8,128)(2,1)S(1)}, u32[]{:S(2)}, u32[]{:S(2)}) collective-permute-start(bf16[288,128]{1,0:T(8,128)(2,1)S(1)} %back_total.1.refs_7_), channel_id=1, source_target_pairs={{0,28},{1,29},{2,30},{3,31},{4,0},{5,1},{6,2},{7,3},{8,4},{9,5},{1... | collective-permute-start | bytes 221192 | tf_op jit(solution)/shard_map/ppermute | solution.py:332
  40.4 6.2 %collective-permute-start.13 = (bf16[288,128]{1,0:T(8,128)(2,1)S(1)}, bf16[288,128]{1,0:T(8,128)(2,1)S(1)}, u32[]{:S(2)}, u32[]{:S(2)}) collective-permute-start(bf16[288,128]{1,0:T(8,128)(2,1)S(1)} %back_total.1.refs_7_), channel_id=1, source_target_pairs={{0,24},{1,25},{2,26},{3,27},{4,28},{5,29},{6,30},{7,31},{8,0},{9,1... | collective-permute-start | bytes 221192 | tf_op jit(solution)/shard_map/ppermute | solution.py:332
  42.1 8.3 %collective-permute-start.14 = (bf16[288,128]{1,0:T(8,128)(2,1)S(1)}, bf16[288,128]{1,0:T(8,128)(2,1)S(1)}, u32[]{:S(2)}, u32[]{:S(2)}) collective-permute-start(bf16[288,128]{1,0:T(8,128)(2,1)S(1)} %back_total.1.refs_7_), channel_id=1, source_target_pairs={{0,20},{1,21},{2,22},{3,23},{4,24},{5,25},{6,26},{7,27},{8,28},{9,... | collective-permute-start | bytes 221192 | tf_op jit(solution)/shard_map/ppermute | solution.py:332
  51.2 8.0 %collective-permute-start.16 = (bf16[256,128]{1,0:T(8,128)(2,1)S(1)}, bf16[256,128]{1,0:T(8,128)(2,1)S(1)}, u32[]{:S(2)}, u32[]{:S(2)}) collective-permute-start(bf16[256,128]{1,0:T(8,128)(2,1)S(1)} %get-tuple-element.71), channel_id=1, source_target_pairs={{0,1},{1,0},{2,3},{3,2},{4,5},{5,4},{6,7},{7,6},{8,9},{9,8},{10,11... | collective-permute-start | bytes 196616 | tf_op jit(solution)/shard_map/ppermute | solution.py:312
  51.3 7.9 %collective-permute-start.17 = (bf16[256,128]{1,0:T(8,128)(2,1)S(1)}, bf16[256,128]{1,0:T(8,128)(2,1)S(1)}, u32[]{:S(2)}, u32[]{:S(2)}) collective-permute-start(bf16[256,128]{1,0:T(8,128)(2,1)S(1)} %get-tuple-element.72), channel_id=1, source_target_pairs={{0,2},{1,3},{2,0},{3,1},{4,6},{5,7},{6,4},{7,5},{8,10},{9,11},{10,... | collective-permute-start | bytes 196616 | tf_op jit(solution)/shard_map/ppermute | solution.py:312
  51.6 7.6 %collective-permute-start.18 = (bf16[256,128]{1,0:T(8,128)(2,1)S(1)}, bf16[256,128]{1,0:T(8,128)(2,1)S(1)}, u32[]{:S(2)}, u32[]{:S(2)}) collective-permute-start(bf16[256,128]{1,0:T(8,128)(2,1)S(1)} %get-tuple-element.73), channel_id=1, source_target_pairs={{0,3},{1,2},{2,1},{3,0},{4,7},{5,6},{6,5},{7,4},{8,11},{9,10},{10,... | collective-permute-start | bytes 196616 | tf_op jit(solution)/shard_map/ppermute | solution.py:312
  53.1 5.4 %collective-permute-start.15 = (f32[64,128]{1,0:T(8,128)S(1)}, f32[64,128]{1,0:T(8,128)S(1)}, u32[]{:S(2)}, u32[]{:S(2)}) collective-permute-start(f32[64,128]{1,0:T(8,128)S(1)} %get-tuple-element.69.mine_ref), channel_id=1, source_target_pairs={{0,16},{1,17},{2,18},{3,19},{4,20},{5,21},{6,22},{7,23},{8,24},{9,... | collective-permute-start | bytes 98312 | tf_op jit(solution)/shard_map/ppermute | solution.py:344
  59.2 3.7 %collective-permute-start.19 = (f32[16,128]{1,0:T(8,128)S(1)}, f32[16,128]{1,0:T(8,128)S(1)}, u32[]{:S(2)}, u32[]{:S(2)}) collective-permute-start(f32[16,128]{1,0:T(8,128)S(1)} %gather.1), channel_id=1, source_target_pairs={{0,32},{32,0},{64,96},{96,64},{128,160},{160,128},{192,224},{224,1... | collective-permute-start | bytes 24584 | tf_op jit(solution)/shard_map/ppermute | solution.py:357
  62.9 4.9 %collective-permute-start.20 = (f32[16,128]{1,0:T(8,128)S(1)}, f32[16,128]{1,0:T(8,128)S(1)}, u32[]{:S(2)}, u32[]{:S(2)}) collective-permute-start(f32[16,128]{1,0:T(8,128)S(1)} %add.9), channel_id=1, source_target_pairs={{0,64},{32,96},{64,0},{96,32},{128,192},{160,224},{192,128},{224,1... | collective-permute-start | bytes 24584 | tf_op jit(solution)/shard_map/ppermute | solution.py:357
  67.8 9.1 %collective-permute-start.21 = (f32[16,128]{1,0:T(8,128)S(1)}, f32[16,128]{1,0:T(8,128)S(1)}, u32[]{:S(2)}, u32[]{:S(2)}) collective-permute-start(f32[16,128]{1,0:T(8,128)S(1)} %add.10), channel_id=1, source_target_pairs={{0,128},{32,160},{64,192},{96,224},{128,0},{160,32},{192,64},{224,... | collective-permute-start | bytes 24584 | tf_op jit(solution)/shard_map/ppermute | solution.py:357
  (6 other events, 32.5 us)
